TPU v7x, 256 devices: a whole 4x4x8 slice. The times are simulated.
256 devices in a mesh: pipe: 8 (over z), seq: 16 (over x, y), tp: 2 (over core).
Axes of the slice: x: 4, y: 4, z: 8, core: 2. Of those that a mesh axis runs over, the one named last changes fastest.
Arguments:
- layer_inputs: bfloat16 [8, 2048, 4096], P('pipe', ('seq', 'tp')), may hold values from -6 to 6
- out_grad: bfloat16 [2048, 4096], P('seq', 'tp'), may hold values from -6 to 6
- short_weights: bfloat16 [8, 7, 3, 4096], P('pipe', None, None, 'tp'), may hold values from -2 to 2
- long_filters: bfloat16 [8, 256, 128], P('pipe', 'tp'), may hold values from -0.15625 to 0.15625
- out_weights: bfloat16 [8, 4096, 4096], P('pipe', 'tp', 'seq'), may hold values from -0.09375 to 0.09375
Outputs:
- input_grad: bfloat16 [8, 2048, 4096], P('pipe', 'seq', 'tp')
- short_grad: float32 [8, 7, 3, 4096], P('pipe', None, None, 'tp')
- long_grad: float32 [8, 256, 128], P('pipe', 'tp')
All inputs are finite; a program needn't handle non-finite values.
Results may differ from a plain program's by a relative error of at most 0.03.
Values may be sent and summed in bfloat16 or wider, within the bound.
No kernel may reach another device: no remote copies, remote signals or barrier semaphores. Data moves between devices by JAX's collectives and lax.ppermute only.
A program may use at most 192 MiB of HBM per device.

v0:
```python
import functools

import jax
import jax.numpy as jnp
from jax import lax
from jax.experimental import pallas as pl
from jax.experimental.pallas import tpu as pltpu
from jax.sharding import PartitionSpec as P

KL = 128
KS = 7
TILE = 128
GW = 16
AUX = 48
EDGE = 8
PAD = 16
WIN = 2 * KL
BF = jnp.bfloat16
F32 = jnp.float32
VMEM_LIMIT = 24 * 1024 * 1024
INTERPRET = False


def call(body, out_shape, *args, **kwargs):
    return pl.pallas_call(
        body,
        out_shape=out_shape,
        compiler_params=pltpu.CompilerParams(vmem_limit_bytes=VMEM_LIMIT),
        interpret=INTERPRET,
        **kwargs,
    )(*args)


def shape(dims, dtype):
    return jax.ShapeDtypeStruct(dims, dtype)


def dot(a, b):
    return jnp.dot(a, b, preferred_element_type=F32)


def dot_nt(a, b):
    return lax.dot_general(a, b, (((1,), (1,)), ((), ())), preferred_element_type=F32)


def swap_matrix(width):
    size = TILE // width
    n = size * TILE
    row = lax.broadcasted_iota(jnp.int32, (n, n), 0)
    col = lax.broadcasted_iota(jnp.int32, (n, n), 1)
    a, b, j = row // TILE, (row // width) % size, row % width
    return (col == b * TILE + a * width + j).astype(F32).astype(BF)


def split_owned(x, planes, width, matrix):
    step = planes * width
    slices = x.shape[1] // step
    size = TILE // width
    pieces = [[None] * (slices // size) for _ in range(planes)]
    for a in range(slices // size):
        for b in range(planes // size):
            tiles = [
                x[:, (a * size + i) * step + b * TILE : (a * size + i) * step + (b + 1) * TILE]
                for i in range(size)
            ]
            moved = dot(jnp.concatenate(tiles, axis=1), matrix).astype(BF)
            for i in range(size):
                pieces[b * size + i][a] = moved[:, i * TILE : (i + 1) * TILE]
    return [jnp.concatenate(p, axis=1) for p in pieces]


def join_owned(parts, width, matrix):
    planes = len(parts)
    size = TILE // width
    slices = parts[0].shape[1] // width
    out = [[None] * (planes // size) for _ in range(slices)]
    for a in range(slices // size):
        for b in range(planes // size):
            tiles = [parts[b * size + i][:, a * TILE : (a + 1) * TILE] for i in range(size)]
            moved = dot(jnp.concatenate(tiles, axis=1), matrix)
            for i in range(size):
                out[a * size + i][b] = moved[:, i * TILE : (i + 1) * TILE]
    return jnp.concatenate([jnp.concatenate(o, axis=1) for o in out], axis=1)


def filter_rows(slices, planes, per):
    n = slices * planes * per
    row = lax.broadcasted_iota(jnp.int32, (n, n), 0)
    col = lax.broadcasted_iota(jnp.int32, (n, n), 1)
    z, k, g = row // (slices * per), (row // per) % slices, row % per
    return (col == k * planes * per + z * per + g).astype(F32).astype(BF)


def pack_body(planes, slices, width, tp_ref, w_ref, sw_ref, lf_ref, x_ref, other_ref, out_ref):
    owned = slices * width
    depth = planes * width
    half = slices * depth
    count = x_ref.shape[0]
    matrix = swap_matrix(width)
    tp = tp_ref[0]
    start = pl.multiple_of(tp * half, TILE)
    for source, place in ((x_ref, tp), (other_ref, 1 - tp)):
        pieces = split_owned(source[:, pl.ds(start, half)], planes, width, matrix)
        at = pl.multiple_of(place * count, PAD)
        for z in range(planes):
            out_ref[z, pl.ds(at, count), :] = pieces[z]
    for z in range(planes):
        block = w_ref[:, z].reshape(owned, depth)
        turned = block.astype(F32).T.astype(BF)
        low = KL + z * width
        out_ref[:, low : low + width, :] = turned.reshape(planes, width, owned)
    base = KL + depth
    taps = [sw_ref[j].astype(F32) for j in range(KS)]
    taps.append(jnp.zeros((32 - 3 * KS, half), F32))
    taps = split_owned(jnp.concatenate(taps, axis=0).astype(BF), planes, width, matrix)
    per = width // GW
    filters = dot(filter_rows(slices, planes, per), lf_ref[...]).astype(BF)
    groups = slices * per
    for z in range(planes):
        out_ref[z, base : base + 32, :] = taps[z]
        out_ref[z, base + 32 : base + AUX, :] = jnp.zeros((GW, owned), BF)
        out_ref[z, base + 32 : base + 32 + groups, :KL] = filters[z * groups : (z + 1) * groups]


def shuffle_body(planes, width, x_ref, out_ref):
    pieces = split_owned(x_ref[...], planes, width, swap_matrix(width))
    for z in range(planes):
        out_ref[z] = pieces[z]


def grouped(toeplitz, rows_per, source, groups):
    channels = source.shape[1]
    tiles = []
    for u in range(channels // TILE):
        per = TILE // GW
        full = dot(toeplitz[u * per * rows_per : (u + 1) * per * rows_per], source[:, u * TILE : (u + 1) * TILE])
        lane = lax.broadcasted_iota(jnp.int32, (rows_per, TILE), 1) // GW
        merged = full[:rows_per]
        for g in range(1, per):
            merged = jnp.where(lane == g, full[g * rows_per : (g + 1) * rows_per], merged)
        tiles.append(merged)
    return jnp.concatenate(tiles, axis=1)


def edge_rows(ref, groups):
    return jnp.concatenate(
        [ref[g * KL + KL - PAD : (g + 1) * KL, :] for g in range(groups)], axis=0
    )


def recompute_body(
    groups, own_ref, prev_ref, prev2_ref, next_ref, aux_ref,
    f0_ref, f1_ref, f2_ref, mixed_ref, back_ref, turned_ref,
    rows_ref, band_ref,
):
    rows_ref[0:PAD, :] = prev2_ref[...].astype(F32)
    rows_ref[PAD : PAD + KL, :] = prev_ref[...].astype(F32)
    rows_ref[PAD + KL : PAD + 2 * KL, :] = own_ref[...].astype(F32)
    rows_ref[PAD + 2 * KL :, :] = next_ref[...].astype(F32)
    taps = aux_ref[0:32, :].astype(F32)

    def feature(f, first, count):
        start = PAD + KL + first
        total = taps[f : f + 1] * rows_ref[start : start + count, :]
        for j in range(1, KS):
            total = total + taps[3 * j + f : 3 * j + f + 1] * rows_ref[start - j : start - j + count, :]
        return total

    f0_ref[...] = feature(0, 0, KL)
    key_tail = feature(1, 0, KL + EDGE)
    value_tail = feature(2, 0, KL + EDGE)
    f1_ref[...] = key_tail
    f2_ref[...] = value_tail
    kv = jnp.concatenate([feature(1, -KL, KL) * feature(2, -KL, KL), key_tail * value_tail], axis=0)
    window = kv[:WIN].astype(BF)
    late = kv[EDGE : EDGE + WIN].astype(BF)

    filters = aux_ref[32 : 32 + groups, :KL]
    tap = lax.broadcasted_iota(jnp.int32, (KL, WIN), 0)
    lane = lax.broadcasted_iota(jnp.int32, (KL, WIN), 1)
    ahead = dot(filters, (lane == KL - tap).astype(F32).astype(BF))
    behind = dot(filters, (lane == tap).astype(F32).astype(BF))
    for g in range(groups):
        wide = jnp.broadcast_to(ahead[g : g + 1], (KL, WIN))
        band_ref[g * KL : (g + 1) * KL, :] = pltpu.roll(wide, 0, 1, stride=1, stride_axis=0).astype(BF)
        wide = jnp.broadcast_to(behind[g : g + 1], (KL, WIN))
        back_ref[g * KL : (g + 1) * KL, :] = pltpu.roll(wide, 0, 1, stride=1, stride_axis=0).astype(BF)
    mixed_ref[0:KL, :] = grouped(band_ref, KL, window, groups)
    mixed_ref[KL:, :] = grouped(edge_rows(band_ref, groups), PAD, late, groups)[PAD - EDGE :]
    source = lax.broadcasted_iota(jnp.int32, (WIN, WIN), 0)
    target = lax.broadcasted_iota(jnp.int32, (WIN, WIN), 1)
    mirror = (source + target == WIN - 1).astype(F32).astype(BF)
    turned_ref[...] = dot(mirror, window).astype(BF)


def project_body(tp_ref, own_ref, other_ref, w_ref, out_ref):
    first = tp_ref[0] == 0
    own, other = own_ref[...], other_ref[...]
    rows = jnp.concatenate([jnp.where(first, own, other), jnp.where(first, other, own)], axis=1)
    slices, _, count, width, owned = w_ref.shape
    for z in range(count):
        out_ref[z] = dot(rows, w_ref[:, 0, z].reshape(slices * width, owned)).astype(BF)


def gate_body(parts_ref, f0_ref, send_ref, dgate_ref, early_ref):
    total = parts_ref[0].astype(F32)
    for z in range(1, parts_ref.shape[0]):
        total = total + parts_ref[z].astype(F32)
    dgate = total.astype(BF)
    dmixed = (dgate.astype(F32) * f0_ref[...]).astype(BF)
    send_ref[0:KL, :] = dmixed
    send_ref[KL:, :] = dgate[:PAD]
    dgate_ref[...] = dgate
    early_ref[...] = dmixed[:PAD]


def finish_body(
    groups, send_ref, dgate_ref, near_ref, far_ref, f1_ref, f2_ref, mixed_ref, back_ref, aux_ref, grad_ref,
    out_ref, dkv_ref, d0_ref, d1_ref, d2_ref,
):
    rows = jnp.concatenate(
        [send_ref[0:KL, :], near_ref[0:KL, :], far_ref[...]], axis=0
    )
    window = rows[:WIN]
    late = rows.astype(F32)[EDGE : EDGE + WIN].astype(BF)
    main = grouped(back_ref, KL, window, groups)
    tail = grouped(edge_rows(back_ref, groups), PAD, late, groups)[PAD - EDGE :]
    dkv_ref[...] = main
    d0_ref[0:KL, :] = dgate_ref[...].astype(F32) * mixed_ref[0:KL, :]
    d0_ref[KL:, :] = near_ref[KL:, :].astype(F32)[:EDGE] * mixed_ref[KL:, :]
    d1_ref[0:KL, :] = main * f2_ref[0:KL, :]
    d1_ref[KL:, :] = tail * f2_ref[KL:, :]
    d2_ref[0:KL, :] = main * f1_ref[0:KL, :]
    d2_ref[KL:, :] = tail * f1_ref[KL:, :]
    taps = aux_ref[0:32, :].astype(F32)
    total = grad_ref[...].astype(F32)
    for j in range(KS):
        for f, ref in enumerate((d0_ref, d1_ref, d2_ref)):
            total = total + taps[3 * j + f : 3 * j + f + 1] * ref[j : j + KL, :]
    out_ref[...] = total.astype(BF)


def filters_body(
    groups, dgate_ref, mixed_ref, dkv_ref, f1_ref, f2_ref, own_ref, prev_ref, send_ref, turned_ref,
    *refs,
):
    out_ref, rows_ref, skew_ref = refs[-3:]
    channels = own_ref.shape[1]
    rows_ref[0:PAD, :] = prev_ref[KL - PAD :, :].astype(F32)
    rows_ref[PAD:, :] = own_ref[...].astype(F32)
    dkv = dkv_ref[...]
    grads = (
        dgate_ref[...].astype(F32) * mixed_ref[0:KL, :],
        dkv * f2_ref[0:KL, :],
        dkv * f1_ref[0:KL, :],
    )
    sums = []
    for j in range(KS):
        source = rows_ref[PAD - j : PAD - j + KL, :]
        for f in range(3):
            sums.append(jnp.sum(grads[f] * source, axis=0, keepdims=True))
    sums.append(jnp.zeros((32 - 3 * KS, channels), F32))
    short = jnp.concatenate(sums, axis=0).astype(BF)
    for u in range(channels // TILE):
        out_ref[u, 0:32, :] = short[:, u * TILE : (u + 1) * TILE]
    lags = []
    per = TILE // GW
    lane = lax.broadcasted_iota(jnp.int32, (KL, TILE), 1) // GW
    for u in range(channels // TILE):
        grad = send_ref[0:KL, u * TILE : (u + 1) * TILE].astype(F32)
        stacked = jnp.concatenate(
            [jnp.where(lane == g, grad, 0.0).astype(BF) for g in range(per)], axis=0
        )
        skew_ref[...] = dot_nt(stacked, turned_ref[:, u * TILE : (u + 1) * TILE])
        for g in range(per):
            rolled = pltpu.roll(skew_ref[g * KL : (g + 1) * KL, :], 0, 1, stride=1, stride_axis=0)
            lags.append(jnp.sum(rolled, axis=0, keepdims=True))
    if groups < GW:
        lags.append(jnp.zeros((GW - groups, WIN), F32))
    sums = pltpu.roll(jnp.concatenate(lags, axis=0), WIN - (KL - 1), 1)
    long = sums[:, :KL].astype(BF)
    for u in range(channels // TILE):
        out_ref[u, 32:AUX, :] = long


def sum_body(copies, in_ref, out_ref):
    total = in_ref[0].astype(F32)
    for s in range(1, in_ref.shape[0]):
        total = total + in_ref[s].astype(F32)
    value = total.astype(BF)
    for s in range(copies):
        out_ref[s] = value


def merge_body(sums_ref, *refs):
    grads, out_ref = refs[:-1], refs[-1]
    halves = sums_ref.shape[0] // len(grads)
    for p, ref in enumerate(grads):
        out_ref[p, :KL, :] = ref[...]
        for u in range(halves):
            out_ref[p, KL:, u * TILE : (u + 1) * TILE] = sums_ref[p * halves + u]


def spread_body(slices, width, in_ref, grad_ref, short_ref, long_ref):
    planes = in_ref.shape[0]
    matrix = swap_matrix(width)
    grad_ref[...] = join_owned([in_ref[z, :KL] for z in range(planes)], width, matrix).astype(BF)
    short = join_owned([in_ref[z, KL : KL + 32] for z in range(planes)], width, matrix)
    for j in range(KS):
        short_ref[j, 0:3, :] = short[3 * j : 3 * j + 3]
    per = width // GW
    groups = slices * per
    stacked = jnp.concatenate(
        [in_ref[z, KL + 32 : KL + 32 + groups, :KL] for z in range(planes)], axis=0
    )
    mover = filter_rows(slices, planes, per)
    long_ref[...] = lax.dot_general(
        mover, stacked, (((0,), (0,)), ((), ())), preferred_element_type=F32
    )


def from_next(x, by):
    size = lax.axis_size("seq")
    return lax.ppermute(x, "seq", [(i, i - by) for i in range(by, size)])


def from_before(x, by):
    size = lax.axis_size("seq")
    return lax.ppermute(x, "seq", [(i, i + by) for i in range(size - by)])


def per_device(layer_inputs, out_grad, short_weights, long_filters, out_weights):
    planes = lax.axis_size("pipe")
    blocks = lax.axis_size("seq")
    depth = out_weights.shape[2]
    half = out_grad.shape[1]
    width = depth // planes
    slices = half // depth
    owned = slices * width
    groups = owned // GW
    tokens = out_grad.shape[0]
    dims = long_filters.shape[1]

    tp_index = lax.axis_index("tp").astype(jnp.int32).reshape(1)
    own_rows = layer_inputs[0]
    swapped = lax.ppermute(own_rows, "tp", [(0, 1), (1, 0)])
    packed = pl.pallas_call(
        functools.partial(pack_body, planes, slices, width),
        out_shape=shape((planes, tokens + depth + AUX, owned), BF),
        in_specs=[pl.BlockSpec(memory_space=pltpu.SMEM)]
        + [pl.BlockSpec(memory_space=pltpu.VMEM)] * 5,
        compiler_params=pltpu.CompilerParams(vmem_limit_bytes=VMEM_LIMIT),
        interpret=INTERPRET,
    )(
        tp_index,
        out_weights[0].reshape(slices, planes, width, depth),
        short_weights[0],
        long_filters[0],
        own_rows,
        swapped,
    )
    packed = lax.all_to_all(packed, "pipe", 0, 0, tiled=True)
    rows = packed[:, :tokens]
    before = from_before(rows, 1)
    before2 = from_before(rows[:, tokens - PAD :], 2)
    after = from_next(rows[:, :PAD], 1)

    def whole(x):
        return pl.BlockSpec(x.shape, lambda i: (0,) * len(x.shape))

    def plane(x, p, count, at=0):
        return pl.BlockSpec((None, count, x.shape[2]), lambda i, p=p, at=at: (p, at, 0))

    def own_block(p):
        return plane(packed, p, tokens)

    def aux_block(p):
        return plane(packed, p, AUX, (tokens + depth) // AUX)

    def recomputed(p):
        results = (
            shape((KL, owned), F32),
            shape((KL + EDGE, owned), F32),
            shape((KL + EDGE, owned), F32),
            shape((KL + EDGE, owned), F32),
            shape((groups * KL, WIN), BF),
            shape((WIN, owned), BF),
        )
        return call(
            functools.partial(recompute_body, groups),
            results,
            packed,
            before,
            before2,
            after,
            packed,
            grid=(1,),
            in_specs=[
                own_block(p),
                plane(before, p, tokens),
                plane(before2, p, PAD),
                plane(after, p, PAD),
                aux_block(p),
            ],
            out_specs=tuple(whole(r) for r in results),
            scratch_shapes=[
                pltpu.VMEM((2 * KL + 2 * PAD, owned), F32),
                pltpu.VMEM((groups * KL, WIN), BF),
            ],
        )

    def gathered(source, first, last):
        pieces = lax.all_gather(source[first : last + 1, tokens : tokens + depth], "seq", axis=0)
        return pieces.reshape(blocks, last + 1 - first, planes, width, owned)

    def copied(p):
        copies = jnp.broadcast_to(packed[p, tokens : tokens + depth][None], (blocks, depth, owned))
        pieces = lax.all_to_all(copies, "seq", 0, 0, tiled=True)
        return pieces.reshape(blocks, 1, planes, width, owned)

    starts = call(
        functools.partial(shuffle_body, planes, width),
        shape((planes, tokens, owned), BF),
        out_grad,
    )
    grad = lax.dynamic_index_in_dim(starts, lax.axis_index("pipe"), 0, keepdims=False)
    swap = [(0, 1), (1, 0)]
    other = lax.ppermute(grad, "tp", swap)

    saved = {planes - 1: recomputed(planes - 1)}
    first_weights, saved[planes - 1], source, grad, other = lax.optimization_barrier(
        (copied(planes - 1), saved[planes - 1], packed, grad, other)
    )
    weights = {planes - 1: (first_weights, 0)}
    last = planes - 2
    for size in (2, 3, planes):
        first = max(0, last - size + 1)
        if last >= first:
            group = gathered(source, first, last)
            weights.update({p: (group, p - first) for p in range(first, last + 1)})
        last = first - 1

    def filter_sums(p, operands, sums):
        halves = owned // TILE
        result = shape((planes * halves, AUX, TILE), BF)
        operands = [*operands[:5], packed, before, *operands[5:]]
        specs = [whole(x) for x in operands]
        specs[5:7] = [own_block(p), plane(before, p, tokens)]
        aliases = {}
        if sums is not None:
            aliases = {len(operands): 0}
            operands.append(sums)
            specs.append(pl.BlockSpec(memory_space=pl.ANY))
        return call(
            functools.partial(filters_body, groups),
            result,
            *operands,
            grid=(1,),
            in_specs=specs,
            out_specs=pl.BlockSpec((halves, AUX, TILE), lambda i, p=p: (p, 0, 0)),
            input_output_aliases=aliases,
            scratch_shapes=[
                pltpu.VMEM((KL + PAD, owned), F32),
                pltpu.VMEM((TILE // GW * KL, WIN), F32),
            ],
        )

    outs = [None] * planes
    sums = None
    late = None
    for p in range(planes - 1, -1, -1):
        group, at = weights[p]
        for q in range(p, max(p - 4, -1) if p == planes - 2 else p - 1, -1):
            if q not in saved:
                saved[q] = recomputed(q)
                if p == planes - 2:
                    group, saved[q] = lax.optimization_barrier((group, saved[q]))
        f0, f1, f2, mixed, back, turned = saved[p]
        if p + 1 < planes:
            other = lax.ppermute(grad, "tp", swap)
        partial = pl.pallas_call(
            project_body,
            out_shape=shape((planes, tokens, owned), BF),
            grid_spec=pltpu.PrefetchScalarGridSpec(
                num_scalar_prefetch=1,
                grid=(2,),
                in_specs=[
                    pl.BlockSpec((tokens, owned), lambda z, t: (0, 0)),
                    pl.BlockSpec((tokens, owned), lambda z, t: (0, 0)),
                    pl.BlockSpec(
                        (blocks, 1, planes // 2, width, owned), lambda z, t, at=at: (0, at, z, 0, 0)
                    ),
                ],
                out_specs=pl.BlockSpec((planes // 2, tokens, owned), lambda z, t: (z, 0, 0)),
            ),
            compiler_params=pltpu.CompilerParams(vmem_limit_bytes=VMEM_LIMIT),
            interpret=INTERPRET,
        )(tp_index, grad, other, group)
        parts = lax.all_to_all(partial, "pipe", 0, 0, tiled=True)
        send, dgate, early = call(
            gate_body,
            (
                shape((KL + PAD, owned), BF),
                shape((KL, owned), BF),
                shape((PAD, owned), BF),
            ),
            parts,
            f0,
        )
        near = from_next(send, 1)
        far = from_next(early, 2)
        if late is not None:
            send, late[0] = lax.optimization_barrier((send, late[0]))
            sums = filter_sums(p + 1, late, sums)
            near, sums = lax.optimization_barrier((near, sums))
        results = (shape((KL, owned), BF), shape((KL, owned), F32))
        operands = (send, dgate, near, far, f1, f2, mixed, back, packed, grad)
        new_grad, dkv = call(
            functools.partial(finish_body, groups),
            results,
            *operands,
            grid=(1,),
            in_specs=[aux_block(p) if x is packed else whole(x) for x in operands],
            out_specs=tuple(whole(r) for r in results),
            scratch_shapes=[pltpu.VMEM((KL + EDGE, owned), F32)] * 3,
        )
        late = [dgate, mixed, dkv, f1, f2, send, turned]
        outs[p] = new_grad
        grad = new_grad

    sums = filter_sums(0, late, sums)
    exchanged = lax.all_to_all(sums, "seq", 0, 0, tiled=True)
    summed = call(
        functools.partial(sum_body, blocks), shape((blocks, AUX, TILE), BF), exchanged
    )
    summed = lax.all_to_all(summed, "seq", 0, 0, tiled=True)
    merged = call(merge_body, shape((planes, tokens + AUX, owned), BF), summed, *outs)
    results = lax.all_to_all(merged, "pipe", 0, 0, tiled=True)
    input_grad, short_result, long_result = call(
        functools.partial(spread_body, slices, width),
        (shape((tokens, half), BF), shape((KS, 8, half), F32), shape((dims, KL), F32)),
        results,
    )
    return input_grad[None], short_result[None, :, :3], long_result[None]


def solution(mesh):
    in_specs = (
        P("pipe", ("seq", "tp"), None),
        P("seq", "tp"),
        P("pipe", None, None, "tp"),
        P("pipe", "tp", None),
        P("pipe", "tp", "seq"),
    )
    out_specs = (P("pipe", "seq", "tp"), P("pipe", None, None, "tp"), P("pipe", "tp", None))
    return jax.shard_map(
        per_device, mesh=mesh, in_specs=in_specs, out_specs=out_specs, check_vma=False
    )
```

profile of v0, /device:TPU:2, one launch (start us, length us, event | category | flops | bytes accessed | tf_op | source)
XLA Modules:
  0.0 500.8 jit_solution(9526353165594751515)
XLA Ops:
  13.7 52.7 %all_to_all.65.own_ref.aux_ref = bf16[8,432,256]{2,1,0:T(8,128)(2,1)S(1)} all-to-all(bf16[8,432,256]{2,1,0:T(8,128)(2,1)S(1)} %shard_map.76), channel_id=1, replica_groups=mesh['pipe'=8,'seq'=16,'tp'=2] {'pipe'}, dimensions={0} | all-to-all | bytes 3538944 | tf_op jit(solution)/shard_map/all_to_all | solution.py:362
  68.1 7.6 %all-to-all-start.1 = ((bf16[16,256,256]{2,1,0:T(8,128)(2,1)}), bf16[16,256,256]{2,1,0:T(8,128)(2,1)}, u32[]{:S(2)}, u32[]{:S(2)}) async-start(bf16[16,256,256]{2,1,0:T(8,128)(2,1)} %broadcast_in_dim.17), calls=%async_computation.1 | async-start | bytes 4194304 | tf_op jit(solution)/shard_map/all_to_all | solution.py:418
  76.6 3.4 collective-permute-start.1
  80.5 4.6 collective-permute-start.2
  85.1 4.3 collective-permute-start.3
  89.5 20.0 %collective-permute-done.2.prev2_ref = bf16[8,16,256]{2,1,0:T(8,128)(2,1)S(1)} collective-permute-done((bf16[8,16,256]{2,1,0:T(8,128)(2,1)S(1)}, bf16[8,16,256]{2,1,0:T(8,128)(2,1)S(1)}, u32[]{:S(2)}, u32[]{:S(2)}) %collective-permute-start.2) | collective-permute-done | bytes 65568 | tf_op jit(solution)/shard_map/ppermute | solution.py:329
  109.6 3.5 collective-permute-done.1.prev_ref
  123.9 17.9 %all_to_all.66.parts_ref = bf16[8,128,256]{2,1,0:T(8,128)(2,1)S(1)} all-to-all(bf16[8,128,256]{2,1,0:T(8,128)(2,1)S(1)} %shard_map.79), channel_id=1, replica_groups=mesh['pipe'=8,'seq'=16,'tp'=2] {'pipe'}, dimensions={0} | all-to-all | bytes 1048576 | tf_op jit(solution)/shard_map/all_to_all | solution.py:499
  141.9 2.9 collective-permute-start.5
  147.2 4.6 collective-permute-done.6.far_ref
  179.0 20.8 %all_to_all.67.parts_ref = bf16[8,128,256]{2,1,0:T(8,128)(2,1)S(1)} all-to-all(bf16[8,128,256]{2,1,0:T(8,128)(2,1)S(1)} %shard_map.86), channel_id=1, replica_groups=mesh['pipe'=8,'seq'=16,'tp'=2] {'pipe'}, dimensions={0} | all-to-all | bytes 1048576 | tf_op jit(solution)/shard_map/all_to_all | solution.py:499
  200.0 4.4 collective-permute-start.8
  208.3 3.1 collective-permute-done.9.far_ref
  214.5 20.5 %all_to_all.68.parts_ref = bf16[8,128,256]{2,1,0:T(8,128)(2,1)S(1)} all-to-all(bf16[8,128,256]{2,1,0:T(8,128)(2,1)S(1)} %shard_map.90), channel_id=1, replica_groups=mesh['pipe'=8,'seq'=16,'tp'=2] {'pipe'}, dimensions={0} | all-to-all | bytes 1048576 | tf_op jit(solution)/shard_map/all_to_all | solution.py:499
  235.1 3.8 collective-permute-start.11
  242.0 4.0 collective-permute-done.12.far_ref
  252.0 20.8 %all_to_all.69.parts_ref = bf16[8,128,256]{2,1,0:T(8,128)(2,1)S(1)} all-to-all(bf16[8,128,256]{2,1,0:T(8,128)(2,1)S(1)} %shard_map.94), channel_id=1, replica_groups=mesh['pipe'=8,'seq'=16,'tp'=2] {'pipe'}, dimensions={0} | all-to-all | bytes 1048576 | tf_op jit(solution)/shard_map/all_to_all | solution.py:499
  272.9 3.5 collective-permute-start.14
  280.4 3.1 collective-permute-done.15.far_ref
  286.5 20.5 %all_to_all.70.parts_ref = bf16[8,128,256]{2,1,0:T(8,128)(2,1)S(1)} all-to-all(bf16[8,128,256]{2,1,0:T(8,128)(2,1)S(1)} %shard_map.98), channel_id=1, replica_groups=mesh['pipe'=8,'seq'=16,'tp'=2] {'pipe'}, dimensions={0} | all-to-all | bytes 1048576 | tf_op jit(solution)/shard_map/all_to_all | solution.py:499
  307.1 3.0 collective-permute-start.17
  313.5 3.6 collective-permute-done.18.far_ref
  321.6 3.5 all-to-all-start.7
  330.9 12.2 %all-to-all-done.7.parts_ref = bf16[8,128,256]{2,1,0:T(8,128)(2,1)S(1)} async-done(((bf16[8,128,256]{2,1,0:T(8,128)(2,1)}), bf16[8,128,256]{2,1,0:T(8,128)(2,1)S(1)}, u32[]{:S(2)}, u32[]{:S(2)}) %all-to-all-start.7) | async-done | bytes 524320 | tf_op jit(solution)/shard_map/all_to_all | solution.py:499
  344.2 3.3 collective-permute-start.20
  362.6 3.7 all-to-all-start.8
  372.2 12.2 %all-to-all-done.8.parts_ref = bf16[8,128,256]{2,1,0:T(8,128)(2,1)S(1)} async-done(((bf16[8,128,256]{2,1,0:T(8,128)(2,1)}), bf16[8,128,256]{2,1,0:T(8,128)(2,1)S(1)}, u32[]{:S(2)}, u32[]{:S(2)}) %all-to-all-start.8) | async-done | bytes 524320 | tf_op jit(solution)/shard_map/all_to_all | solution.py:499
  401.8 3.5 all-to-all-start.9
  411.2 12.2 %all-to-all-done.9.parts_ref = bf16[8,128,256]{2,1,0:T(8,128)(2,1)S(1)} async-done(((bf16[8,128,256]{2,1,0:T(8,128)(2,1)}), bf16[8,128,256]{2,1,0:T(8,128)(2,1)S(1)}, u32[]{:S(2)}, u32[]{:S(2)}) %all-to-all-start.9) | async-done | bytes 524320 | tf_op jit(solution)/shard_map/all_to_all | solution.py:499
  437.8 20.5 %all_to_all.71.in_ref = bf16[16,48,128]{2,1,0:T(8,128)(2,1)S(1)} all-to-all(bf16[16,48,128]{2,1,0:T(8,128)(2,1)S(1)} %shard_map.117), channel_id=1, replica_groups=mesh['pipe'=8,'seq'=16,'tp'=2] {'seq'}, dimensions={0} | all-to-all | bytes 393216 | tf_op jit(solution)/shard_map/all_to_all | solution.py:532
  458.3 11.6 %all_to_all.72.sums_ref = bf16[16,48,128]{2,1,0:T(8,128)(2,1)S(1)} all-to-all(bf16[16,48,128]{2,1,0:T(8,128)(2,1)S(1)} %shard_map.118), channel_id=1, replica_groups=mesh['pipe'=8,'seq'=16,'tp'=2] {'seq'}, dimensions={0} | all-to-all | bytes 393216 | tf_op jit(solution)/shard_map/all_to_all | solution.py:536
  470.0 21.5 %all_to_all.73.in_ref = bf16[8,176,256]{2,1,0:T(8,128)(2,1)S(1)} all-to-all(bf16[8,176,256]{2,1,0:T(8,128)(2,1)S(1)} %shard_map.119), channel_id=1, replica_groups=mesh['pipe'=8,'seq'=16,'tp'=2] {'pipe'}, dimensions={0} | all-to-all | bytes 1441792 | tf_op jit(solution)/shard_map/all_to_all | solution.py:538
  (400 shorter events, 148.6 us)
Async XLA Ops:
  7.2 2.2 collective-permute-start
  68.1 50.5 %all-to-all-start.1 = ((bf16[16,256,256]{2,1,0:T(8,128)(2,1)}), bf16[16,256,256]{2,1,0:T(8,128)(2,1)}, u32[]{:S(2)}, u32[]{:S(2)}) async-start(bf16[16,256,256]{2,1,0:T(8,128)(2,1)} %broadcast_in_dim.17), calls=%async_computation.1 | async-start | bytes 4194304 | tf_op jit(solution)/shard_map/all_to_all | solution.py:418
  75.7 100.3 %all-gather.7.cloned.1.call-start = ((), (), s32[]{:S(2)}) async-start(), calls=%async_computation.13 | async-start | bytes 4456448 | tf_op jit(solution)/shard_map/all_gather | solution.py:413
  76.6 36.5 %collective-permute-start.1 = (bf16[8,128,256]{2,1,0:T(8,128)(2,1)}, bf16[8,128,256]{2,1,0:T(8,128)(2,1)S(1)}, u32[]{:S(2)}, u32[]{:S(2)}) collective-permute-start(bf16[8,128,256]{2,1,0:T(8,128)(2,1)} %slice.35), channel_id=1, source_target_pairs={{0,2},{2,4},{4,6},{6,8},{8,10},{10,12},{12,14},{14,16},{16,18},{18... | collective-permute-start | bytes 1572872 | tf_op jit(solution)/shard_map/ppermute | solution.py:329
  80.5 29.0 %collective-permute-start.2 = (bf16[8,16,256]{2,1,0:T(8,128)(2,1)S(1)}, bf16[8,16,256]{2,1,0:T(8,128)(2,1)S(1)}, u32[]{:S(2)}, u32[]{:S(2)}) collective-permute-start(bf16[8,16,256]{2,1,0:T(8,128)(2,1)S(1)} %get-tuple-element.326), channel_id=1, source_target_pairs={{0,4},{2,6},{4,8},{6,10},{8,12},{10,14},{12,16},{14,18},{16,20},{1... | collective-permute-start | bytes 196616 | tf_op jit(solution)/shard_map/ppermute | solution.py:329
  85.1 24.4 %collective-permute-start.3 = (bf16[8,16,256]{2,1,0:T(8,128)(2,1)S(1)}, bf16[8,16,256]{2,1,0:T(8,128)(2,1)S(1)}, u32[]{:S(2)}, u32[]{:S(2)}) collective-permute-start(bf16[8,16,256]{2,1,0:T(8,128)(2,1)S(1)} %get-tuple-element.325), channel_id=1, source_target_pairs={{2,0},{4,2},{6,4},{8,6},{10,8},{12,10},{14,12},{16,14},{18,16},{20... | collective-permute-start | bytes 196616 | tf_op jit(solution)/shard_map/ppermute | solution.py:324
  89.4 28.5 %collective-permute-start.4 = (bf16[128,256]{1,0:T(8,128)(2,1)S(1)}, bf16[128,256]{1,0:T(8,128)(2,1)S(1)}, u32[]{:S(2)}, u32[]{:S(2)}) collective-permute-start(bf16[128,256]{1,0:T(8,128)(2,1)S(1)} %dynamic-slice_bitcast_fusion.own_ref.grad_ref), channel_id=1, source_target_pairs={{0,1},{1,0},{2,3},{3,2},{4,5},{5,4},{6,7},{7,6},{8,9},{9,8},{10,11... | collective-permute-start | bytes 196616 | tf_op jit(solution)/shard_map/ppermute | solution.py:428
  119.5 128.9 %all-gather.9.cloned.1.call-start = ((), (), s32[]{:S(2)}) async-start(), calls=%async_computation.14 | async-start | bytes 6684672 | tf_op jit(solution)/shard_map/all_gather | solution.py:413
  120.3 237.4 %all-gather.11.cloned.1.call-start = ((), (), s32[]{:S(2)}) async-start(), calls=%async_computation.15 | async-start | bytes 4456448 | tf_op jit(solution)/shard_map/all_gather | solution.py:413
  141.9 9.9 %collective-permute-start.5 = (bf16[144,256]{1,0:T(8,128)(2,1)S(1)}, bf16[144,256]{1,0:T(8,128)(2,1)S(1)}, u32[]{:S(2)}, u32[]{:S(2)}) collective-permute-start(bf16[144,256]{1,0:T(8,128)(2,1)S(1)} %get-tuple-element.170.send_ref), channel_id=1, source_target_pairs={{2,0},{4,2},{6,4},{8,6},{10,8},{12,10},{14,12},{16,14},{18,16},{20... | collective-permute-start | bytes 221192 | tf_op jit(solution)/shard_map/ppermute | solution.py:324
  144.8 7.0 %collective-permute-start.6 = (bf16[16,256]{1,0:T(8,128)(2,1)S(1)}, bf16[16,256]{1,0:T(8,128)(2,1)S(1)}, u32[]{:S(2)}, u32[]{:S(2)}) collective-permute-start(bf16[16,256]{1,0:T(8,128)(2,1)S(1)} %get-tuple-element.172), channel_id=1, source_target_pairs={{4,0},{6,2},{8,4},{10,6},{12,8},{14,10},{16,12},{18,14},{20,16},{2... | collective-permute-start | bytes 24584 | tf_op jit(solution)/shard_map/ppermute | solution.py:324
  153.5 22.4 %collective-permute-start.7 = (bf16[128,256]{1,0:T(8,128)(2,1)S(1)}, bf16[128,256]{1,0:T(8,128)(2,1)S(1)}, u32[]{:S(2)}, u32[]{:S(2)}) collective-permute-start(bf16[128,256]{1,0:T(8,128)(2,1)S(1)} %get-tuple-element.177.own_ref.grad_ref.refs_7_), channel_id=1, source_target_pairs={{0,1},{1,0},{2,3},{3,2},{4,5},{5,4},{6,7},{7,6},{8,9},{9,8},{10,11... | collective-permute-start | bytes 196616 | tf_op jit(solution)/shard_map/ppermute | solution.py:480
  200.0 8.3 %collective-permute-start.8 = (bf16[144,256]{1,0:T(8,128)(2,1)S(1)}, bf16[144,256]{1,0:T(8,128)(2,1)S(1)}, u32[]{:S(2)}, u32[]{:S(2)}) collective-permute-start(bf16[144,256]{1,0:T(8,128)(2,1)S(1)} %get-tuple-element.209.send_ref), channel_id=1, source_target_pairs={{2,0},{4,2},{6,4},{8,6},{10,8},{12,10},{14,12},{16,14},{18,16},{20... | collective-permute-start | bytes 221192 | tf_op jit(solution)/shard_map/ppermute | solution.py:324
  204.4 7.0 %collective-permute-start.9 = (bf16[16,256]{1,0:T(8,128)(2,1)S(1)}, bf16[16,256]{1,0:T(8,128)(2,1)S(1)}, u32[]{:S(2)}, u32[]{:S(2)}) collective-permute-start(bf16[16,256]{1,0:T(8,128)(2,1)S(1)} %get-tuple-element.215), channel_id=1, source_target_pairs={{4,0},{6,2},{8,4},{10,6},{12,8},{14,10},{16,12},{18,14},{20,16},{2... | collective-permute-start | bytes 24584 | tf_op jit(solution)/shard_map/ppermute | solution.py:324
  212.3 1.3 collective-permute-start.10
  235.1 6.9 %collective-permute-start.11 = (bf16[144,256]{1,0:T(8,128)(2,1)S(1)}, bf16[144,256]{1,0:T(8,128)(2,1)S(1)}, u32[]{:S(2)}, u32[]{:S(2)}) collective-permute-start(bf16[144,256]{1,0:T(8,128)(2,1)S(1)} %get-tuple-element.223.send_ref), channel_id=1, source_target_pairs={{2,0},{4,2},{6,4},{8,6},{10,8},{12,10},{14,12},{16,14},{18,16},{20... | collective-permute-start | bytes 221192 | tf_op jit(solution)/shard_map/ppermute | solution.py:324
  238.9 7.0 %collective-permute-start.12 = (bf16[16,256]{1,0:T(8,128)(2,1)S(1)}, bf16[16,256]{1,0:T(8,128)(2,1)S(1)}, u32[]{:S(2)}, u32[]{:S(2)}) collective-permute-start(bf16[16,256]{1,0:T(8,128)(2,1)S(1)} %get-tuple-element.230), channel_id=1, source_target_pairs={{4,0},{6,2},{8,4},{10,6},{12,8},{14,10},{16,12},{18,14},{20,16},{2... | collective-permute-start | bytes 24584 | tf_op jit(solution)/shard_map/ppermute | solution.py:324
  246.8 1.6 collective-permute-start.13
  272.9 7.5 %collective-permute-start.14 = (bf16[144,256]{1,0:T(8,128)(2,1)S(1)}, bf16[144,256]{1,0:T(8,128)(2,1)S(1)}, u32[]{:S(2)}, u32[]{:S(2)}) collective-permute-start(bf16[144,256]{1,0:T(8,128)(2,1)S(1)} %get-tuple-element.238.send_ref), channel_id=1, source_target_pairs={{2,0},{4,2},{6,4},{8,6},{10,8},{12,10},{14,12},{16,14},{18,16},{20... | collective-permute-start | bytes 221192 | tf_op jit(solution)/shard_map/ppermute | solution.py:324
  276.4 7.0 %collective-permute-start.15 = (bf16[16,256]{1,0:T(8,128)(2,1)S(1)}, bf16[16,256]{1,0:T(8,128)(2,1)S(1)}, u32[]{:S(2)}, u32[]{:S(2)}) collective-permute-start(bf16[16,256]{1,0:T(8,128)(2,1)S(1)} %get-tuple-element.245), channel_id=1, source_target_pairs={{4,0},{6,2},{8,4},{10,6},{12,8},{14,10},{16,12},{18,14},{20,16},{2... | collective-permute-start | bytes 24584 | tf_op jit(solution)/shard_map/ppermute | solution.py:324
  284.4 1.3 collective-permute-start.16
  307.1 6.4 %collective-permute-start.17 = (bf16[144,256]{1,0:T(8,128)(2,1)S(1)}, bf16[144,256]{1,0:T(8,128)(2,1)S(1)}, u32[]{:S(2)}, u32[]{:S(2)}) collective-permute-start(bf16[144,256]{1,0:T(8,128)(2,1)S(1)} %get-tuple-element.253.send_ref), channel_id=1, source_target_pairs={{2,0},{4,2},{6,4},{8,6},{10,8},{12,10},{14,12},{16,14},{18,16},{20... | collective-permute-start | bytes 221192 | tf_op jit(solution)/shard_map/ppermute | solution.py:324
  310.1 7.0 %collective-permute-start.18 = (bf16[16,256]{1,0:T(8,128)(2,1)S(1)}, bf16[16,256]{1,0:T(8,128)(2,1)S(1)}, u32[]{:S(2)}, u32[]{:S(2)}) collective-permute-start(bf16[16,256]{1,0:T(8,128)(2,1)S(1)} %get-tuple-element.260), channel_id=1, source_target_pairs={{4,0},{6,2},{8,4},{10,6},{12,8},{14,10},{16,12},{18,14},{20,16},{2... | collective-permute-start | bytes 24584 | tf_op jit(solution)/shard_map/ppermute | solution.py:324
  321.6 21.6 %all-to-all-start.7 = ((bf16[8,128,256]{2,1,0:T(8,128)(2,1)}), bf16[8,128,256]{2,1,0:T(8,128)(2,1)S(1)}, u32[]{:S(2)}, u32[]{:S(2)}) async-start(bf16[8,128,256]{2,1,0:T(8,128)(2,1)} %copy-done.5), calls=%async_computation.7 | async-start | bytes 1048576 | tf_op jit(solution)/shard_map/all_to_all | solution.py:499
  344.2 11.8 %collective-permute-start.20 = (bf16[144,256]{1,0:T(8,128)(2,1)S(1)}, bf16[144,256]{1,0:T(8,128)(2,1)S(1)}, u32[]{:S(2)}, u32[]{:S(2)}) collective-permute-start(bf16[144,256]{1,0:T(8,128)(2,1)S(1)} %get-tuple-element.268.send_ref), channel_id=1, source_target_pairs={{2,0},{4,2},{6,4},{8,6},{10,8},{12,10},{14,12},{16,14},{18,16},{20... | collective-permute-start | bytes 221192 | tf_op jit(solution)/shard_map/ppermute | solution.py:324
  347.6 8.5 %collective-permute-start.21 = (bf16[16,256]{1,0:T(8,128)(2,1)S(1)}, bf16[16,256]{1,0:T(8,128)(2,1)S(1)}, u32[]{:S(2)}, u32[]{:S(2)}) collective-permute-start(bf16[16,256]{1,0:T(8,128)(2,1)S(1)} %get-tuple-element.275), channel_id=1, source_target_pairs={{4,0},{6,2},{8,4},{10,6},{12,8},{14,10},{16,12},{18,14},{20,16},{2... | collective-permute-start | bytes 24584 | tf_op jit(solution)/shard_map/ppermute | solution.py:324
  362.6 21.8 %all-to-all-start.8 = ((bf16[8,128,256]{2,1,0:T(8,128)(2,1)}), bf16[8,128,256]{2,1,0:T(8,128)(2,1)S(1)}, u32[]{:S(2)}, u32[]{:S(2)}) async-start(bf16[8,128,256]{2,1,0:T(8,128)(2,1)} %shard_map.107), calls=%async_computation.8 | async-start | bytes 1048576 | tf_op jit(solution)/shard_map/all_to_all | solution.py:499
  385.6 11.3 %collective-permute-start.23 = (bf16[144,256]{1,0:T(8,128)(2,1)S(1)}, bf16[144,256]{1,0:T(8,128)(2,1)S(1)}, u32[]{:S(2)}, u32[]{:S(2)}) collective-permute-start(bf16[144,256]{1,0:T(8,128)(2,1)S(1)} %get-tuple-element.283.send_ref), channel_id=1, source_target_pairs={{2,0},{4,2},{6,4},{8,6},{10,8},{12,10},{14,12},{16,14},{18,16},{20... | collective-permute-start | bytes 221192 | tf_op jit(solution)/shard_map/ppermute | solution.py:324
  387.5 9.3 %collective-permute-start.24 = (bf16[16,256]{1,0:T(8,128)(2,1)S(1)}, bf16[16,256]{1,0:T(8,128)(2,1)S(1)}, u32[]{:S(2)}, u32[]{:S(2)}) collective-permute-start(bf16[16,256]{1,0:T(8,128)(2,1)S(1)} %get-tuple-element.290), channel_id=1, source_target_pairs={{4,0},{6,2},{8,4},{10,6},{12,8},{14,10},{16,12},{18,14},{20,16},{2... | collective-permute-start | bytes 24584 | tf_op jit(solution)/shard_map/ppermute | solution.py:324
  401.8 21.6 %all-to-all-start.9 = ((bf16[8,128,256]{2,1,0:T(8,128)(2,1)}), bf16[8,128,256]{2,1,0:T(8,128)(2,1)S(1)}, u32[]{:S(2)}, u32[]{:S(2)}) async-start(bf16[8,128,256]{2,1,0:T(8,128)(2,1)} %shard_map.112), calls=%async_computation.9 | async-start | bytes 1048576 | tf_op jit(solution)/shard_map/all_to_all | solution.py:499
  424.5 11.3 %collective-permute-start.26 = (bf16[144,256]{1,0:T(8,128)(2,1)S(1)}, bf16[144,256]{1,0:T(8,128)(2,1)S(1)}, u32[]{:S(2)}, u32[]{:S(2)}) collective-permute-start(bf16[144,256]{1,0:T(8,128)(2,1)S(1)} %get-tuple-element.300.send_ref), channel_id=1, source_target_pairs={{2,0},{4,2},{6,4},{8,6},{10,8},{12,10},{14,12},{16,14},{18,16},{20... | collective-permute-start | bytes 221192 | tf_op jit(solution)/shard_map/ppermute | solution.py:324
  426.4 9.3 %collective-permute-start.27 = (bf16[16,256]{1,0:T(8,128)(2,1)S(1)}, bf16[16,256]{1,0:T(8,128)(2,1)S(1)}, u32[]{:S(2)}, u32[]{:S(2)}) collective-permute-start(bf16[16,256]{1,0:T(8,128)(2,1)S(1)} %get-tuple-element.306), channel_id=1, source_target_pairs={{4,0},{6,2},{8,4},{10,6},{12,8},{14,10},{16,12},{18,14},{20,16},{2... | collective-permute-start | bytes 24584 | tf_op jit(solution)/shard_map/ppermute | solution.py:324
  (150 other events, 1073.1 us)
Sparse Core Ops, SparseCore 0:
  119.6 52.5 all-gather.6
  175.2 66.1 all-gather.8
  243.9 58.0 all-gather.10
where the time goes:
time: 509 us; the launch traced here: 501 us
  blocking collectives  207 us (41%)
  waiting for transfers between devices  88.2 us (17%)
  local copies, waits for them, and re-layouts  75.4 us (15%)
  starting transfers between devices  73 us (14%)
  Pallas kernels  41.9 us (8%)
  between operations  15.6 us (3%)
    all_to_all x5, blocking collectives, per_device(): parts = lax.all_to_all(partial, 'pipe', 0, 0, tiled=True)  100 us
    unnamed x296, local copies, waits for them, and re-layouts  71.3 us
    all_to_all x1, blocking collectives, per_device(): packed = lax.all_to_all(packed, 'pipe', 0, 0, tiled=True)  52.7 us
    ppermute x17, starting transfers between devices, from_next(): return lax.ppermute(x, 'seq', [(i, i - by) for i in range(by, size)])  45.6 us
    all_to_all x3, waiting for transfers between devices, per_device(): parts = lax.all_to_all(partial, 'pipe', 0, 0, tiled=True)  36.6 us
    pallas_call x36, Pallas kernels, call(): pl.pallas_call(body, out_shape=out_shape, compiler_params=pltpu.CompilerP...  31.6 us
    ppermute x2, waiting for transfers between devices, from_before(): return lax.ppermute(x, 'seq', [(i, i + by) for i in range(size - by)])  23.5 us
    all_to_all x1, blocking collectives, per_device(): results = lax.all_to_all(merged, 'pipe', 0, 0, tiled=True)  21.5 us
  transfers between devices with their start and end apart: 35, of which 18 were waited for; matrix products, arithmetic and copies ran while one was open for 1% of the time, Pallas kernels for 7%

commit v1 on v0

--- a/solution.py
+++ b/solution.py
@@ -13,6 +13,7 @@
 GW = 16
 AUX = 48
 EDGE = 8
+REACH = KL + EDGE
 PAD = 16
 WIN = 2 * KL
 BF = jnp.bfloat16
@@ -149,9 +150,7 @@
 
 
 def recompute_body(
-    groups, own_ref, prev_ref, prev2_ref, next_ref, aux_ref,
-    f0_ref, f1_ref, f2_ref, mixed_ref, back_ref, turned_ref,
-    rows_ref, band_ref,
+    groups, own_ref, prev_ref, prev2_ref, next_ref, aux_ref, features_ref, back_ref, rows_ref, band_ref,
 ):
     rows_ref[0:PAD, :] = prev2_ref[...].astype(F32)
     rows_ref[PAD : PAD + KL, :] = prev_ref[...].astype(F32)
@@ -166,11 +165,11 @@
             total = total + taps[3 * j + f : 3 * j + f + 1] * rows_ref[start - j : start - j + count, :]
         return total
 
-    f0_ref[...] = feature(0, 0, KL)
-    key_tail = feature(1, 0, KL + EDGE)
-    value_tail = feature(2, 0, KL + EDGE)
-    f1_ref[...] = key_tail
-    f2_ref[...] = value_tail
+    features_ref[0:REACH, :] = feature(0, 0, REACH)
+    key_tail = feature(1, 0, REACH)
+    value_tail = feature(2, 0, REACH)
+    features_ref[REACH : 2 * REACH, :] = key_tail
+    features_ref[2 * REACH : 3 * REACH, :] = value_tail
     kv = jnp.concatenate([feature(1, -KL, KL) * feature(2, -KL, KL), key_tail * value_tail], axis=0)
     window = kv[:WIN].astype(BF)
     late = kv[EDGE : EDGE + WIN].astype(BF)
@@ -185,12 +184,12 @@
         band_ref[g * KL : (g + 1) * KL, :] = pltpu.roll(wide, 0, 1, stride=1, stride_axis=0).astype(BF)
         wide = jnp.broadcast_to(behind[g : g + 1], (KL, WIN))
         back_ref[g * KL : (g + 1) * KL, :] = pltpu.roll(wide, 0, 1, stride=1, stride_axis=0).astype(BF)
-    mixed_ref[0:KL, :] = grouped(band_ref, KL, window, groups)
-    mixed_ref[KL:, :] = grouped(edge_rows(band_ref, groups), PAD, late, groups)[PAD - EDGE :]
+    features_ref[3 * REACH : 3 * REACH + KL, :] = grouped(band_ref, KL, window, groups)
+    features_ref[3 * REACH + KL :, :] = grouped(edge_rows(band_ref, groups), PAD, late, groups)[PAD - EDGE :]
     source = lax.broadcasted_iota(jnp.int32, (WIN, WIN), 0)
     target = lax.broadcasted_iota(jnp.int32, (WIN, WIN), 1)
     mirror = (source + target == WIN - 1).astype(F32).astype(BF)
-    turned_ref[...] = dot(mirror, window).astype(BF)
+    back_ref[groups * KL :, :] = dot(mirror, window).astype(BF)
 
 
 def project_body(tp_ref, own_ref, other_ref, w_ref, out_ref):
@@ -202,12 +201,12 @@
         out_ref[z] = dot(rows, w_ref[:, 0, z].reshape(slices * width, owned)).astype(BF)
 
 
-def gate_body(parts_ref, f0_ref, send_ref, dgate_ref, early_ref):
+def gate_body(parts_ref, features_ref, send_ref, dgate_ref, early_ref):
     total = parts_ref[0].astype(F32)
     for z in range(1, parts_ref.shape[0]):
         total = total + parts_ref[z].astype(F32)
     dgate = total.astype(BF)
-    dmixed = (dgate.astype(F32) * f0_ref[...]).astype(BF)
+    dmixed = (dgate.astype(F32) * features_ref[0:KL, :]).astype(BF)
     send_ref[0:KL, :] = dmixed
     send_ref[KL:, :] = dgate[:PAD]
     dgate_ref[...] = dgate
@@ -215,8 +214,8 @@
 
 
 def finish_body(
-    groups, send_ref, dgate_ref, near_ref, far_ref, f1_ref, f2_ref, mixed_ref, back_ref, aux_ref, grad_ref,
-    out_ref, dkv_ref, d0_ref, d1_ref, d2_ref,
+    groups, send_ref, dgate_ref, near_ref, far_ref, features_ref, back_ref, aux_ref, grad_ref,
+    out_ref, trail_ref, d0_ref, d1_ref, d2_ref,
 ):
     rows = jnp.concatenate(
         [send_ref[0:KL, :], near_ref[0:KL, :], far_ref[...]], axis=0
@@ -225,40 +224,35 @@
     late = rows.astype(F32)[EDGE : EDGE + WIN].astype(BF)
     main = grouped(back_ref, KL, window, groups)
     tail = grouped(edge_rows(back_ref, groups), PAD, late, groups)[PAD - EDGE :]
-    dkv_ref[...] = main
-    d0_ref[0:KL, :] = dgate_ref[...].astype(F32) * mixed_ref[0:KL, :]
-    d0_ref[KL:, :] = near_ref[KL:, :].astype(F32)[:EDGE] * mixed_ref[KL:, :]
-    d1_ref[0:KL, :] = main * f2_ref[0:KL, :]
-    d1_ref[KL:, :] = tail * f2_ref[KL:, :]
-    d2_ref[0:KL, :] = main * f1_ref[0:KL, :]
-    d2_ref[KL:, :] = tail * f1_ref[KL:, :]
+    key, value, mixed = REACH, 2 * REACH, 3 * REACH
+    d0_ref[0:KL, :] = dgate_ref[...].astype(F32) * features_ref[mixed : mixed + KL, :]
+    d0_ref[KL:, :] = near_ref[KL:, :].astype(F32)[:EDGE] * features_ref[mixed + KL :, :]
+    d1_ref[0:KL, :] = main * features_ref[value : value + KL, :]
+    d1_ref[KL:, :] = tail * features_ref[value + KL : mixed, :]
+    d2_ref[0:KL, :] = main * features_ref[key : key + KL, :]
+    d2_ref[KL:, :] = tail * features_ref[key + KL : value, :]
     taps = aux_ref[0:32, :].astype(F32)
     total = grad_ref[...].astype(F32)
-    for j in range(KS):
-        for f, ref in enumerate((d0_ref, d1_ref, d2_ref)):
+    for f, ref in enumerate((d0_ref, d1_ref, d2_ref)):
+        trail_ref[f * KL : (f + 1) * KL, :] = ref[0:KL, :]
+        for j in range(KS):
             total = total + taps[3 * j + f : 3 * j + f + 1] * ref[j : j + KL, :]
     out_ref[...] = total.astype(BF)
 
 
 def filters_body(
-    groups, dgate_ref, mixed_ref, dkv_ref, f1_ref, f2_ref, own_ref, prev_ref, send_ref, turned_ref,
-    *refs,
+    groups, trail_ref, send_ref, back_ref, own_ref, prev_ref, *refs,
 ):
     out_ref, rows_ref, skew_ref = refs[-3:]
     channels = own_ref.shape[1]
-    rows_ref[0:PAD, :] = prev_ref[KL - PAD :, :].astype(F32)
+    rows_ref[0:PAD, :] = prev_ref[...].astype(F32)
     rows_ref[PAD:, :] = own_ref[...].astype(F32)
-    dkv = dkv_ref[...]
-    grads = (
-        dgate_ref[...].astype(F32) * mixed_ref[0:KL, :],
-        dkv * f2_ref[0:KL, :],
-        dkv * f1_ref[0:KL, :],
-    )
     sums = []
     for j in range(KS):
         source = rows_ref[PAD - j : PAD - j + KL, :]
         for f in range(3):
-            sums.append(jnp.sum(grads[f] * source, axis=0, keepdims=True))
+            grads = trail_ref[f * KL : (f + 1) * KL, :]
+            sums.append(jnp.sum(grads * source, axis=0, keepdims=True))
     sums.append(jnp.zeros((32 - 3 * KS, channels), F32))
     short = jnp.concatenate(sums, axis=0).astype(BF)
     for u in range(channels // TILE):
@@ -271,7 +265,7 @@
         stacked = jnp.concatenate(
             [jnp.where(lane == g, grad, 0.0).astype(BF) for g in range(per)], axis=0
         )
-        skew_ref[...] = dot_nt(stacked, turned_ref[:, u * TILE : (u + 1) * TILE])
+        skew_ref[...] = dot_nt(stacked, back_ref[groups * KL :, u * TILE : (u + 1) * TILE])
         for g in range(per):
             rolled = pltpu.roll(skew_ref[g * KL : (g + 1) * KL, :], 0, 1, stride=1, stride_axis=0)
             lags.append(jnp.sum(rolled, axis=0, keepdims=True))
@@ -360,10 +354,14 @@
         swapped,
     )
     packed = lax.all_to_all(packed, "pipe", 0, 0, tiled=True)
-    rows = packed[:, :tokens]
-    before = from_before(rows, 1)
-    before2 = from_before(rows[:, tokens - PAD :], 2)
-    after = from_next(rows[:, :PAD], 1)
+    top = planes - 1
+
+    def surroundings(rows):
+        return (
+            from_before(rows, 1),
+            from_before(rows[:, tokens - PAD :], 2),
+            from_next(rows[:, :PAD], 1),
+        )
 
     def whole(x):
         return pl.BlockSpec(x.shape, lambda i: (0,) * len(x.shape))
@@ -377,15 +375,9 @@
     def aux_block(p):
         return plane(packed, p, AUX, (tokens + depth) // AUX)
 
-    def recomputed(p):
-        results = (
-            shape((KL, owned), F32),
-            shape((KL + EDGE, owned), F32),
-            shape((KL + EDGE, owned), F32),
-            shape((KL + EDGE, owned), F32),
-            shape((groups * KL, WIN), BF),
-            shape((WIN, owned), BF),
-        )
+    def recomputed(p, around, at):
+        results = (shape((4 * REACH, owned), F32), shape((groups * KL + WIN, owned), BF))
+        before, before2, after = around
         return call(
             functools.partial(recompute_body, groups),
             results,
@@ -397,9 +389,9 @@
             grid=(1,),
             in_specs=[
                 own_block(p),
-                plane(before, p, tokens),
-                plane(before2, p, PAD),
-                plane(after, p, PAD),
+                plane(before, at, tokens),
+                plane(before2, at, PAD),
+                plane(after, at, PAD),
                 aux_block(p),
             ],
             out_specs=tuple(whole(r) for r in results),
@@ -427,11 +419,14 @@
     swap = [(0, 1), (1, 0)]
     other = lax.ppermute(grad, "tp", swap)
 
-    saved = {planes - 1: recomputed(planes - 1)}
-    first_weights, saved[planes - 1], source, grad, other = lax.optimization_barrier(
-        (copied(planes - 1), saved[planes - 1], packed, grad, other)
-    )
-    weights = {planes - 1: (first_weights, 0)}
+    around = {top: (surroundings(packed[top:, :tokens]), 0)}
+    saved = {top: recomputed(top, *around[top])}
+    first_weights, saved[top], source, grad, other = lax.optimization_barrier(
+        (copied(top), saved[top], packed, grad, other)
+    )
+    others = surroundings(source[:top, :tokens])
+    around.update({p: (others, p) for p in range(top)})
+    weights = {top: (first_weights, 0)}
     last = planes - 2
     for size in (2, 3, planes):
         first = max(0, last - size + 1)
@@ -443,9 +438,10 @@
     def filter_sums(p, operands, sums):
         halves = owned // TILE
         result = shape((planes * halves, AUX, TILE), BF)
-        operands = [*operands[:5], packed, before, *operands[5:]]
+        (before, _, _), at = around[p]
         specs = [whole(x) for x in operands]
-        specs[5:7] = [own_block(p), plane(before, p, tokens)]
+        specs += [own_block(p), plane(before, at, PAD, tokens // PAD - 1)]
+        operands = [*operands, packed, before]
         aliases = {}
         if sums is not None:
             aliases = {len(operands): 0}
@@ -470,12 +466,11 @@
     late = None
     for p in range(planes - 1, -1, -1):
         group, at = weights[p]
-        for q in range(p, max(p - 4, -1) if p == planes - 2 else p - 1, -1):
-            if q not in saved:
-                saved[q] = recomputed(q)
-                if p == planes - 2:
-                    group, saved[q] = lax.optimization_barrier((group, saved[q]))
-        f0, f1, f2, mixed, back, turned = saved[p]
+        if p == top - 1:
+            for q in range(top):
+                saved[q] = recomputed(q, *around[q])
+            group, saved = lax.optimization_barrier((group, saved))
+        features, back = saved[p]
         if p + 1 < planes:
             other = lax.ppermute(grad, "tp", swap)
         partial = pl.pallas_call(
@@ -505,7 +500,7 @@
                 shape((PAD, owned), BF),
             ),
             parts,
-            f0,
+            features,
         )
         near = from_next(send, 1)
         far = from_next(early, 2)
@@ -513,18 +508,18 @@
             send, late[0] = lax.optimization_barrier((send, late[0]))
             sums = filter_sums(p + 1, late, sums)
             near, sums = lax.optimization_barrier((near, sums))
-        results = (shape((KL, owned), BF), shape((KL, owned), F32))
-        operands = (send, dgate, near, far, f1, f2, mixed, back, packed, grad)
-        new_grad, dkv = call(
+        results = (shape((KL, owned), BF), shape((3 * KL, owned), F32))
+        operands = (send, dgate, near, far, features, back, packed, grad)
+        new_grad, trail = call(
             functools.partial(finish_body, groups),
             results,
             *operands,
             grid=(1,),
             in_specs=[aux_block(p) if x is packed else whole(x) for x in operands],
             out_specs=tuple(whole(r) for r in results),
-            scratch_shapes=[pltpu.VMEM((KL + EDGE, owned), F32)] * 3,
+            scratch_shapes=[pltpu.VMEM((REACH, owned), F32)] * 3,
         )
-        late = [dgate, mixed, dkv, f1, f2, send, turned]
+        late = [trail, send, back]
         outs[p] = new_grad
         grad = new_grad
 

time: 509 us -> 494 us (0.971)
  local copies, waits for them, and re-layouts: 75.4 us -> 33.8 us
  blocking collectives: 207 us -> 244 us
  waiting for transfers between devices: 88.2 us -> 69.3 us
  starting transfers between devices: 73 us -> 80.5 us
    all_to_all x5 -> x7, blocking collectives: 100 us -> 143 us  [per_device(): parts = lax.all_to_all(partial, 'pipe', 0, 0, tiled=True)]
    unnamed x296 -> x146, local copies, waits for them, and re-layouts: 71.3 us -> 29.7 us
    all_to_all x3 -> x1, waiting for transfers between devices: 36.6 us -> 11 us  [per_device(): parts = lax.all_to_all(partial, 'pipe', 0, 0, tiled=True)]
    ppermute x17 -> x18, waiting for transfers between devices: 18.7 us -> 34.7 us  [from_next(): return lax.ppermute(x, 'seq', [(i, i - by) for i in range(by, size)])]
    ppermute x2 -> x4, waiting for transfers between devices: 23.5 us -> 14.5 us  [from_before(): return lax.ppermute(x, 'seq', [(i, i + by) for i in range(size - by)])]
    ppermute x2 -> x4, starting transfers between devices: 7.94 us -> 16.1 us  [from_before(): return lax.ppermute(x, 'seq', [(i, i + by) for i in range(size - by)])]
    all_to_all x3 -> x1, starting transfers between devices: 10.7 us -> 4.14 us  [per_device(): parts = lax.all_to_all(partial, 'pipe', 0, 0, tiled=True)]
    ppermute x17 -> x18, starting transfers between devices: 45.6 us -> 52 us  [from_next(): return lax.ppermute(x, 'seq', [(i, i - by) for i in range(by, size)])]
  transfers between devices with their start and end apart: 35 -> 36, of which waited for: 18 -> 23; matrix products, arithmetic and copies ran while one was open for 1% -> 1% of each run, Pallas kernels for 7% -> 7%
where the time goes in v1:
time: 494 us; the launch traced here: 487 us
  blocking collectives  244 us (49%)
  starting transfers between devices  80.5 us (16%)
  waiting for transfers between devices  69.3 us (14%)
  Pallas kernels  44.2 us (9%)
  local copies, waits for them, and re-layouts  33.8 us (7%)
  between operations  15.3 us (3%)
    all_to_all x7, blocking collectives, per_device(): parts = lax.all_to_all(partial, 'pipe', 0, 0, tiled=True)  143 us
    all_to_all x1, blocking collectives, per_device(): packed = lax.all_to_all(packed, 'pipe', 0, 0, tiled=True)  52.7 us
    ppermute x18, starting transfers between devices, from_next(): return lax.ppermute(x, 'seq', [(i, i - by) for i in range(by, size)])  52 us
    ppermute x18, waiting for transfers between devices, from_next(): return lax.ppermute(x, 'seq', [(i, i - by) for i in range(by, size)])  34.7 us
    pallas_call x36, Pallas kernels, call(): pl.pallas_call(body, out_shape=out_shape, compiler_params=pltpu.CompilerP...  34.6 us
    unnamed x146, local copies, waits for them, and re-layouts  29.7 us
    all_to_all x1, blocking collectives, per_device(): results = lax.all_to_all(merged, 'pipe', 0, 0, tiled=True)  20.6 us
    ppermute x4, starting transfers between devices, from_before(): return lax.ppermute(x, 'seq', [(i, i + by) for i in range(size - by)])  16.1 us
  transfers between devices with their start and end apart: 36, of which 23 were waited for; matrix products, arithmetic and copies ran while one was open for 1% of the time, Pallas kernels for 7%

profile of v1, /device:TPU:2, one launch (start us, length us, event | category | flops | bytes accessed | tf_op | source)
XLA Modules:
  0.0 486.8 jit_solution(17918231354827008141)
XLA Ops:
  13.7 52.7 %all_to_all.65.own_ref.aux_ref = bf16[8,432,256]{2,1,0:T(8,128)(2,1)S(1)} all-to-all(bf16[8,432,256]{2,1,0:T(8,128)(2,1)S(1)} %shard_map.76), channel_id=1, replica_groups=mesh['pipe'=8,'seq'=16,'tp'=2] {'pipe'}, dimensions={0} | all-to-all | bytes 3538944 | tf_op jit(solution)/shard_map/all_to_all | solution.py:356
  68.0 7.6 %all-to-all-start.1 = ((bf16[16,256,256]{2,1,0:T(8,128)(2,1)}), bf16[16,256,256]{2,1,0:T(8,128)(2,1)}, u32[]{:S(2)}, u32[]{:S(2)}) async-start(bf16[16,256,256]{2,1,0:T(8,128)(2,1)} %broadcast_in_dim.17), calls=%async_computation.1 | async-start | bytes 4194304 | tf_op jit(solution)/shard_map/all_to_all | solution.py:410
  76.4 3.4 collective-permute-start.1
  79.8 4.6 collective-permute-start.2
  84.4 4.3 collective-permute-start.3
  88.7 13.3 %collective-permute-done.2.prev2_ref = bf16[1,16,256]{2,1,0:T(8,128)(2,1)S(1)} collective-permute-done((bf16[1,16,256]{2,1,0:T(8,128)(2,1)S(1)}, bf16[1,16,256]{2,1,0:T(8,128)(2,1)S(1)}, u32[]{:S(2)}, u32[]{:S(2)}) %collective-permute-start.2) | collective-permute-done | bytes 8224 | tf_op jit(solution)/shard_map/ppermute | solution.py:323
  110.1 4.1 all-to-all-start.2
  117.9 11.0 %all-to-all-done.2.parts_ref = bf16[8,128,256]{2,1,0:T(8,128)(2,1)} async-done(((bf16[8,128,256]{2,1,0:T(8,128)(2,1)}), bf16[8,128,256]{2,1,0:T(8,128)(2,1)}, u32[]{:S(2)}, u32[]{:S(2)}) %all-to-all-start.2) | async-done | bytes 524320 | tf_op jit(solution)/shard_map/all_to_all | solution.py:494
  135.5 4.9 %collective-permute-done.6.far_ref = bf16[16,256]{1,0:T(8,128)(2,1)S(1)} collective-permute-done((bf16[16,256]{1,0:T(8,128)(2,1)S(1)}, bf16[16,256]{1,0:T(8,128)(2,1)S(1)}, u32[]{:S(2)}, u32[]{:S(2)}) %collective-permute-start.6) | collective-permute-done | bytes 8224 | tf_op jit(solution)/shard_map/ppermute | solution.py:318
  143.1 5.3 %collective-permute-start.9 = (bf16[7,16,256]{2,1,0:T(8,128)(2,1)S(1)}, bf16[7,16,256]{2,1,0:T(8,128)(2,1)S(1)}, u32[]{:S(2)}, u32[]{:S(2)}) collective-permute-start(bf16[7,16,256]{2,1,0:T(8,128)(2,1)S(1)} %get-tuple-element.228), channel_id=1, source_target_pairs={{0,4},{2,6},{4,8},{6,10},{8,12},{10,14},{12,16},{14,18},{16,20},{1... | collective-permute-start | bytes 172040 | tf_op jit(solution)/shard_map/ppermute | solution.py:323
  148.3 4.0 collective-permute-start.10
  178.9 20.1 %all_to_all.66.parts_ref = bf16[8,128,256]{2,1,0:T(8,128)(2,1)S(1)} all-to-all(bf16[8,128,256]{2,1,0:T(8,128)(2,1)S(1)} %shard_map.89), channel_id=1, replica_groups=mesh['pipe'=8,'seq'=16,'tp'=2] {'pipe'}, dimensions={0} | all-to-all | bytes 1048576 | tf_op jit(solution)/shard_map/all_to_all | solution.py:494
  199.1 4.8 collective-permute-start.11
  207.3 3.9 collective-permute-done.12.far_ref
  214.1 20.5 %all_to_all.67.parts_ref = bf16[8,128,256]{2,1,0:T(8,128)(2,1)S(1)} all-to-all(bf16[8,128,256]{2,1,0:T(8,128)(2,1)S(1)} %shard_map.93), channel_id=1, replica_groups=mesh['pipe'=8,'seq'=16,'tp'=2] {'pipe'}, dimensions={0} | all-to-all | bytes 1048576 | tf_op jit(solution)/shard_map/all_to_all | solution.py:494
  241.0 3.6 collective-permute-done.15.far_ref
  248.0 3.0 copy-done
  253.6 20.8 %all_to_all.68.parts_ref = bf16[8,128,256]{2,1,0:T(8,128)(2,1)S(1)} all-to-all(bf16[8,128,256]{2,1,0:T(8,128)(2,1)S(1)} %shard_map.97), channel_id=1, replica_groups=mesh['pipe'=8,'seq'=16,'tp'=2] {'pipe'}, dimensions={0} | all-to-all | bytes 1048576 | tf_op jit(solution)/shard_map/all_to_all | solution.py:494
  274.4 3.8 collective-permute-start.17
  288.4 20.5 %all_to_all.69.parts_ref = bf16[8,128,256]{2,1,0:T(8,128)(2,1)S(1)} all-to-all(bf16[8,128,256]{2,1,0:T(8,128)(2,1)S(1)} %shard_map.101), channel_id=1, replica_groups=mesh['pipe'=8,'seq'=16,'tp'=2] {'pipe'}, dimensions={0} | all-to-all | bytes 1048576 | tf_op jit(solution)/shard_map/all_to_all | solution.py:494
  315.5 3.5 collective-permute-done.21.far_ref
  322.0 20.5 %all_to_all.70.parts_ref = bf16[8,128,256]{2,1,0:T(8,128)(2,1)S(1)} all-to-all(bf16[8,128,256]{2,1,0:T(8,128)(2,1)S(1)} %shard_map.105), channel_id=1, replica_groups=mesh['pipe'=8,'seq'=16,'tp'=2] {'pipe'}, dimensions={0} | all-to-all | bytes 1048576 | tf_op jit(solution)/shard_map/all_to_all | solution.py:494
  342.6 3.9 collective-permute-start.23
  349.8 4.0 collective-permute-done.24.far_ref
  361.4 20.6 %all_to_all.71.parts_ref = bf16[8,128,256]{2,1,0:T(8,128)(2,1)S(1)} all-to-all(bf16[8,128,256]{2,1,0:T(8,128)(2,1)S(1)} %shard_map.109), channel_id=1, replica_groups=mesh['pipe'=8,'seq'=16,'tp'=2] {'pipe'}, dimensions={0} | all-to-all | bytes 1048576 | tf_op jit(solution)/shard_map/all_to_all | solution.py:494
  388.5 3.6 collective-permute-done.27.far_ref
  396.0 20.5 %all_to_all.72.parts_ref = bf16[8,128,256]{2,1,0:T(8,128)(2,1)S(1)} all-to-all(bf16[8,128,256]{2,1,0:T(8,128)(2,1)S(1)} %shard_map.113), channel_id=1, replica_groups=mesh['pipe'=8,'seq'=16,'tp'=2] {'pipe'}, dimensions={0} | all-to-all | bytes 1048576 | tf_op jit(solution)/shard_map/all_to_all | solution.py:494
  416.6 3.4 collective-permute-start.29
  423.0 4.0 collective-permute-done.30.far_ref
  429.0 15.2 %all_to_all.73.in_ref = bf16[16,48,128]{2,1,0:T(8,128)(2,1)S(1)} all-to-all(bf16[16,48,128]{2,1,0:T(8,128)(2,1)S(1)} %shard_map.117), channel_id=1, replica_groups=mesh['pipe'=8,'seq'=16,'tp'=2] {'seq'}, dimensions={0} | all-to-all | bytes 393216 | tf_op jit(solution)/shard_map/all_to_all | solution.py:527
  444.2 11.6 %all_to_all.74.sums_ref = bf16[16,48,128]{2,1,0:T(8,128)(2,1)S(1)} all-to-all(bf16[16,48,128]{2,1,0:T(8,128)(2,1)S(1)} %shard_map.118), channel_id=1, replica_groups=mesh['pipe'=8,'seq'=16,'tp'=2] {'seq'}, dimensions={0} | all-to-all | bytes 393216 | tf_op jit(solution)/shard_map/all_to_all | solution.py:531
  456.8 20.6 %all_to_all.75.in_ref = bf16[8,176,256]{2,1,0:T(8,128)(2,1)S(1)} all-to-all(bf16[8,176,256]{2,1,0:T(8,128)(2,1)S(1)} %shard_map.119), channel_id=1, replica_groups=mesh['pipe'=8,'seq'=16,'tp'=2] {'pipe'}, dimensions={0} | all-to-all | bytes 1441792 | tf_op jit(solution)/shard_map/all_to_all | solution.py:533
  (256 shorter events, 124.0 us)
Async XLA Ops:
  7.2 2.2 collective-permute-start
  68.0 36.8 %all-to-all-start.1 = ((bf16[16,256,256]{2,1,0:T(8,128)(2,1)}), bf16[16,256,256]{2,1,0:T(8,128)(2,1)}, u32[]{:S(2)}, u32[]{:S(2)}) async-start(bf16[16,256,256]{2,1,0:T(8,128)(2,1)} %broadcast_in_dim.17), calls=%async_computation.1 | async-start | bytes 4194304 | tf_op jit(solution)/shard_map/all_to_all | solution.py:410
  75.6 100.2 %all-gather.7.cloned.1.call-start = ((), (), s32[]{:S(2)}) async-start(), calls=%async_computation.13 | async-start | bytes 4456448 | tf_op jit(solution)/shard_map/all_gather | solution.py:405
  76.3 28.5 %collective-permute-start.4 = (bf16[128,256]{1,0:T(8,128)(2,1)S(1)}, bf16[128,256]{1,0:T(8,128)(2,1)S(1)}, u32[]{:S(2)}, u32[]{:S(2)}) collective-permute-start(bf16[128,256]{1,0:T(8,128)(2,1)S(1)} %dynamic-slice_bitcast_fusion.own_ref.grad_ref), channel_id=1, source_target_pairs={{0,1},{1,0},{2,3},{3,2},{4,5},{5,4},{6,7},{7,6},{8,9},{9,8},{10,11... | collective-permute-start | bytes 196616 | tf_op jit(solution)/shard_map/ppermute | solution.py:420
  76.4 26.0 %collective-permute-start.1 = (bf16[1,128,256]{2,1,0:T(8,128)(2,1)S(1)}, bf16[1,128,256]{2,1,0:T(8,128)(2,1)S(1)}, u32[]{:S(2)}, u32[]{:S(2)}) collective-permute-start(bf16[1,128,256]{2,1,0:T(8,128)(2,1)S(1)} %slice.49), channel_id=1, source_target_pairs={{0,2},{2,4},{4,6},{6,8},{8,10},{10,12},{12,14},{14,16},{16,18},{18... | collective-permute-start | bytes 196616 | tf_op jit(solution)/shard_map/ppermute | solution.py:323
  79.8 22.2 %collective-permute-start.2 = (bf16[1,16,256]{2,1,0:T(8,128)(2,1)S(1)}, bf16[1,16,256]{2,1,0:T(8,128)(2,1)S(1)}, u32[]{:S(2)}, u32[]{:S(2)}) collective-permute-start(bf16[1,16,256]{2,1,0:T(8,128)(2,1)S(1)} %get-tuple-element.230), channel_id=1, source_target_pairs={{0,4},{2,6},{4,8},{6,10},{8,12},{10,14},{12,16},{14,18},{16,20},{1... | collective-permute-start | bytes 24584 | tf_op jit(solution)/shard_map/ppermute | solution.py:323
  84.4 17.6 %collective-permute-start.3 = (bf16[1,16,256]{2,1,0:T(8,128)(2,1)S(1)}, bf16[1,16,256]{2,1,0:T(8,128)(2,1)S(1)}, u32[]{:S(2)}, u32[]{:S(2)}) collective-permute-start(bf16[1,16,256]{2,1,0:T(8,128)(2,1)S(1)} %get-tuple-element.229), channel_id=1, source_target_pairs={{2,0},{4,2},{6,4},{8,6},{10,8},{12,10},{14,12},{16,14},{18,16},{20... | collective-permute-start | bytes 24584 | tf_op jit(solution)/shard_map/ppermute | solution.py:318
  105.8 142.3 %all-gather.9.cloned.1.call-start = ((), (), s32[]{:S(2)}) async-start(), calls=%async_computation.14 | async-start | bytes 6684672 | tf_op jit(solution)/shard_map/all_gather | solution.py:405
  106.7 249.4 %all-gather.11.cloned.1.call-start = ((), (), s32[]{:S(2)}) async-start(), calls=%async_computation.15 | async-start | bytes 4456448 | tf_op jit(solution)/shard_map/all_gather | solution.py:405
  110.1 18.8 %all-to-all-start.2 = ((bf16[8,128,256]{2,1,0:T(8,128)(2,1)}), bf16[8,128,256]{2,1,0:T(8,128)(2,1)}, u32[]{:S(2)}, u32[]{:S(2)}) async-start(bf16[8,128,256]{2,1,0:T(8,128)(2,1)} %copy-done.36), calls=%async_computation.2 | async-start | bytes 1048576 | tf_op jit(solution)/shard_map/all_to_all | solution.py:494
  115.1 40.9 %collective-permute-start.8 = (bf16[7,128,256]{2,1,0:T(8,128)(2,1)}, bf16[7,128,256]{2,1,0:T(8,128)(2,1)S(1)}, u32[]{:S(2)}, u32[]{:S(2)}) collective-permute-start(bf16[7,128,256]{2,1,0:T(8,128)(2,1)} %slice.42), channel_id=1, source_target_pairs={{0,2},{2,4},{4,6},{6,8},{8,10},{10,12},{12,14},{14,16},{16,18},{18... | collective-permute-start | bytes 1376264 | tf_op jit(solution)/shard_map/ppermute | solution.py:323
  131.1 9.3 %collective-permute-start.5 = (bf16[144,256]{1,0:T(8,128)(2,1)S(1)}, bf16[144,256]{1,0:T(8,128)(2,1)S(1)}, u32[]{:S(2)}, u32[]{:S(2)}) collective-permute-start(bf16[144,256]{1,0:T(8,128)(2,1)S(1)} %get-tuple-element.117.send_ref), channel_id=1, source_target_pairs={{2,0},{4,2},{6,4},{8,6},{10,8},{12,10},{14,12},{16,14},{18,16},{20... | collective-permute-start | bytes 221192 | tf_op jit(solution)/shard_map/ppermute | solution.py:318
  133.3 7.0 %collective-permute-start.6 = (bf16[16,256]{1,0:T(8,128)(2,1)S(1)}, bf16[16,256]{1,0:T(8,128)(2,1)S(1)}, u32[]{:S(2)}, u32[]{:S(2)}) collective-permute-start(bf16[16,256]{1,0:T(8,128)(2,1)S(1)} %get-tuple-element.119), channel_id=1, source_target_pairs={{4,0},{6,2},{8,4},{10,6},{12,8},{14,10},{16,12},{18,14},{20,16},{2... | collective-permute-start | bytes 24584 | tf_op jit(solution)/shard_map/ppermute | solution.py:318
  143.0 32.8 %collective-permute-start.7 = (bf16[128,256]{1,0:T(8,128)(2,1)S(1)}, bf16[128,256]{1,0:T(8,128)(2,1)S(1)}, u32[]{:S(2)}, u32[]{:S(2)}) collective-permute-start(bf16[128,256]{1,0:T(8,128)(2,1)S(1)} %get-tuple-element.121.own_ref.grad_ref.refs_7_), channel_id=1, source_target_pairs={{0,1},{1,0},{2,3},{3,2},{4,5},{5,4},{6,7},{7,6},{8,9},{9,8},{10,11... | collective-permute-start | bytes 196616 | tf_op jit(solution)/shard_map/ppermute | solution.py:475
  143.1 10.1 %collective-permute-start.9 = (bf16[7,16,256]{2,1,0:T(8,128)(2,1)S(1)}, bf16[7,16,256]{2,1,0:T(8,128)(2,1)S(1)}, u32[]{:S(2)}, u32[]{:S(2)}) collective-permute-start(bf16[7,16,256]{2,1,0:T(8,128)(2,1)S(1)} %get-tuple-element.228), channel_id=1, source_target_pairs={{0,4},{2,6},{4,8},{6,10},{8,12},{10,14},{12,16},{14,18},{16,20},{1... | collective-permute-start | bytes 172040 | tf_op jit(solution)/shard_map/ppermute | solution.py:323
  148.3 7.7 %collective-permute-start.10 = (bf16[7,16,256]{2,1,0:T(8,128)(2,1)S(1)}, bf16[7,16,256]{2,1,0:T(8,128)(2,1)S(1)}, u32[]{:S(2)}, u32[]{:S(2)}) collective-permute-start(bf16[7,16,256]{2,1,0:T(8,128)(2,1)S(1)} %get-tuple-element.227), channel_id=1, source_target_pairs={{2,0},{4,2},{6,4},{8,6},{10,8},{12,10},{14,12},{16,14},{18,16},{20... | collective-permute-start | bytes 172040 | tf_op jit(solution)/shard_map/ppermute | solution.py:318
  199.1 8.2 %collective-permute-start.11 = (bf16[144,256]{1,0:T(8,128)(2,1)S(1)}, bf16[144,256]{1,0:T(8,128)(2,1)S(1)}, u32[]{:S(2)}, u32[]{:S(2)}) collective-permute-start(bf16[144,256]{1,0:T(8,128)(2,1)S(1)} %get-tuple-element.141.send_ref), channel_id=1, source_target_pairs={{2,0},{4,2},{6,4},{8,6},{10,8},{12,10},{14,12},{16,14},{18,16},{20... | collective-permute-start | bytes 221192 | tf_op jit(solution)/shard_map/ppermute | solution.py:318
  203.9 7.2 %collective-permute-start.12 = (bf16[16,256]{1,0:T(8,128)(2,1)S(1)}, bf16[16,256]{1,0:T(8,128)(2,1)S(1)}, u32[]{:S(2)}, u32[]{:S(2)}) collective-permute-start(bf16[16,256]{1,0:T(8,128)(2,1)S(1)} %get-tuple-element.145), channel_id=1, source_target_pairs={{4,0},{6,2},{8,4},{10,6},{12,8},{14,10},{16,12},{18,14},{20,16},{2... | collective-permute-start | bytes 24584 | tf_op jit(solution)/shard_map/ppermute | solution.py:318
  212.0 1.3 collective-permute-start.13
  234.7 6.2 %collective-permute-start.14 = (bf16[144,256]{1,0:T(8,128)(2,1)S(1)}, bf16[144,256]{1,0:T(8,128)(2,1)S(1)}, u32[]{:S(2)}, u32[]{:S(2)}) collective-permute-start(bf16[144,256]{1,0:T(8,128)(2,1)S(1)} %get-tuple-element.151.send_ref), channel_id=1, source_target_pairs={{2,0},{4,2},{6,4},{8,6},{10,8},{12,10},{14,12},{16,14},{18,16},{20... | collective-permute-start | bytes 221192 | tf_op jit(solution)/shard_map/ppermute | solution.py:318
  237.5 7.0 %collective-permute-start.15 = (bf16[16,256]{1,0:T(8,128)(2,1)S(1)}, bf16[16,256]{1,0:T(8,128)(2,1)S(1)}, u32[]{:S(2)}, u32[]{:S(2)}) collective-permute-start(bf16[16,256]{1,0:T(8,128)(2,1)S(1)} %get-tuple-element.156), channel_id=1, source_target_pairs={{4,0},{6,2},{8,4},{10,6},{12,8},{14,10},{16,12},{18,14},{20,16},{2... | collective-permute-start | bytes 24584 | tf_op jit(solution)/shard_map/ppermute | solution.py:318
  274.4 8.4 %collective-permute-start.17 = (bf16[144,256]{1,0:T(8,128)(2,1)S(1)}, bf16[144,256]{1,0:T(8,128)(2,1)S(1)}, u32[]{:S(2)}, u32[]{:S(2)}) collective-permute-start(bf16[144,256]{1,0:T(8,128)(2,1)S(1)} %get-tuple-element.162.send_ref), channel_id=1, source_target_pairs={{2,0},{4,2},{6,4},{8,6},{10,8},{12,10},{14,12},{16,14},{18,16},{20... | collective-permute-start | bytes 221192 | tf_op jit(solution)/shard_map/ppermute | solution.py:318
  278.2 7.2 %collective-permute-start.18 = (bf16[16,256]{1,0:T(8,128)(2,1)S(1)}, bf16[16,256]{1,0:T(8,128)(2,1)S(1)}, u32[]{:S(2)}, u32[]{:S(2)}) collective-permute-start(bf16[16,256]{1,0:T(8,128)(2,1)S(1)} %get-tuple-element.167), channel_id=1, source_target_pairs={{4,0},{6,2},{8,4},{10,6},{12,8},{14,10},{16,12},{18,14},{20,16},{2... | collective-permute-start | bytes 24584 | tf_op jit(solution)/shard_map/ppermute | solution.py:318
  309.0 6.5 %collective-permute-start.20 = (bf16[144,256]{1,0:T(8,128)(2,1)S(1)}, bf16[144,256]{1,0:T(8,128)(2,1)S(1)}, u32[]{:S(2)}, u32[]{:S(2)}) collective-permute-start(bf16[144,256]{1,0:T(8,128)(2,1)S(1)} %get-tuple-element.173.send_ref), channel_id=1, source_target_pairs={{2,0},{4,2},{6,4},{8,6},{10,8},{12,10},{14,12},{16,14},{18,16},{20... | collective-permute-start | bytes 221192 | tf_op jit(solution)/shard_map/ppermute | solution.py:318
  311.9 7.0 %collective-permute-start.21 = (bf16[16,256]{1,0:T(8,128)(2,1)S(1)}, bf16[16,256]{1,0:T(8,128)(2,1)S(1)}, u32[]{:S(2)}, u32[]{:S(2)}) collective-permute-start(bf16[16,256]{1,0:T(8,128)(2,1)S(1)} %get-tuple-element.178), channel_id=1, source_target_pairs={{4,0},{6,2},{8,4},{10,6},{12,8},{14,10},{16,12},{18,14},{20,16},{2... | collective-permute-start | bytes 24584 | tf_op jit(solution)/shard_map/ppermute | solution.py:318
  342.6 7.2 %collective-permute-start.23 = (bf16[144,256]{1,0:T(8,128)(2,1)S(1)}, bf16[144,256]{1,0:T(8,128)(2,1)S(1)}, u32[]{:S(2)}, u32[]{:S(2)}) collective-permute-start(bf16[144,256]{1,0:T(8,128)(2,1)S(1)} %get-tuple-element.184.send_ref), channel_id=1, source_target_pairs={{2,0},{4,2},{6,4},{8,6},{10,8},{12,10},{14,12},{16,14},{18,16},{20... | collective-permute-start | bytes 221192 | tf_op jit(solution)/shard_map/ppermute | solution.py:318
  346.5 7.3 %collective-permute-start.24 = (bf16[16,256]{1,0:T(8,128)(2,1)S(1)}, bf16[16,256]{1,0:T(8,128)(2,1)S(1)}, u32[]{:S(2)}, u32[]{:S(2)}) collective-permute-start(bf16[16,256]{1,0:T(8,128)(2,1)S(1)} %get-tuple-element.189), channel_id=1, source_target_pairs={{4,0},{6,2},{8,4},{10,6},{12,8},{14,10},{16,12},{18,14},{20,16},{2... | collective-permute-start | bytes 24584 | tf_op jit(solution)/shard_map/ppermute | solution.py:318
  356.0 1.6 collective-permute-start.25
  382.2 6.4 %collective-permute-start.26 = (bf16[144,256]{1,0:T(8,128)(2,1)S(1)}, bf16[144,256]{1,0:T(8,128)(2,1)S(1)}, u32[]{:S(2)}, u32[]{:S(2)}) collective-permute-start(bf16[144,256]{1,0:T(8,128)(2,1)S(1)} %get-tuple-element.195.send_ref), channel_id=1, source_target_pairs={{2,0},{4,2},{6,4},{8,6},{10,8},{12,10},{14,12},{16,14},{18,16},{20... | collective-permute-start | bytes 221192 | tf_op jit(solution)/shard_map/ppermute | solution.py:318
  385.1 7.0 %collective-permute-start.27 = (bf16[16,256]{1,0:T(8,128)(2,1)S(1)}, bf16[16,256]{1,0:T(8,128)(2,1)S(1)}, u32[]{:S(2)}, u32[]{:S(2)}) collective-permute-start(bf16[16,256]{1,0:T(8,128)(2,1)S(1)} %get-tuple-element.200), channel_id=1, source_target_pairs={{4,0},{6,2},{8,4},{10,6},{12,8},{14,10},{16,12},{18,14},{20,16},{2... | collective-permute-start | bytes 24584 | tf_op jit(solution)/shard_map/ppermute | solution.py:318
  416.6 6.4 %collective-permute-start.29 = (bf16[144,256]{1,0:T(8,128)(2,1)S(1)}, bf16[144,256]{1,0:T(8,128)(2,1)S(1)}, u32[]{:S(2)}, u32[]{:S(2)}) collective-permute-start(bf16[144,256]{1,0:T(8,128)(2,1)S(1)} %get-tuple-element.206.send_ref), channel_id=1, source_target_pairs={{2,0},{4,2},{6,4},{8,6},{10,8},{12,10},{14,12},{16,14},{18,16},{20... | collective-permute-start | bytes 221192 | tf_op jit(solution)/shard_map/ppermute | solution.py:318
  420.0 7.0 %collective-permute-start.30 = (bf16[16,256]{1,0:T(8,128)(2,1)S(1)}, bf16[16,256]{1,0:T(8,128)(2,1)S(1)}, u32[]{:S(2)}, u32[]{:S(2)}) collective-permute-start(bf16[16,256]{1,0:T(8,128)(2,1)S(1)} %get-tuple-element.211), channel_id=1, source_target_pairs={{4,0},{6,2},{8,4},{10,6},{12,8},{14,10},{16,12},{18,14},{20,16},{2... | collective-permute-start | bytes 24584 | tf_op jit(solution)/shard_map/ppermute | solution.py:318
  (76 other events, 891.2 us)
Sparse Core Ops, SparseCore 0:
  105.9 57.9 all-gather.6
  166.3 67.3 all-gather.8
  236.1 57.3 all-gather.10

commit v2 on v1

--- a/solution.py
+++ b/solution.py
@@ -356,12 +356,8 @@
     packed = lax.all_to_all(packed, "pipe", 0, 0, tiled=True)
     top = planes - 1
 
-    def surroundings(rows):
-        return (
-            from_before(rows, 1),
-            from_before(rows[:, tokens - PAD :], 2),
-            from_next(rows[:, :PAD], 1),
-        )
+    before2 = from_before(packed[:, tokens - PAD : tokens], 2)
+    after = from_next(packed[:, :PAD], 1)
 
     def whole(x):
         return pl.BlockSpec(x.shape, lambda i: (0,) * len(x.shape))
@@ -375,9 +371,8 @@
     def aux_block(p):
         return plane(packed, p, AUX, (tokens + depth) // AUX)
 
-    def recomputed(p, around, at):
+    def recomputed(p, before, at):
         results = (shape((4 * REACH, owned), F32), shape((groups * KL + WIN, owned), BF))
-        before, before2, after = around
         return call(
             functools.partial(recompute_body, groups),
             results,
@@ -390,8 +385,8 @@
             in_specs=[
                 own_block(p),
                 plane(before, at, tokens),
-                plane(before2, at, PAD),
-                plane(after, at, PAD),
+                plane(before2, p, PAD),
+                plane(after, p, PAD),
                 aux_block(p),
             ],
             out_specs=tuple(whole(r) for r in results),
@@ -419,29 +414,29 @@
     swap = [(0, 1), (1, 0)]
     other = lax.ppermute(grad, "tp", swap)
 
-    around = {top: (surroundings(packed[top:, :tokens]), 0)}
-    saved = {top: recomputed(top, *around[top])}
+    before = {top: (from_before(packed[top:, :tokens], 1), 0)}
+    saved = {top: recomputed(top, *before[top])}
     first_weights, saved[top], source, grad, other = lax.optimization_barrier(
         (copied(top), saved[top], packed, grad, other)
     )
-    others = surroundings(source[:top, :tokens])
-    around.update({p: (others, p) for p in range(top)})
+    others = from_before(source[:top, :tokens], 1)
+    before.update({p: (others, p) for p in range(top)})
     weights = {top: (first_weights, 0)}
     last = planes - 2
-    for size in (2, 3, planes):
+    for size in (1, 2, 2, planes):
         first = max(0, last - size + 1)
         if last >= first:
-            group = gathered(source, first, last)
+            group = gathered(packed, first, last)
             weights.update({p: (group, p - first) for p in range(first, last + 1)})
         last = first - 1
 
     def filter_sums(p, operands, sums):
         halves = owned // TILE
         result = shape((planes * halves, AUX, TILE), BF)
-        (before, _, _), at = around[p]
+        earlier, at = before[p]
         specs = [whole(x) for x in operands]
-        specs += [own_block(p), plane(before, at, PAD, tokens // PAD - 1)]
-        operands = [*operands, packed, before]
+        specs += [own_block(p), plane(earlier, at, PAD, tokens // PAD - 1)]
+        operands = [*operands, packed, earlier]
         aliases = {}
         if sums is not None:
             aliases = {len(operands): 0}
@@ -466,10 +461,6 @@
     late = None
     for p in range(planes - 1, -1, -1):
         group, at = weights[p]
-        if p == top - 1:
-            for q in range(top):
-                saved[q] = recomputed(q, *around[q])
-            group, saved = lax.optimization_barrier((group, saved))
         features, back = saved[p]
         if p + 1 < planes:
             other = lax.ppermute(grad, "tp", swap)
@@ -508,6 +499,11 @@
             send, late[0] = lax.optimization_barrier((send, late[0]))
             sums = filter_sums(p + 1, late, sums)
             near, sums = lax.optimization_barrier((near, sums))
+        if p > 0:
+            earlier, at = before[p - 1]
+            send, earlier = lax.optimization_barrier((send, earlier))
+            saved[p - 1] = recomputed(p - 1, earlier, at)
+            near, saved[p - 1] = lax.optimization_barrier((near, saved[p - 1]))
         results = (shape((KL, owned), BF), shape((3 * KL, owned), F32))
         operands = (send, dgate, near, far, features, back, packed, grad)
         new_grad, trail = call(

time: 494 us -> 472 us (0.955)
  waiting for transfers between devices: 69.3 us -> 60.1 us
  local copies, waits for them, and re-layouts: 33.8 us -> 25.5 us
  starting transfers between devices: 80.5 us -> 75.4 us
    ppermute x18 -> x17, waiting for transfers between devices: 34.7 us -> 15.5 us  [from_next(): return lax.ppermute(x, 'seq', [(i, i - by) for i in range(by, size)])]
    unnamed x146 -> x100, local copies, waits for them, and re-layouts: 29.7 us -> 21.5 us
    all_gather x3 -> x4, waiting for transfers between devices: 0.01 us -> 6.04 us  [gathered(): lax.all_gather(source[first:last + 1, tokens:tokens + depth], 'seq', axis=0)]
    ppermute x4 -> x3, starting transfers between devices: 16.1 us -> 10.5 us  [from_before(): return lax.ppermute(x, 'seq', [(i, i + by) for i in range(size - by)])]
    ppermute x4 -> x3, waiting for transfers between devices: 14.5 us -> 17 us  [from_before(): return lax.ppermute(x, 'seq', [(i, i + by) for i in range(size - by)])]
    ppermute x18 -> x17, starting transfers between devices: 52 us -> 52.4 us  [from_next(): return lax.ppermute(x, 'seq', [(i, i - by) for i in range(by, size)])]
  transfers between devices with their start and end apart: 36 -> 35, of which waited for: 23 -> 21; matrix products, arithmetic and copies ran while one was open for 1% -> 1% of each run, Pallas kernels for 7% -> 7%
where the time goes in v2:
time: 472 us; the launch traced here: 464 us
  blocking collectives  245 us (52%)
  starting transfers between devices  75.4 us (16%)
  waiting for transfers between devices  60.1 us (13%)
  Pallas kernels  42.4 us (9%)
  local copies, waits for them, and re-layouts  25.5 us (5%)
  between operations  15.2 us (3%)
    all_to_all x7, blocking collectives, per_device(): parts = lax.all_to_all(partial, 'pipe', 0, 0, tiled=True)  147 us
    all_to_all x1, blocking collectives, per_device(): packed = lax.all_to_all(packed, 'pipe', 0, 0, tiled=True)  52.7 us
    ppermute x17, starting transfers between devices, from_next(): return lax.ppermute(x, 'seq', [(i, i - by) for i in range(by, size)])  52.4 us
    pallas_call x36, Pallas kernels, call(): pl.pallas_call(body, out_shape=out_shape, compiler_params=pltpu.CompilerP...  32.4 us
    unnamed x100, local copies, waits for them, and re-layouts  21.5 us
    all_to_all x1, blocking collectives, per_device(): results = lax.all_to_all(merged, 'pipe', 0, 0, tiled=True)  20.6 us
    ppermute x3, waiting for transfers between devices, from_before(): return lax.ppermute(x, 'seq', [(i, i + by) for i in range(size - by)])  17 us
    ppermute x17, waiting for transfers between devices, from_next(): return lax.ppermute(x, 'seq', [(i, i - by) for i in range(by, size)])  15.5 us
  transfers between devices with their start and end apart: 35, of which 21 were waited for; matrix products, arithmetic and copies ran while one was open for 1% of the time, Pallas kernels for 7%

profile of v2, /device:TPU:2, one launch (start us, length us, event | category | flops | bytes accessed | tf_op | source)
XLA Modules:
  0.0 463.6 jit_solution(6294950737008279955)
XLA Ops:
  13.8 52.7 %all_to_all.65.own_ref.aux_ref = bf16[8,432,256]{2,1,0:T(8,128)(2,1)S(1)} all-to-all(bf16[8,432,256]{2,1,0:T(8,128)(2,1)S(1)} %shard_map.76), channel_id=1, replica_groups=mesh['pipe'=8,'seq'=16,'tp'=2] {'pipe'}, dimensions={0} | all-to-all | bytes 3538944 | tf_op jit(solution)/shard_map/all_to_all | solution.py:356
  70.5 7.6 %all-to-all-start.1 = ((bf16[16,256,256]{2,1,0:T(8,128)(2,1)}), bf16[16,256,256]{2,1,0:T(8,128)(2,1)}, u32[]{:S(2)}, u32[]{:S(2)}) async-start(bf16[16,256,256]{2,1,0:T(8,128)(2,1)} %broadcast_in_dim.17), calls=%async_computation.1 | async-start | bytes 4194304 | tf_op jit(solution)/shard_map/all_to_all | solution.py:405
  79.3 3.4 collective-permute-start.1
  82.7 4.6 collective-permute-start.2
  87.3 4.3 collective-permute-start.3
  91.7 16.8 %collective-permute-done.1.prev_ref = bf16[1,128,256]{2,1,0:T(8,128)(2,1)S(1)} collective-permute-done((bf16[1,128,256]{2,1,0:T(8,128)(2,1)S(1)}, bf16[1,128,256]{2,1,0:T(8,128)(2,1)S(1)}, u32[]{:S(2)}, u32[]{:S(2)}) %collective-permute-start.1) | collective-permute-done | bytes 65568 | tf_op jit(solution)/shard_map/ppermute | solution.py:323
  114.3 4.1 all-to-all-start.2
  121.8 10.9 %all-to-all-done.2.parts_ref = bf16[8,128,256]{2,1,0:T(8,128)(2,1)} async-done(((bf16[8,128,256]{2,1,0:T(8,128)(2,1)}), bf16[8,128,256]{2,1,0:T(8,128)(2,1)}, u32[]{:S(2)}, u32[]{:S(2)}) %all-to-all-start.2) | async-done | bytes 524320 | tf_op jit(solution)/shard_map/all_to_all | solution.py:485
  134.9 2.9 collective-permute-start.6
  137.8 3.2 collective-permute-start.7
  151.4 20.5 %all_to_all.66.parts_ref = bf16[8,128,256]{2,1,0:T(8,128)(2,1)S(1)} all-to-all(bf16[8,128,256]{2,1,0:T(8,128)(2,1)S(1)} %shard_map.83), channel_id=1, replica_groups=mesh['pipe'=8,'seq'=16,'tp'=2] {'pipe'}, dimensions={0} | all-to-all | bytes 1048576 | tf_op jit(solution)/shard_map/all_to_all | solution.py:485
  172.0 3.7 collective-permute-start.9
  175.7 3.8 collective-permute-start.10
  185.5 6.0 %all-gather.11.cloned.1.call-done = bf16[32,256,256]{2,1,0:T(8,128)(2,1)} async-done(((bf16[2,256,256]{2,1,0:T(8,128)(2,1)}), bf16[32,256,256]{2,1,0:T(8,128)(2,1)}) %all-gather.11.cloned.1.call-update) | async-done | bytes 4194320 | tf_op jit(solution)/shard_map/all_gather | solution.py:400
  194.6 24.3 %all_to_all.67.parts_ref = bf16[8,128,256]{2,1,0:T(8,128)(2,1)S(1)} all-to-all(bf16[8,128,256]{2,1,0:T(8,128)(2,1)S(1)} %shard_map.88), channel_id=1, replica_groups=mesh['pipe'=8,'seq'=16,'tp'=2] {'pipe'}, dimensions={0} | all-to-all | bytes 1048576 | tf_op jit(solution)/shard_map/all_to_all | solution.py:485
  219.0 4.1 collective-permute-start.12
  223.1 2.7 collective-permute-start.13
  233.1 20.5 %all_to_all.68.parts_ref = bf16[8,128,256]{2,1,0:T(8,128)(2,1)S(1)} all-to-all(bf16[8,128,256]{2,1,0:T(8,128)(2,1)S(1)} %shard_map.93), channel_id=1, replica_groups=mesh['pipe'=8,'seq'=16,'tp'=2] {'pipe'}, dimensions={0} | all-to-all | bytes 1048576 | tf_op jit(solution)/shard_map/all_to_all | solution.py:485
  253.7 3.6 collective-permute-start.15
  270.2 20.5 %all_to_all.69.parts_ref = bf16[8,128,256]{2,1,0:T(8,128)(2,1)S(1)} all-to-all(bf16[8,128,256]{2,1,0:T(8,128)(2,1)S(1)} %shard_map.98), channel_id=1, replica_groups=mesh['pipe'=8,'seq'=16,'tp'=2] {'pipe'}, dimensions={0} | all-to-all | bytes 1048576 | tf_op jit(solution)/shard_map/all_to_all | solution.py:485
  290.8 3.5 collective-permute-start.18
  304.5 20.5 %all_to_all.70.parts_ref = bf16[8,128,256]{2,1,0:T(8,128)(2,1)S(1)} all-to-all(bf16[8,128,256]{2,1,0:T(8,128)(2,1)S(1)} %shard_map.103), channel_id=1, replica_groups=mesh['pipe'=8,'seq'=16,'tp'=2] {'pipe'}, dimensions={0} | all-to-all | bytes 1048576 | tf_op jit(solution)/shard_map/all_to_all | solution.py:485
  325.1 3.3 collective-permute-start.21
  328.4 2.7 collective-permute-start.22
  342.2 20.5 %all_to_all.71.parts_ref = bf16[8,128,256]{2,1,0:T(8,128)(2,1)S(1)} all-to-all(bf16[8,128,256]{2,1,0:T(8,128)(2,1)S(1)} %shard_map.108), channel_id=1, replica_groups=mesh['pipe'=8,'seq'=16,'tp'=2] {'pipe'}, dimensions={0} | all-to-all | bytes 1048576 | tf_op jit(solution)/shard_map/all_to_all | solution.py:485
  362.7 3.9 collective-permute-start.24
  376.7 20.5 %all_to_all.72.parts_ref = bf16[8,128,256]{2,1,0:T(8,128)(2,1)S(1)} all-to-all(bf16[8,128,256]{2,1,0:T(8,128)(2,1)S(1)} %shard_map.113), channel_id=1, replica_groups=mesh['pipe'=8,'seq'=16,'tp'=2] {'pipe'}, dimensions={0} | all-to-all | bytes 1048576 | tf_op jit(solution)/shard_map/all_to_all | solution.py:485
  397.3 2.8 collective-permute-start.27
  403.5 3.6 collective-permute-done.28.far_ref
  409.1 12.7 %all_to_all.73.in_ref = bf16[16,48,128]{2,1,0:T(8,128)(2,1)S(1)} all-to-all(bf16[16,48,128]{2,1,0:T(8,128)(2,1)S(1)} %shard_map.117), channel_id=1, replica_groups=mesh['pipe'=8,'seq'=16,'tp'=2] {'seq'}, dimensions={0} | all-to-all | bytes 393216 | tf_op jit(solution)/shard_map/all_to_all | solution.py:523
  421.9 11.6 %all_to_all.74.sums_ref = bf16[16,48,128]{2,1,0:T(8,128)(2,1)S(1)} all-to-all(bf16[16,48,128]{2,1,0:T(8,128)(2,1)S(1)} %shard_map.118), channel_id=1, replica_groups=mesh['pipe'=8,'seq'=16,'tp'=2] {'seq'}, dimensions={0} | all-to-all | bytes 393216 | tf_op jit(solution)/shard_map/all_to_all | solution.py:527
  433.6 20.6 %all_to_all.75.in_ref = bf16[8,176,256]{2,1,0:T(8,128)(2,1)S(1)} all-to-all(bf16[8,176,256]{2,1,0:T(8,128)(2,1)S(1)} %shard_map.119), channel_id=1, replica_groups=mesh['pipe'=8,'seq'=16,'tp'=2] {'pipe'}, dimensions={0} | all-to-all | bytes 1441792 | tf_op jit(solution)/shard_map/all_to_all | solution.py:529
  (206 shorter events, 101.8 us)
Async XLA Ops:
  7.2 141.0 %all-gather.9.cloned.1.call-start = ((), (), s32[]{:S(2)}) async-start(), calls=%async_computation.13 | async-start | bytes 2228224 | tf_op jit(solution)/shard_map/all_gather | solution.py:400
  7.2 2.2 collective-permute-start
  67.2 124.4 %all-gather.11.cloned.1.call-start = ((), (), s32[]{:S(2)}) async-start(), calls=%async_computation.14 | async-start | bytes 4456448 | tf_op jit(solution)/shard_map/all_gather | solution.py:400
  68.2 197.7 %all-gather.13.cloned.1.call-start = ((), (), s32[]{:S(2)}) async-start(), calls=%async_computation.15 | async-start | bytes 4456448 | tf_op jit(solution)/shard_map/all_gather | solution.py:400
  70.5 40.7 %all-to-all-start.1 = ((bf16[16,256,256]{2,1,0:T(8,128)(2,1)}), bf16[16,256,256]{2,1,0:T(8,128)(2,1)}, u32[]{:S(2)}, u32[]{:S(2)}) async-start(bf16[16,256,256]{2,1,0:T(8,128)(2,1)} %broadcast_in_dim.17), calls=%async_computation.1 | async-start | bytes 4194304 | tf_op jit(solution)/shard_map/all_to_all | solution.py:405
  78.1 258.9 %all-gather.15.cloned.1.call-start = ((), (), s32[]{:S(2)}) async-start(), calls=%async_computation.16 | async-start | bytes 4456448 | tf_op jit(solution)/shard_map/all_gather | solution.py:400
  79.3 29.2 %collective-permute-start.1 = (bf16[1,128,256]{2,1,0:T(8,128)(2,1)S(1)}, bf16[1,128,256]{2,1,0:T(8,128)(2,1)S(1)}, u32[]{:S(2)}, u32[]{:S(2)}) collective-permute-start(bf16[1,128,256]{2,1,0:T(8,128)(2,1)S(1)} %slice.41), channel_id=1, source_target_pairs={{0,2},{2,4},{4,6},{6,8},{8,10},{10,12},{12,14},{14,16},{16,18},{18... | collective-permute-start | bytes 196616 | tf_op jit(solution)/shard_map/ppermute | solution.py:323
  82.7 26.0 %collective-permute-start.2 = (bf16[8,16,256]{2,1,0:T(8,128)(2,1)S(1)}, bf16[8,16,256]{2,1,0:T(8,128)(2,1)S(1)}, u32[]{:S(2)}, u32[]{:S(2)}) collective-permute-start(bf16[8,16,256]{2,1,0:T(8,128)(2,1)S(1)} %get-tuple-element.271), channel_id=1, source_target_pairs={{0,4},{2,6},{4,8},{6,10},{8,12},{10,14},{12,16},{14,18},{16,20},{1... | collective-permute-start | bytes 196616 | tf_op jit(solution)/shard_map/ppermute | solution.py:323
  87.3 21.4 %collective-permute-start.3 = (bf16[8,16,256]{2,1,0:T(8,128)(2,1)S(1)}, bf16[8,16,256]{2,1,0:T(8,128)(2,1)S(1)}, u32[]{:S(2)}, u32[]{:S(2)}) collective-permute-start(bf16[8,16,256]{2,1,0:T(8,128)(2,1)S(1)} %get-tuple-element.270), channel_id=1, source_target_pairs={{2,0},{4,2},{6,4},{8,6},{10,8},{12,10},{14,12},{16,14},{18,16},{20... | collective-permute-start | bytes 196616 | tf_op jit(solution)/shard_map/ppermute | solution.py:318
  91.6 19.6 %collective-permute-start.4 = (bf16[128,256]{1,0:T(8,128)(2,1)S(1)}, bf16[128,256]{1,0:T(8,128)(2,1)S(1)}, u32[]{:S(2)}, u32[]{:S(2)}) collective-permute-start(bf16[128,256]{1,0:T(8,128)(2,1)S(1)} %dynamic-slice_bitcast_fusion.own_ref.grad_ref), channel_id=1, source_target_pairs={{0,1},{1,0},{2,3},{3,2},{4,5},{5,4},{6,7},{7,6},{8,9},{9,8},{10,11... | collective-permute-start | bytes 196616 | tf_op jit(solution)/shard_map/ppermute | solution.py:415
  114.3 18.5 %all-to-all-start.2 = ((bf16[8,128,256]{2,1,0:T(8,128)(2,1)}), bf16[8,128,256]{2,1,0:T(8,128)(2,1)}, u32[]{:S(2)}, u32[]{:S(2)}) async-start(bf16[8,128,256]{2,1,0:T(8,128)(2,1)} %copy-done.29), calls=%async_computation.2 | async-start | bytes 1048576 | tf_op jit(solution)/shard_map/all_to_all | solution.py:485
  119.3 21.8 %collective-permute-start.5 = (bf16[7,128,256]{2,1,0:T(8,128)(2,1)}, bf16[7,128,256]{2,1,0:T(8,128)(2,1)S(1)}, u32[]{:S(2)}, u32[]{:S(2)}) collective-permute-start(bf16[7,128,256]{2,1,0:T(8,128)(2,1)} %slice.34), channel_id=1, source_target_pairs={{0,2},{2,4},{4,6},{6,8},{8,10},{10,12},{12,14},{14,16},{16,18},{18... | collective-permute-start | bytes 1376264 | tf_op jit(solution)/shard_map/ppermute | solution.py:323
  134.9 8.8 %collective-permute-start.6 = (bf16[144,256]{1,0:T(8,128)(2,1)S(1)}, bf16[144,256]{1,0:T(8,128)(2,1)S(1)}, u32[]{:S(2)}, u32[]{:S(2)}) collective-permute-start(bf16[144,256]{1,0:T(8,128)(2,1)S(1)} %get-tuple-element.139.send_ref), channel_id=1, source_target_pairs={{2,0},{4,2},{6,4},{8,6},{10,8},{12,10},{14,12},{16,14},{18,16},{20... | collective-permute-start | bytes 221192 | tf_op jit(solution)/shard_map/ppermute | solution.py:318
  137.8 7.4 %collective-permute-start.7 = (bf16[16,256]{1,0:T(8,128)(2,1)S(1)}, bf16[16,256]{1,0:T(8,128)(2,1)S(1)}, u32[]{:S(2)}, u32[]{:S(2)}) collective-permute-start(bf16[16,256]{1,0:T(8,128)(2,1)S(1)} %get-tuple-element.145), channel_id=1, source_target_pairs={{4,0},{6,2},{8,4},{10,6},{12,8},{14,10},{16,12},{18,14},{20,16},{2... | collective-permute-start | bytes 24584 | tf_op jit(solution)/shard_map/ppermute | solution.py:318
  172.0 11.4 %collective-permute-start.9 = (bf16[144,256]{1,0:T(8,128)(2,1)S(1)}, bf16[144,256]{1,0:T(8,128)(2,1)S(1)}, u32[]{:S(2)}, u32[]{:S(2)}) collective-permute-start(bf16[144,256]{1,0:T(8,128)(2,1)S(1)} %get-tuple-element.152.send_ref), channel_id=1, source_target_pairs={{2,0},{4,2},{6,4},{8,6},{10,8},{12,10},{14,12},{16,14},{18,16},{20... | collective-permute-start | bytes 221192 | tf_op jit(solution)/shard_map/ppermute | solution.py:318
  175.7 7.7 %collective-permute-start.10 = (bf16[16,256]{1,0:T(8,128)(2,1)S(1)}, bf16[16,256]{1,0:T(8,128)(2,1)S(1)}, u32[]{:S(2)}, u32[]{:S(2)}) collective-permute-start(bf16[16,256]{1,0:T(8,128)(2,1)S(1)} %get-tuple-element.160), channel_id=1, source_target_pairs={{4,0},{6,2},{8,4},{10,6},{12,8},{14,10},{16,12},{18,14},{20,16},{2... | collective-permute-start | bytes 24584 | tf_op jit(solution)/shard_map/ppermute | solution.py:318
  184.2 1.3 collective-permute-start.11
  219.0 9.6 %collective-permute-start.12 = (bf16[144,256]{1,0:T(8,128)(2,1)S(1)}, bf16[144,256]{1,0:T(8,128)(2,1)S(1)}, u32[]{:S(2)}, u32[]{:S(2)}) collective-permute-start(bf16[144,256]{1,0:T(8,128)(2,1)S(1)} %get-tuple-element.167.send_ref), channel_id=1, source_target_pairs={{2,0},{4,2},{6,4},{8,6},{10,8},{12,10},{14,12},{16,14},{18,16},{20... | collective-permute-start | bytes 221192 | tf_op jit(solution)/shard_map/ppermute | solution.py:318
  223.1 7.0 %collective-permute-start.13 = (bf16[16,256]{1,0:T(8,128)(2,1)S(1)}, bf16[16,256]{1,0:T(8,128)(2,1)S(1)}, u32[]{:S(2)}, u32[]{:S(2)}) collective-permute-start(bf16[16,256]{1,0:T(8,128)(2,1)S(1)} %get-tuple-element.176), channel_id=1, source_target_pairs={{4,0},{6,2},{8,4},{10,6},{12,8},{14,10},{16,12},{18,14},{20,16},{2... | collective-permute-start | bytes 24584 | tf_op jit(solution)/shard_map/ppermute | solution.py:318
  230.9 1.3 collective-permute-start.14
  253.7 8.5 %collective-permute-start.15 = (bf16[144,256]{1,0:T(8,128)(2,1)S(1)}, bf16[144,256]{1,0:T(8,128)(2,1)S(1)}, u32[]{:S(2)}, u32[]{:S(2)}) collective-permute-start(bf16[144,256]{1,0:T(8,128)(2,1)S(1)} %get-tuple-element.183.send_ref), channel_id=1, source_target_pairs={{2,0},{4,2},{6,4},{8,6},{10,8},{12,10},{14,12},{16,14},{18,16},{20... | collective-permute-start | bytes 221192 | tf_op jit(solution)/shard_map/ppermute | solution.py:318
  257.3 7.0 %collective-permute-start.16 = (bf16[16,256]{1,0:T(8,128)(2,1)S(1)}, bf16[16,256]{1,0:T(8,128)(2,1)S(1)}, u32[]{:S(2)}, u32[]{:S(2)}) collective-permute-start(bf16[16,256]{1,0:T(8,128)(2,1)S(1)} %get-tuple-element.192), channel_id=1, source_target_pairs={{4,0},{6,2},{8,4},{10,6},{12,8},{14,10},{16,12},{18,14},{20,16},{2... | collective-permute-start | bytes 24584 | tf_op jit(solution)/shard_map/ppermute | solution.py:318
  290.8 8.4 %collective-permute-start.18 = (bf16[144,256]{1,0:T(8,128)(2,1)S(1)}, bf16[144,256]{1,0:T(8,128)(2,1)S(1)}, u32[]{:S(2)}, u32[]{:S(2)}) collective-permute-start(bf16[144,256]{1,0:T(8,128)(2,1)S(1)} %get-tuple-element.199.send_ref), channel_id=1, source_target_pairs={{2,0},{4,2},{6,4},{8,6},{10,8},{12,10},{14,12},{16,14},{18,16},{20... | collective-permute-start | bytes 221192 | tf_op jit(solution)/shard_map/ppermute | solution.py:318
  294.3 7.2 %collective-permute-start.19 = (bf16[16,256]{1,0:T(8,128)(2,1)S(1)}, bf16[16,256]{1,0:T(8,128)(2,1)S(1)}, u32[]{:S(2)}, u32[]{:S(2)}) collective-permute-start(bf16[16,256]{1,0:T(8,128)(2,1)S(1)} %get-tuple-element.208), channel_id=1, source_target_pairs={{4,0},{6,2},{8,4},{10,6},{12,8},{14,10},{16,12},{18,14},{20,16},{2... | collective-permute-start | bytes 24584 | tf_op jit(solution)/shard_map/ppermute | solution.py:318
  302.3 1.3 collective-permute-start.20
  325.1 8.8 %collective-permute-start.21 = (bf16[144,256]{1,0:T(8,128)(2,1)S(1)}, bf16[144,256]{1,0:T(8,128)(2,1)S(1)}, u32[]{:S(2)}, u32[]{:S(2)}) collective-permute-start(bf16[144,256]{1,0:T(8,128)(2,1)S(1)} %get-tuple-element.215.send_ref), channel_id=1, source_target_pairs={{2,0},{4,2},{6,4},{8,6},{10,8},{12,10},{14,12},{16,14},{18,16},{20... | collective-permute-start | bytes 221192 | tf_op jit(solution)/shard_map/ppermute | solution.py:318
  328.4 7.0 %collective-permute-start.22 = (bf16[16,256]{1,0:T(8,128)(2,1)S(1)}, bf16[16,256]{1,0:T(8,128)(2,1)S(1)}, u32[]{:S(2)}, u32[]{:S(2)}) collective-permute-start(bf16[16,256]{1,0:T(8,128)(2,1)S(1)} %get-tuple-element.224), channel_id=1, source_target_pairs={{4,0},{6,2},{8,4},{10,6},{12,8},{14,10},{16,12},{18,14},{20,16},{2... | collective-permute-start | bytes 24584 | tf_op jit(solution)/shard_map/ppermute | solution.py:318
  337.0 1.4 collective-permute-start.23
  362.7 8.7 %collective-permute-start.24 = (bf16[144,256]{1,0:T(8,128)(2,1)S(1)}, bf16[144,256]{1,0:T(8,128)(2,1)S(1)}, u32[]{:S(2)}, u32[]{:S(2)}) collective-permute-start(bf16[144,256]{1,0:T(8,128)(2,1)S(1)} %get-tuple-element.231.send_ref), channel_id=1, source_target_pairs={{2,0},{4,2},{6,4},{8,6},{10,8},{12,10},{14,12},{16,14},{18,16},{20... | collective-permute-start | bytes 221192 | tf_op jit(solution)/shard_map/ppermute | solution.py:318
  366.7 7.0 %collective-permute-start.25 = (bf16[16,256]{1,0:T(8,128)(2,1)S(1)}, bf16[16,256]{1,0:T(8,128)(2,1)S(1)}, u32[]{:S(2)}, u32[]{:S(2)}) collective-permute-start(bf16[16,256]{1,0:T(8,128)(2,1)S(1)} %get-tuple-element.240), channel_id=1, source_target_pairs={{4,0},{6,2},{8,4},{10,6},{12,8},{14,10},{16,12},{18,14},{20,16},{2... | collective-permute-start | bytes 24584 | tf_op jit(solution)/shard_map/ppermute | solution.py:318
  397.3 6.2 %collective-permute-start.27 = (bf16[144,256]{1,0:T(8,128)(2,1)S(1)}, bf16[144,256]{1,0:T(8,128)(2,1)S(1)}, u32[]{:S(2)}, u32[]{:S(2)}) collective-permute-start(bf16[144,256]{1,0:T(8,128)(2,1)S(1)} %get-tuple-element.246.send_ref), channel_id=1, source_target_pairs={{2,0},{4,2},{6,4},{8,6},{10,8},{12,10},{14,12},{16,14},{18,16},{20... | collective-permute-start | bytes 221192 | tf_op jit(solution)/shard_map/ppermute | solution.py:318
  400.1 7.0 %collective-permute-start.28 = (bf16[16,256]{1,0:T(8,128)(2,1)S(1)}, bf16[16,256]{1,0:T(8,128)(2,1)S(1)}, u32[]{:S(2)}, u32[]{:S(2)}) collective-permute-start(bf16[16,256]{1,0:T(8,128)(2,1)S(1)} %get-tuple-element.251), channel_id=1, source_target_pairs={{4,0},{6,2},{8,4},{10,6},{12,8},{14,10},{16,12},{18,14},{20,16},{2... | collective-permute-start | bytes 24584 | tf_op jit(solution)/shard_map/ppermute | solution.py:318
  (52 other events, 422.0 us)
Sparse Core Ops, SparseCore 0:
  67.4 64.4 all-gather.8
  134.3 57.2 all-gather.10
  194.0 57.7 all-gather.12
  254.1 56.7 all-gather.14

commit v3 on v2

--- a/solution.py
+++ b/solution.py
@@ -92,7 +92,14 @@
     return (col == k * planes * per + z * per + g).astype(F32).astype(BF)
 
 
-def pack_body(planes, slices, width, tp_ref, w_ref, sw_ref, lf_ref, x_ref, other_ref, out_ref):
+def pack_body(
+    planes, slices, width, tp_ref, w_hbm, sw_ref, lf_ref, x_hbm, other_hbm, out_ref,
+    w_ref, x_ref, other_ref, sems,
+):
+    pairs = ((x_hbm, x_ref), (other_hbm, other_ref), (w_hbm, w_ref))
+    copies = [pltpu.make_async_copy(a, b, sems.at[i]) for i, (a, b) in enumerate(pairs)]
+    for copy in copies:
+        copy.start()
     owned = slices * width
     depth = planes * width
     half = slices * depth
@@ -100,11 +107,13 @@
     matrix = swap_matrix(width)
     tp = tp_ref[0]
     start = pl.multiple_of(tp * half, TILE)
-    for source, place in ((x_ref, tp), (other_ref, 1 - tp)):
+    for copy, source, place in ((copies[0], x_ref, tp), (copies[1], other_ref, 1 - tp)):
+        copy.wait()
         pieces = split_owned(source[:, pl.ds(start, half)], planes, width, matrix)
         at = pl.multiple_of(place * count, PAD)
         for z in range(planes):
             out_ref[z, pl.ds(at, count), :] = pieces[z]
+    copies[2].wait()
     for z in range(planes):
         block = w_ref[:, z].reshape(owned, depth)
         turned = block.astype(F32).T.astype(BF)
@@ -341,8 +350,20 @@
     packed = pl.pallas_call(
         functools.partial(pack_body, planes, slices, width),
         out_shape=shape((planes, tokens + depth + AUX, owned), BF),
-        in_specs=[pl.BlockSpec(memory_space=pltpu.SMEM)]
-        + [pl.BlockSpec(memory_space=pltpu.VMEM)] * 5,
+        in_specs=[
+            pl.BlockSpec(memory_space=pltpu.SMEM),
+            pl.BlockSpec(memory_space=pl.ANY),
+            pl.BlockSpec(memory_space=pltpu.VMEM),
+            pl.BlockSpec(memory_space=pltpu.VMEM),
+            pl.BlockSpec(memory_space=pl.ANY),
+            pl.BlockSpec(memory_space=pl.ANY),
+        ],
+        scratch_shapes=[
+            pltpu.VMEM((slices, planes, width, depth), BF),
+            pltpu.VMEM(own_rows.shape, BF),
+            pltpu.VMEM(own_rows.shape, BF),
+            pltpu.SemaphoreType.DMA((3,)),
+        ],
         compiler_params=pltpu.CompilerParams(vmem_limit_bytes=VMEM_LIMIT),
         interpret=INTERPRET,
     )(
@@ -423,7 +444,7 @@
     before.update({p: (others, p) for p in range(top)})
     weights = {top: (first_weights, 0)}
     last = planes - 2
-    for size in (1, 2, 2, planes):
+    for size in (2, 2, planes):
         first = max(0, last - size + 1)
         if last >= first:
             group = gathered(packed, first, last)
@@ -499,6 +520,11 @@
             send, late[0] = lax.optimization_barrier((send, late[0]))
             sums = filter_sums(p + 1, late, sums)
             near, sums = lax.optimization_barrier((near, sums))
+        if 0 < p < top - 1 and weights[p - 1][0] is not group:
+            near, fetched = lax.optimization_barrier((near, weights[p - 1][0]))
+            weights.update(
+                {q: (fetched, i) for q, (g, i) in weights.items() if g is weights[p - 1][0]}
+            )
         if p > 0:
             earlier, at = before[p - 1]
             send, earlier = lax.optimization_barrier((send, earlier))

time: 472 us -> 473 us (level)
  starting transfers between devices: 75.4 us -> 69.5 us
    all_gather x4 -> x3, waiting for transfers between devices: 6.04 us -> 0.02 us  [gathered(): lax.all_gather(source[first:last + 1, tokens:tokens + depth], 'seq', axis=0)]
    ppermute x17, starting transfers between devices: 52.4 us -> 46.5 us  [from_next(): return lax.ppermute(x, 'seq', [(i, i - by) for i in range(by, size)])]
    ppermute x3, waiting for transfers between devices: 17 us -> 22.7 us  [from_before(): return lax.ppermute(x, 'seq', [(i, i + by) for i in range(size - by)])]
    unnamed x100 -> x108, local copies, waits for them, and re-layouts: 21.5 us -> 25.1 us
  transfers between devices with their start and end apart: 35 -> 34, of which waited for: 21 -> 20; matrix products, arithmetic and copies ran while one was open for 1% -> 1% of each run, Pallas kernels for 7% -> 7%
where the time goes in v3:
time: 473 us; the launch traced here: 464 us
  blocking collectives  247 us (52%)
  starting transfers between devices  69.5 us (15%)
  waiting for transfers between devices  61.6 us (13%)
  Pallas kernels  41.7 us (9%)
  local copies, waits for them, and re-layouts  29.1 us (6%)
  between operations  15.2 us (3%)
    all_to_all x7, blocking collectives, per_device(): parts = lax.all_to_all(partial, 'pipe', 0, 0, tiled=True)  148 us
    all_to_all x1, blocking collectives, per_device(): packed = lax.all_to_all(packed, 'pipe', 0, 0, tiled=True)  52.7 us
    ppermute x17, starting transfers between devices, from_next(): return lax.ppermute(x, 'seq', [(i, i - by) for i in range(by, size)])  46.5 us
    pallas_call x36, Pallas kernels, call(): pl.pallas_call(body, out_shape=out_shape, compiler_params=pltpu.CompilerP...  32.4 us
    unnamed x108, local copies, waits for them, and re-layouts  25.1 us
    ppermute x3, waiting for transfers between devices, from_before(): return lax.ppermute(x, 'seq', [(i, i + by) for i in range(size - by)])  22.7 us
    all_to_all x1, blocking collectives, per_device(): results = lax.all_to_all(merged, 'pipe', 0, 0, tiled=True)  20.6 us
    ppermute x17, waiting for transfers between devices, from_next(): return lax.ppermute(x, 'seq', [(i, i - by) for i in range(by, size)])  16.3 us
  transfers between devices with their start and end apart: 34, of which 20 were waited for; matrix products, arithmetic and copies ran while one was open for 1% of the time, Pallas kernels for 7%

profile of v3, /device:TPU:2, one launch (start us, length us, event | category | flops | bytes accessed | tf_op | source)
XLA Modules:
  0.0 464.2 jit_solution(5565744612268946974)
XLA Ops:
  14.3 52.7 %all_to_all.65.own_ref.aux_ref = bf16[8,432,256]{2,1,0:T(8,128)(2,1)S(1)} all-to-all(bf16[8,432,256]{2,1,0:T(8,128)(2,1)S(1)} %shard_map.76), channel_id=1, replica_groups=mesh['pipe'=8,'seq'=16,'tp'=2] {'pipe'}, dimensions={0} | all-to-all | bytes 3538944 | tf_op jit(solution)/shard_map/all_to_all | solution.py:377
  71.0 7.6 %all-to-all-start.1 = ((bf16[16,256,256]{2,1,0:T(8,128)(2,1)}), bf16[16,256,256]{2,1,0:T(8,128)(2,1)}, u32[]{:S(2)}, u32[]{:S(2)}) async-start(bf16[16,256,256]{2,1,0:T(8,128)(2,1)} %broadcast_in_dim.17), calls=%async_computation.1 | async-start | bytes 4194304 | tf_op jit(solution)/shard_map/all_to_all | solution.py:426
  79.2 3.4 collective-permute-start.1
  82.6 4.6 collective-permute-start.2
  87.2 4.3 collective-permute-start.3
  91.6 18.8 %collective-permute-done.1.prev_ref = bf16[1,128,256]{2,1,0:T(8,128)(2,1)S(1)} collective-permute-done((bf16[1,128,256]{2,1,0:T(8,128)(2,1)S(1)}, bf16[1,128,256]{2,1,0:T(8,128)(2,1)S(1)}, u32[]{:S(2)}, u32[]{:S(2)}) %collective-permute-start.1) | collective-permute-done | bytes 65568 | tf_op jit(solution)/shard_map/ppermute | solution.py:332
  117.3 4.1 all-to-all-start.2
  122.3 2.5 collective-permute-start.5
  124.7 12.6 %all-to-all-done.2.parts_ref = bf16[8,128,256]{2,1,0:T(8,128)(2,1)} async-done(((bf16[8,128,256]{2,1,0:T(8,128)(2,1)}), bf16[8,128,256]{2,1,0:T(8,128)(2,1)}, u32[]{:S(2)}, u32[]{:S(2)}) %all-to-all-start.2) | async-done | bytes 524320 | tf_op jit(solution)/shard_map/all_to_all | solution.py:506
  139.6 2.6 collective-permute-start.6
  142.2 2.4 collective-permute-start.7
  144.6 3.1 collective-permute-done.5.prev_ref
  157.1 24.8 %all_to_all.66.parts_ref = bf16[8,128,256]{2,1,0:T(8,128)(2,1)S(1)} all-to-all(bf16[8,128,256]{2,1,0:T(8,128)(2,1)S(1)} %shard_map.83), channel_id=1, replica_groups=mesh['pipe'=8,'seq'=16,'tp'=2] {'pipe'}, dimensions={0} | all-to-all | bytes 1048576 | tf_op jit(solution)/shard_map/all_to_all | solution.py:506
  182.0 2.6 collective-permute-start.9
  194.8 20.5 %all_to_all.67.parts_ref = bf16[8,128,256]{2,1,0:T(8,128)(2,1)S(1)} all-to-all(bf16[8,128,256]{2,1,0:T(8,128)(2,1)S(1)} %shard_map.88), channel_id=1, replica_groups=mesh['pipe'=8,'seq'=16,'tp'=2] {'pipe'}, dimensions={0} | all-to-all | bytes 1048576 | tf_op jit(solution)/shard_map/all_to_all | solution.py:506
  215.4 3.2 collective-permute-start.12
  233.4 20.4 %all_to_all.68.parts_ref = bf16[8,128,256]{2,1,0:T(8,128)(2,1)S(1)} all-to-all(bf16[8,128,256]{2,1,0:T(8,128)(2,1)S(1)} %shard_map.93), channel_id=1, replica_groups=mesh['pipe'=8,'seq'=16,'tp'=2] {'pipe'}, dimensions={0} | all-to-all | bytes 1048576 | tf_op jit(solution)/shard_map/all_to_all | solution.py:506
  253.9 3.2 collective-permute-start.15
  267.3 20.5 %all_to_all.69.parts_ref = bf16[8,128,256]{2,1,0:T(8,128)(2,1)S(1)} all-to-all(bf16[8,128,256]{2,1,0:T(8,128)(2,1)S(1)} %shard_map.98), channel_id=1, replica_groups=mesh['pipe'=8,'seq'=16,'tp'=2] {'pipe'}, dimensions={0} | all-to-all | bytes 1048576 | tf_op jit(solution)/shard_map/all_to_all | solution.py:506
  287.9 3.3 collective-permute-start.18
  291.2 2.5 collective-permute-start.19
  303.4 2.8 copy-done
  307.0 20.5 %all_to_all.70.parts_ref = bf16[8,128,256]{2,1,0:T(8,128)(2,1)S(1)} all-to-all(bf16[8,128,256]{2,1,0:T(8,128)(2,1)S(1)} %shard_map.103), channel_id=1, replica_groups=mesh['pipe'=8,'seq'=16,'tp'=2] {'pipe'}, dimensions={0} | all-to-all | bytes 1048576 | tf_op jit(solution)/shard_map/all_to_all | solution.py:506
  327.6 4.0 collective-permute-start.21
  341.7 20.5 %all_to_all.71.parts_ref = bf16[8,128,256]{2,1,0:T(8,128)(2,1)S(1)} all-to-all(bf16[8,128,256]{2,1,0:T(8,128)(2,1)S(1)} %shard_map.108), channel_id=1, replica_groups=mesh['pipe'=8,'seq'=16,'tp'=2] {'pipe'}, dimensions={0} | all-to-all | bytes 1048576 | tf_op jit(solution)/shard_map/all_to_all | solution.py:506
  362.3 2.8 collective-permute-start.24
  375.1 20.5 %all_to_all.72.parts_ref = bf16[8,128,256]{2,1,0:T(8,128)(2,1)S(1)} all-to-all(bf16[8,128,256]{2,1,0:T(8,128)(2,1)S(1)} %shard_map.113), channel_id=1, replica_groups=mesh['pipe'=8,'seq'=16,'tp'=2] {'pipe'}, dimensions={0} | all-to-all | bytes 1048576 | tf_op jit(solution)/shard_map/all_to_all | solution.py:506
  395.7 3.4 collective-permute-start.27
  402.2 4.0 collective-permute-done.28.far_ref
  408.1 14.3 %all_to_all.73.in_ref = bf16[16,48,128]{2,1,0:T(8,128)(2,1)S(1)} all-to-all(bf16[16,48,128]{2,1,0:T(8,128)(2,1)S(1)} %shard_map.117), channel_id=1, replica_groups=mesh['pipe'=8,'seq'=16,'tp'=2] {'seq'}, dimensions={0} | all-to-all | bytes 393216 | tf_op jit(solution)/shard_map/all_to_all | solution.py:549
  422.5 11.6 %all_to_all.74.sums_ref = bf16[16,48,128]{2,1,0:T(8,128)(2,1)S(1)} all-to-all(bf16[16,48,128]{2,1,0:T(8,128)(2,1)S(1)} %shard_map.118), channel_id=1, replica_groups=mesh['pipe'=8,'seq'=16,'tp'=2] {'seq'}, dimensions={0} | all-to-all | bytes 393216 | tf_op jit(solution)/shard_map/all_to_all | solution.py:553
  434.2 20.6 %all_to_all.75.in_ref = bf16[8,176,256]{2,1,0:T(8,128)(2,1)S(1)} all-to-all(bf16[8,176,256]{2,1,0:T(8,128)(2,1)S(1)} %shard_map.119), channel_id=1, replica_groups=mesh['pipe'=8,'seq'=16,'tp'=2] {'pipe'}, dimensions={0} | all-to-all | bytes 1441792 | tf_op jit(solution)/shard_map/all_to_all | solution.py:555
  (213 shorter events, 104.1 us)
Async XLA Ops:
  7.2 146.0 %all-gather.7.cloned.1.call-start = ((), (), s32[]{:S(2)}) async-start(), calls=%async_computation.13 | async-start | bytes 4456448 | tf_op jit(solution)/shard_map/all_gather | solution.py:421
  7.2 2.2 collective-permute-start
  67.9 155.5 %all-gather.9.cloned.1.call-start = ((), (), s32[]{:S(2)}) async-start(), calls=%async_computation.14 | async-start | bytes 4456448 | tf_op jit(solution)/shard_map/all_gather | solution.py:421
  68.7 228.6 %all-gather.11.cloned.1.call-start = ((), (), s32[]{:S(2)}) async-start(), calls=%async_computation.15 | async-start | bytes 6684672 | tf_op jit(solution)/shard_map/all_gather | solution.py:421
  71.0 42.6 %all-to-all-start.1 = ((bf16[16,256,256]{2,1,0:T(8,128)(2,1)}), bf16[16,256,256]{2,1,0:T(8,128)(2,1)}, u32[]{:S(2)}, u32[]{:S(2)}) async-start(bf16[16,256,256]{2,1,0:T(8,128)(2,1)} %broadcast_in_dim.17), calls=%async_computation.1 | async-start | bytes 4194304 | tf_op jit(solution)/shard_map/all_to_all | solution.py:426
  79.2 31.2 %collective-permute-start.1 = (bf16[1,128,256]{2,1,0:T(8,128)(2,1)S(1)}, bf16[1,128,256]{2,1,0:T(8,128)(2,1)S(1)}, u32[]{:S(2)}, u32[]{:S(2)}) collective-permute-start(bf16[1,128,256]{2,1,0:T(8,128)(2,1)S(1)} %slice.37), channel_id=1, source_target_pairs={{0,2},{2,4},{4,6},{6,8},{8,10},{10,12},{12,14},{14,16},{16,18},{18... | collective-permute-start | bytes 196616 | tf_op jit(solution)/shard_map/ppermute | solution.py:332
  82.6 28.6 %collective-permute-start.2 = (bf16[8,16,256]{2,1,0:T(8,128)(2,1)S(1)}, bf16[8,16,256]{2,1,0:T(8,128)(2,1)S(1)}, u32[]{:S(2)}, u32[]{:S(2)}) collective-permute-start(bf16[8,16,256]{2,1,0:T(8,128)(2,1)S(1)} %get-tuple-element.276), channel_id=1, source_target_pairs={{0,4},{2,6},{4,8},{6,10},{8,12},{10,14},{12,16},{14,18},{16,20},{1... | collective-permute-start | bytes 196616 | tf_op jit(solution)/shard_map/ppermute | solution.py:332
  87.2 24.0 %collective-permute-start.3 = (bf16[8,16,256]{2,1,0:T(8,128)(2,1)S(1)}, bf16[8,16,256]{2,1,0:T(8,128)(2,1)S(1)}, u32[]{:S(2)}, u32[]{:S(2)}) collective-permute-start(bf16[8,16,256]{2,1,0:T(8,128)(2,1)S(1)} %get-tuple-element.275), channel_id=1, source_target_pairs={{2,0},{4,2},{6,4},{8,6},{10,8},{12,10},{14,12},{16,14},{18,16},{20... | collective-permute-start | bytes 196616 | tf_op jit(solution)/shard_map/ppermute | solution.py:327
  91.5 22.1 %collective-permute-start.4 = (bf16[128,256]{1,0:T(8,128)(2,1)S(1)}, bf16[128,256]{1,0:T(8,128)(2,1)S(1)}, u32[]{:S(2)}, u32[]{:S(2)}) collective-permute-start(bf16[128,256]{1,0:T(8,128)(2,1)S(1)} %dynamic-slice_bitcast_fusion.own_ref.grad_ref), channel_id=1, source_target_pairs={{0,1},{1,0},{2,3},{3,2},{4,5},{5,4},{6,7},{7,6},{8,9},{9,8},{10,11... | collective-permute-start | bytes 196616 | tf_op jit(solution)/shard_map/ppermute | solution.py:436
  117.3 20.1 %all-to-all-start.2 = ((bf16[8,128,256]{2,1,0:T(8,128)(2,1)}), bf16[8,128,256]{2,1,0:T(8,128)(2,1)}, u32[]{:S(2)}, u32[]{:S(2)}) async-start(bf16[8,128,256]{2,1,0:T(8,128)(2,1)} %copy-done.30), calls=%async_computation.2 | async-start | bytes 1048576 | tf_op jit(solution)/shard_map/all_to_all | solution.py:506
  122.3 25.4 %collective-permute-start.5 = (bf16[7,128,256]{2,1,0:T(8,128)(2,1)}, bf16[7,128,256]{2,1,0:T(8,128)(2,1)S(1)}, u32[]{:S(2)}, u32[]{:S(2)}) collective-permute-start(bf16[7,128,256]{2,1,0:T(8,128)(2,1)} %slice.31), channel_id=1, source_target_pairs={{0,2},{2,4},{4,6},{6,8},{8,10},{10,12},{12,14},{14,16},{16,18},{18... | collective-permute-start | bytes 1376264 | tf_op jit(solution)/shard_map/ppermute | solution.py:332
  139.6 10.8 %collective-permute-start.6 = (bf16[144,256]{1,0:T(8,128)(2,1)S(1)}, bf16[144,256]{1,0:T(8,128)(2,1)S(1)}, u32[]{:S(2)}, u32[]{:S(2)}) collective-permute-start(bf16[144,256]{1,0:T(8,128)(2,1)S(1)} %get-tuple-element.143.send_ref), channel_id=1, source_target_pairs={{2,0},{4,2},{6,4},{8,6},{10,8},{12,10},{14,12},{16,14},{18,16},{20... | collective-permute-start | bytes 221192 | tf_op jit(solution)/shard_map/ppermute | solution.py:327
  142.2 8.2 %collective-permute-start.7 = (bf16[16,256]{1,0:T(8,128)(2,1)S(1)}, bf16[16,256]{1,0:T(8,128)(2,1)S(1)}, u32[]{:S(2)}, u32[]{:S(2)}) collective-permute-start(bf16[16,256]{1,0:T(8,128)(2,1)S(1)} %get-tuple-element.149), channel_id=1, source_target_pairs={{4,0},{6,2},{8,4},{10,6},{12,8},{14,10},{16,12},{18,14},{20,16},{2... | collective-permute-start | bytes 24584 | tf_op jit(solution)/shard_map/ppermute | solution.py:327
  182.0 7.6 %collective-permute-start.9 = (bf16[144,256]{1,0:T(8,128)(2,1)S(1)}, bf16[144,256]{1,0:T(8,128)(2,1)S(1)}, u32[]{:S(2)}, u32[]{:S(2)}) collective-permute-start(bf16[144,256]{1,0:T(8,128)(2,1)S(1)} %get-tuple-element.156.send_ref), channel_id=1, source_target_pairs={{2,0},{4,2},{6,4},{8,6},{10,8},{12,10},{14,12},{16,14},{18,16},{20... | collective-permute-start | bytes 221192 | tf_op jit(solution)/shard_map/ppermute | solution.py:327
  184.6 7.2 %collective-permute-start.10 = (bf16[16,256]{1,0:T(8,128)(2,1)S(1)}, bf16[16,256]{1,0:T(8,128)(2,1)S(1)}, u32[]{:S(2)}, u32[]{:S(2)}) collective-permute-start(bf16[16,256]{1,0:T(8,128)(2,1)S(1)} %get-tuple-element.164), channel_id=1, source_target_pairs={{4,0},{6,2},{8,4},{10,6},{12,8},{14,10},{16,12},{18,14},{20,16},{2... | collective-permute-start | bytes 24584 | tf_op jit(solution)/shard_map/ppermute | solution.py:327
  192.7 1.3 collective-permute-start.11
  215.4 8.0 %collective-permute-start.12 = (bf16[144,256]{1,0:T(8,128)(2,1)S(1)}, bf16[144,256]{1,0:T(8,128)(2,1)S(1)}, u32[]{:S(2)}, u32[]{:S(2)}) collective-permute-start(bf16[144,256]{1,0:T(8,128)(2,1)S(1)} %get-tuple-element.171.send_ref), channel_id=1, source_target_pairs={{2,0},{4,2},{6,4},{8,6},{10,8},{12,10},{14,12},{16,14},{18,16},{20... | collective-permute-start | bytes 221192 | tf_op jit(solution)/shard_map/ppermute | solution.py:327
  218.6 7.2 %collective-permute-start.13 = (bf16[16,256]{1,0:T(8,128)(2,1)S(1)}, bf16[16,256]{1,0:T(8,128)(2,1)S(1)}, u32[]{:S(2)}, u32[]{:S(2)}) collective-permute-start(bf16[16,256]{1,0:T(8,128)(2,1)S(1)} %get-tuple-element.181), channel_id=1, source_target_pairs={{4,0},{6,2},{8,4},{10,6},{12,8},{14,10},{16,12},{18,14},{20,16},{2... | collective-permute-start | bytes 24584 | tf_op jit(solution)/shard_map/ppermute | solution.py:327
  229.0 1.3 collective-permute-start.14
  253.9 8.2 %collective-permute-start.15 = (bf16[144,256]{1,0:T(8,128)(2,1)S(1)}, bf16[144,256]{1,0:T(8,128)(2,1)S(1)}, u32[]{:S(2)}, u32[]{:S(2)}) collective-permute-start(bf16[144,256]{1,0:T(8,128)(2,1)S(1)} %get-tuple-element.189.send_ref), channel_id=1, source_target_pairs={{2,0},{4,2},{6,4},{8,6},{10,8},{12,10},{14,12},{16,14},{18,16},{20... | collective-permute-start | bytes 221192 | tf_op jit(solution)/shard_map/ppermute | solution.py:327
  257.1 7.2 %collective-permute-start.16 = (bf16[16,256]{1,0:T(8,128)(2,1)S(1)}, bf16[16,256]{1,0:T(8,128)(2,1)S(1)}, u32[]{:S(2)}, u32[]{:S(2)}) collective-permute-start(bf16[16,256]{1,0:T(8,128)(2,1)S(1)} %get-tuple-element.198), channel_id=1, source_target_pairs={{4,0},{6,2},{8,4},{10,6},{12,8},{14,10},{16,12},{18,14},{20,16},{2... | collective-permute-start | bytes 24584 | tf_op jit(solution)/shard_map/ppermute | solution.py:327
  265.2 1.3 collective-permute-start.17
  287.9 8.7 %collective-permute-start.18 = (bf16[144,256]{1,0:T(8,128)(2,1)S(1)}, bf16[144,256]{1,0:T(8,128)(2,1)S(1)}, u32[]{:S(2)}, u32[]{:S(2)}) collective-permute-start(bf16[144,256]{1,0:T(8,128)(2,1)S(1)} %get-tuple-element.205.send_ref), channel_id=1, source_target_pairs={{2,0},{4,2},{6,4},{8,6},{10,8},{12,10},{14,12},{16,14},{18,16},{20... | collective-permute-start | bytes 221192 | tf_op jit(solution)/shard_map/ppermute | solution.py:327
  291.2 7.0 %collective-permute-start.19 = (bf16[16,256]{1,0:T(8,128)(2,1)S(1)}, bf16[16,256]{1,0:T(8,128)(2,1)S(1)}, u32[]{:S(2)}, u32[]{:S(2)}) collective-permute-start(bf16[16,256]{1,0:T(8,128)(2,1)S(1)} %get-tuple-element.215), channel_id=1, source_target_pairs={{4,0},{6,2},{8,4},{10,6},{12,8},{14,10},{16,12},{18,14},{20,16},{2... | collective-permute-start | bytes 24584 | tf_op jit(solution)/shard_map/ppermute | solution.py:327
  302.1 1.3 collective-permute-start.20
  327.6 9.0 %collective-permute-start.21 = (bf16[144,256]{1,0:T(8,128)(2,1)S(1)}, bf16[144,256]{1,0:T(8,128)(2,1)S(1)}, u32[]{:S(2)}, u32[]{:S(2)}) collective-permute-start(bf16[144,256]{1,0:T(8,128)(2,1)S(1)} %get-tuple-element.223.send_ref), channel_id=1, source_target_pairs={{2,0},{4,2},{6,4},{8,6},{10,8},{12,10},{14,12},{16,14},{18,16},{20... | collective-permute-start | bytes 221192 | tf_op jit(solution)/shard_map/ppermute | solution.py:327
  331.7 7.0 %collective-permute-start.22 = (bf16[16,256]{1,0:T(8,128)(2,1)S(1)}, bf16[16,256]{1,0:T(8,128)(2,1)S(1)}, u32[]{:S(2)}, u32[]{:S(2)}) collective-permute-start(bf16[16,256]{1,0:T(8,128)(2,1)S(1)} %get-tuple-element.232), channel_id=1, source_target_pairs={{4,0},{6,2},{8,4},{10,6},{12,8},{14,10},{16,12},{18,14},{20,16},{2... | collective-permute-start | bytes 24584 | tf_op jit(solution)/shard_map/ppermute | solution.py:327
  339.5 1.3 collective-permute-start.23
  362.3 7.5 %collective-permute-start.24 = (bf16[144,256]{1,0:T(8,128)(2,1)S(1)}, bf16[144,256]{1,0:T(8,128)(2,1)S(1)}, u32[]{:S(2)}, u32[]{:S(2)}) collective-permute-start(bf16[144,256]{1,0:T(8,128)(2,1)S(1)} %get-tuple-element.239.send_ref), channel_id=1, source_target_pairs={{2,0},{4,2},{6,4},{8,6},{10,8},{12,10},{14,12},{16,14},{18,16},{20... | collective-permute-start | bytes 221192 | tf_op jit(solution)/shard_map/ppermute | solution.py:327
  365.1 7.0 %collective-permute-start.25 = (bf16[16,256]{1,0:T(8,128)(2,1)S(1)}, bf16[16,256]{1,0:T(8,128)(2,1)S(1)}, u32[]{:S(2)}, u32[]{:S(2)}) collective-permute-start(bf16[16,256]{1,0:T(8,128)(2,1)S(1)} %get-tuple-element.248), channel_id=1, source_target_pairs={{4,0},{6,2},{8,4},{10,6},{12,8},{14,10},{16,12},{18,14},{20,16},{2... | collective-permute-start | bytes 24584 | tf_op jit(solution)/shard_map/ppermute | solution.py:327
  395.7 6.4 %collective-permute-start.27 = (bf16[144,256]{1,0:T(8,128)(2,1)S(1)}, bf16[144,256]{1,0:T(8,128)(2,1)S(1)}, u32[]{:S(2)}, u32[]{:S(2)}) collective-permute-start(bf16[144,256]{1,0:T(8,128)(2,1)S(1)} %get-tuple-element.254.send_ref), channel_id=1, source_target_pairs={{2,0},{4,2},{6,4},{8,6},{10,8},{12,10},{14,12},{16,14},{18,16},{20... | collective-permute-start | bytes 221192 | tf_op jit(solution)/shard_map/ppermute | solution.py:327
  399.1 7.0 %collective-permute-start.28 = (bf16[16,256]{1,0:T(8,128)(2,1)S(1)}, bf16[16,256]{1,0:T(8,128)(2,1)S(1)}, u32[]{:S(2)}, u32[]{:S(2)}) collective-permute-start(bf16[16,256]{1,0:T(8,128)(2,1)S(1)} %get-tuple-element.259), channel_id=1, source_target_pairs={{4,0},{6,2},{8,4},{10,6},{12,8},{14,10},{16,12},{18,14},{20,16},{2... | collective-permute-start | bytes 24584 | tf_op jit(solution)/shard_map/ppermute | solution.py:327
  (55 other events, 417.3 us)
Sparse Core Ops, SparseCore 0:
  68.0 80.1 all-gather.6
  150.7 55.7 all-gather.8
  209.0 66.4 all-gather.10

commit v4 on v2

--- a/solution.py
+++ b/solution.py
@@ -92,10 +92,30 @@
     return (col == k * planes * per + z * per + g).astype(F32).astype(BF)
 
 
-def pack_body(planes, slices, width, tp_ref, w_ref, sw_ref, lf_ref, x_ref, other_ref, out_ref):
+def pack_body(planes, slices, width, w_ref, sw_ref, lf_ref, out_ref):
     owned = slices * width
     depth = planes * width
     half = slices * depth
+    for z in range(planes):
+        block = w_ref[:, z].reshape(owned, depth)
+        turned = block.astype(F32).T.astype(BF)
+        low = AUX + z * width
+        out_ref[:, low : low + width, :] = turned.reshape(planes, width, owned)
+    taps = [sw_ref[j].astype(F32) for j in range(KS)]
+    taps.append(jnp.zeros((32 - 3 * KS, half), F32))
+    taps = jnp.concatenate(taps, axis=0).astype(BF)
+    taps = split_owned(taps, planes, width, swap_matrix(width))
+    per = width // GW
+    filters = dot(filter_rows(slices, planes, per), lf_ref[...]).astype(BF)
+    groups = slices * per
+    for z in range(planes):
+        out_ref[z, 0:32, :] = taps[z]
+        out_ref[z, 32:AUX, :] = jnp.zeros((GW, owned), BF)
+        out_ref[z, 32 : 32 + groups, :KL] = filters[z * groups : (z + 1) * groups]
+
+
+def scatter_body(planes, slices, width, tp_ref, x_ref, other_ref, out_ref):
+    half = slices * planes * width
     count = x_ref.shape[0]
     matrix = swap_matrix(width)
     tp = tp_ref[0]
@@ -105,22 +125,6 @@
         at = pl.multiple_of(place * count, PAD)
         for z in range(planes):
             out_ref[z, pl.ds(at, count), :] = pieces[z]
-    for z in range(planes):
-        block = w_ref[:, z].reshape(owned, depth)
-        turned = block.astype(F32).T.astype(BF)
-        low = KL + z * width
-        out_ref[:, low : low + width, :] = turned.reshape(planes, width, owned)
-    base = KL + depth
-    taps = [sw_ref[j].astype(F32) for j in range(KS)]
-    taps.append(jnp.zeros((32 - 3 * KS, half), F32))
-    taps = split_owned(jnp.concatenate(taps, axis=0).astype(BF), planes, width, matrix)
-    per = width // GW
-    filters = dot(filter_rows(slices, planes, per), lf_ref[...]).astype(BF)
-    groups = slices * per
-    for z in range(planes):
-        out_ref[z, base : base + 32, :] = taps[z]
-        out_ref[z, base + 32 : base + AUX, :] = jnp.zeros((GW, owned), BF)
-        out_ref[z, base + 32 : base + 32 + groups, :KL] = filters[z * groups : (z + 1) * groups]
 
 
 def shuffle_body(planes, width, x_ref, out_ref):
@@ -335,29 +339,40 @@
     tokens = out_grad.shape[0]
     dims = long_filters.shape[1]
 
+    top = planes - 1
     tp_index = lax.axis_index("tp").astype(jnp.int32).reshape(1)
     own_rows = layer_inputs[0]
     swapped = lax.ppermute(own_rows, "tp", [(0, 1), (1, 0)])
-    packed = pl.pallas_call(
+    packed = call(
         functools.partial(pack_body, planes, slices, width),
-        out_shape=shape((planes, tokens + depth + AUX, owned), BF),
-        in_specs=[pl.BlockSpec(memory_space=pltpu.SMEM)]
-        + [pl.BlockSpec(memory_space=pltpu.VMEM)] * 5,
-        compiler_params=pltpu.CompilerParams(vmem_limit_bytes=VMEM_LIMIT),
-        interpret=INTERPRET,
-    )(
-        tp_index,
+        shape((planes, AUX + depth, owned), BF),
         out_weights[0].reshape(slices, planes, width, depth),
         short_weights[0],
         long_filters[0],
+    )
+    packed = lax.all_to_all(packed, "pipe", 0, 0, tiled=True)
+    scattered = call(
+        functools.partial(scatter_body, planes, slices, width),
+        shape((planes, tokens, owned), BF),
+        tp_index,
         own_rows,
         swapped,
-    )
-    packed = lax.all_to_all(packed, "pipe", 0, 0, tiled=True)
-    top = planes - 1
-
-    before2 = from_before(packed[:, tokens - PAD : tokens], 2)
-    after = from_next(packed[:, :PAD], 1)
+        in_specs=[pl.BlockSpec(memory_space=pltpu.SMEM)]
+        + [pl.BlockSpec(memory_space=pltpu.VMEM)] * 2,
+    )
+
+    def gathered(source, first, last):
+        pieces = lax.all_gather(source[first : last + 1, AUX:], "seq", axis=0)
+        return pieces.reshape(blocks, last + 1 - first, planes, width, owned)
+
+    copies = jnp.broadcast_to(packed[top, AUX:][None], (blocks, depth, owned))
+    pieces = lax.all_to_all(copies, "seq", 0, 0, tiled=True)
+    first_weights = pieces.reshape(blocks, 1, planes, width, owned)
+    first_weights, scattered = lax.optimization_barrier((first_weights, scattered))
+    rows = lax.all_to_all(scattered, "pipe", 0, 0, tiled=True)
+    before = from_before(rows, 1)
+    before2 = from_before(rows[:, tokens - PAD :], 2)
+    after = from_next(rows[:, :PAD], 1)
 
     def whole(x):
         return pl.BlockSpec(x.shape, lambda i: (0,) * len(x.shape))
@@ -366,25 +381,25 @@
         return pl.BlockSpec((None, count, x.shape[2]), lambda i, p=p, at=at: (p, at, 0))
 
     def own_block(p):
-        return plane(packed, p, tokens)
+        return plane(rows, p, tokens)
 
     def aux_block(p):
-        return plane(packed, p, AUX, (tokens + depth) // AUX)
-
-    def recomputed(p, before, at):
+        return plane(packed, p, AUX)
+
+    def recomputed(p, earlier):
         results = (shape((4 * REACH, owned), F32), shape((groups * KL + WIN, owned), BF))
         return call(
             functools.partial(recompute_body, groups),
             results,
-            packed,
-            before,
+            rows,
+            earlier,
             before2,
             after,
             packed,
             grid=(1,),
             in_specs=[
                 own_block(p),
-                plane(before, at, tokens),
+                plane(earlier, p, tokens),
                 plane(before2, p, PAD),
                 plane(after, p, PAD),
                 aux_block(p),
@@ -396,15 +411,6 @@
             ],
         )
 
-    def gathered(source, first, last):
-        pieces = lax.all_gather(source[first : last + 1, tokens : tokens + depth], "seq", axis=0)
-        return pieces.reshape(blocks, last + 1 - first, planes, width, owned)
-
-    def copied(p):
-        copies = jnp.broadcast_to(packed[p, tokens : tokens + depth][None], (blocks, depth, owned))
-        pieces = lax.all_to_all(copies, "seq", 0, 0, tiled=True)
-        return pieces.reshape(blocks, 1, planes, width, owned)
-
     starts = call(
         functools.partial(shuffle_body, planes, width),
         shape((planes, tokens, owned), BF),
@@ -414,13 +420,7 @@
     swap = [(0, 1), (1, 0)]
     other = lax.ppermute(grad, "tp", swap)
 
-    before = {top: (from_before(packed[top:, :tokens], 1), 0)}
-    saved = {top: recomputed(top, *before[top])}
-    first_weights, saved[top], source, grad, other = lax.optimization_barrier(
-        (copied(top), saved[top], packed, grad, other)
-    )
-    others = from_before(source[:top, :tokens], 1)
-    before.update({p: (others, p) for p in range(top)})
+    saved = {top: recomputed(top, before)}
     weights = {top: (first_weights, 0)}
     last = planes - 2
     for size in (1, 2, 2, planes):
@@ -433,10 +433,9 @@
     def filter_sums(p, operands, sums):
         halves = owned // TILE
         result = shape((planes * halves, AUX, TILE), BF)
-        earlier, at = before[p]
         specs = [whole(x) for x in operands]
-        specs += [own_block(p), plane(earlier, at, PAD, tokens // PAD - 1)]
-        operands = [*operands, packed, earlier]
+        specs += [own_block(p), plane(before, p, PAD, tokens // PAD - 1)]
+        operands = [*operands, rows, before]
         aliases = {}
         if sums is not None:
             aliases = {len(operands): 0}
@@ -482,6 +481,8 @@
             compiler_params=pltpu.CompilerParams(vmem_limit_bytes=VMEM_LIMIT),
             interpret=INTERPRET,
         )(tp_index, grad, other, group)
+        if p == top:
+            partial, rows = lax.optimization_barrier((partial, rows))
         parts = lax.all_to_all(partial, "pipe", 0, 0, tiled=True)
         send, dgate, early = call(
             gate_body,
@@ -499,10 +500,14 @@
             send, late[0] = lax.optimization_barrier((send, late[0]))
             sums = filter_sums(p + 1, late, sums)
             near, sums = lax.optimization_barrier((near, sums))
+        if 0 < p < top - 1 and weights[p - 1][0] is not group:
+            near, fetched = lax.optimization_barrier((near, weights[p - 1][0]))
+            weights.update(
+                {q: (fetched, i) for q, (g, i) in weights.items() if g is weights[p - 1][0]}
+            )
         if p > 0:
-            earlier, at = before[p - 1]
-            send, earlier = lax.optimization_barrier((send, earlier))
-            saved[p - 1] = recomputed(p - 1, earlier, at)
+            send, earlier = lax.optimization_barrier((send, before))
+            saved[p - 1] = recomputed(p - 1, earlier)
             near, saved[p - 1] = lax.optimization_barrier((near, saved[p - 1]))
         results = (shape((KL, owned), BF), shape((3 * KL, owned), F32))
         operands = (send, dgate, near, far, features, back, packed, grad)

time: 472 us -> 481 us (1.019)
  local copies, waits for them, and re-layouts: 25.5 us -> 40.2 us
  blocking collectives: 245 us -> 237 us
    all_to_all x1 -> x2, waiting for transfers between devices: 0.01 us -> 29.2 us  [the longest x1 20.6 us: per_device(): pieces = lax.all_to_all(copies, 'seq', 0, 0, tiled=True)]
    ppermute x3 -> x2, waiting for transfers between devices: 17 us -> 0.01 us  [from_before(): return lax.ppermute(x, 'seq', [(i, i + by) for i in range(size - by)])]
    unnamed x100 -> x120, local copies, waits for them, and re-layouts: 21.5 us -> 37.1 us
    all_to_all x1, blocking collectives: 52.7 us -> 41.2 us  [per_device(): packed = lax.all_to_all(packed, 'pipe', 0, 0, tiled=True)]
    all_to_all x1, waiting for transfers between devices: 10.9 us -> 0.01 us  [per_device(): parts = lax.all_to_all(partial, 'pipe', 0, 0, tiled=True)]
    all_gather x4, waiting for transfers between devices: 6.04 us -> 0.03 us  [gathered(): pieces = lax.all_gather(source[first:last + 1, AUX:], 'seq', axis=0)]
    pallas_call x36 -> x38, Pallas kernels: 32.4 us -> 37.5 us  [call(): pl.pallas_call(body, out_shape=out_shape, compiler_params=pltpu.CompilerP...]
    all_to_all x1 -> x2, starting transfers between devices: 7.61 us -> 11.1 us  [the longest x1 7.48 us: per_device(): pieces = lax.all_to_all(copies, 'seq', 0, 0, tiled=True)]
  transfers between devices with their start and end apart: 35 -> 35, of which waited for: 21 -> 21; matrix products, arithmetic and copies ran while one was open for 1% -> 1% of each run, Pallas kernels for 7% -> 8%
where the time goes in v4:
time: 481 us; the launch traced here: 471 us
  blocking collectives  237 us (49%)
  starting transfers between devices  75.7 us (16%)
  waiting for transfers between devices  57.9 us (12%)
  Pallas kernels  45.4 us (9%)
  local copies, waits for them, and re-layouts  40.2 us (8%)
  between operations  15.2 us (3%)
    all_to_all x7, blocking collectives, per_device(): parts = lax.all_to_all(partial, 'pipe', 0, 0, tiled=True)  148 us
    ppermute x17, starting transfers between devices, from_next(): return lax.ppermute(x, 'seq', [(i, i - by) for i in range(by, size)])  50.4 us
    all_to_all x1, blocking collectives, per_device(): packed = lax.all_to_all(packed, 'pipe', 0, 0, tiled=True)  41.2 us
    pallas_call x38, Pallas kernels, call(): pl.pallas_call(body, out_shape=out_shape, compiler_params=pltpu.CompilerP...  37.5 us
    unnamed x120, local copies, waits for them, and re-layouts  37.1 us
    all_to_all x1, waiting for transfers between devices, per_device(): pieces = lax.all_to_all(copies, 'seq', 0, 0, tiled=True)  20.6 us
    all_to_all x1, blocking collectives, per_device(): results = lax.all_to_all(merged, 'pipe', 0, 0, tiled=True)  20.6 us
    all_to_all x1, blocking collectives, per_device(): exchanged = lax.all_to_all(sums, 'seq', 0, 0, tiled=True)  15.6 us
  transfers between devices with their start and end apart: 35, of which 21 were waited for; matrix products, arithmetic and copies ran while one was open for 1% of the time, Pallas kernels for 8%

profile of v4, /device:TPU:2, one launch (start us, length us, event | category | flops | bytes accessed | tf_op | source)
XLA Modules:
  0.0 471.3 jit_solution(9380540537427011230)
XLA Ops:
  10.8 41.2 %all_to_all.70.aux_ref = bf16[8,304,256]{2,1,0:T(8,128)(2,1)S(1)} all-to-all(bf16[8,304,256]{2,1,0:T(8,128)(2,1)S(1)} %shard_map.77), channel_id=1, replica_groups=mesh['pipe'=8,'seq'=16,'tp'=2] {'pipe'}, dimensions={0} | all-to-all | bytes 2490368 | tf_op jit(solution)/shard_map/all_to_all | solution.py:353
  56.0 7.5 %all-to-all-start.1 = ((bf16[16,256,256]{2,1,0:T(8,128)(2,1)}), bf16[16,256,256]{2,1,0:T(8,128)(2,1)S(1)}, u32[]{:S(2)}, u32[]{:S(2)}) async-start(bf16[16,256,256]{2,1,0:T(8,128)(2,1)} %broadcast_in_dim.17), calls=%async_computation.1 | async-start | bytes 4194304 | tf_op jit(solution)/shard_map/all_to_all | solution.py:369
  70.2 20.6 %all-to-all-done.1 = bf16[16,256,256]{2,1,0:T(8,128)(2,1)S(1)} async-done(((bf16[16,256,256]{2,1,0:T(8,128)(2,1)}), bf16[16,256,256]{2,1,0:T(8,128)(2,1)S(1)}, u32[]{:S(2)}, u32[]{:S(2)}) %all-to-all-start.1) | async-done | bytes 2097184 | tf_op jit(solution)/shard_map/all_to_all | solution.py:369
  92.2 3.6 all-to-all-start.2
  101.5 8.6 %all-to-all-done.2.own_ref = bf16[8,128,256]{2,1,0:T(8,128)(2,1)S(1)} async-done(((bf16[8,128,256]{2,1,0:T(8,128)(2,1)}), bf16[8,128,256]{2,1,0:T(8,128)(2,1)S(1)}, u32[]{:S(2)}, u32[]{:S(2)}) %all-to-all-start.2) | async-done | bytes 524320 | tf_op jit(solution)/shard_map/all_to_all | solution.py:372
  110.0 4.2 all-to-all-start.3
  114.2 2.5 collective-permute-start.2
  116.7 6.7 %collective-permute-start.3 = (bf16[8,16,256]{2,1,0:T(8,128)(2,1)S(1)}, bf16[8,16,256]{2,1,0:T(8,128)(2,1)S(1)}, u32[]{:S(2)}, u32[]{:S(2)}) collective-permute-start(bf16[8,16,256]{2,1,0:T(8,128)(2,1)S(1)} %get-tuple-element.275), channel_id=1, source_target_pairs={{0,4},{2,6},{4,8},{6,10},{8,12},{10,14},{12,16},{14,18},{16,20},{1... | collective-permute-start | bytes 196616 | tf_op jit(solution)/shard_map/ppermute | solution.py:327
  123.5 4.6 collective-permute-start.4
  128.1 3.0 collective-permute-done.4.next_ref
  136.9 6.5 %collective-permute-start.5 = (bf16[144,256]{1,0:T(8,128)(2,1)S(1)}, bf16[144,256]{1,0:T(8,128)(2,1)S(1)}, u32[]{:S(2)}, u32[]{:S(2)}) collective-permute-start(bf16[144,256]{1,0:T(8,128)(2,1)S(1)} %get-tuple-element.138.send_ref), channel_id=1, source_target_pairs={{2,0},{4,2},{6,4},{8,6},{10,8},{12,10},{14,12},{16,14},{18,16},{20... | collective-permute-start | bytes 221192 | tf_op jit(solution)/shard_map/ppermute | solution.py:322
  157.4 24.8 %all_to_all.71.parts_ref = bf16[8,128,256]{2,1,0:T(8,128)(2,1)S(1)} all-to-all(bf16[8,128,256]{2,1,0:T(8,128)(2,1)S(1)} %shard_map.84), channel_id=1, replica_groups=mesh['pipe'=8,'seq'=16,'tp'=2] {'pipe'}, dimensions={0} | all-to-all | bytes 1048576 | tf_op jit(solution)/shard_map/all_to_all | solution.py:486
  182.2 2.8 collective-permute-start.8
  195.9 2.3 copy-done.4
  199.0 20.6 %all_to_all.72.parts_ref = bf16[8,128,256]{2,1,0:T(8,128)(2,1)S(1)} all-to-all(bf16[8,128,256]{2,1,0:T(8,128)(2,1)S(1)} %shard_map.89), channel_id=1, replica_groups=mesh['pipe'=8,'seq'=16,'tp'=2] {'pipe'}, dimensions={0} | all-to-all | bytes 1048576 | tf_op jit(solution)/shard_map/all_to_all | solution.py:486
  219.6 3.6 collective-permute-start.11
  233.5 20.5 %all_to_all.73.parts_ref = bf16[8,128,256]{2,1,0:T(8,128)(2,1)S(1)} all-to-all(bf16[8,128,256]{2,1,0:T(8,128)(2,1)S(1)} %shard_map.94), channel_id=1, replica_groups=mesh['pipe'=8,'seq'=16,'tp'=2] {'pipe'}, dimensions={0} | all-to-all | bytes 1048576 | tf_op jit(solution)/shard_map/all_to_all | solution.py:486
  254.1 3.0 collective-permute-start.14
  257.1 2.7 collective-permute-start.15
  271.4 20.6 %all_to_all.74.parts_ref = bf16[8,128,256]{2,1,0:T(8,128)(2,1)S(1)} all-to-all(bf16[8,128,256]{2,1,0:T(8,128)(2,1)S(1)} %shard_map.99), channel_id=1, replica_groups=mesh['pipe'=8,'seq'=16,'tp'=2] {'pipe'}, dimensions={0} | all-to-all | bytes 1048576 | tf_op jit(solution)/shard_map/all_to_all | solution.py:486
  292.2 4.1 collective-permute-start.17
  306.3 20.5 %all_to_all.75.parts_ref = bf16[8,128,256]{2,1,0:T(8,128)(2,1)S(1)} all-to-all(bf16[8,128,256]{2,1,0:T(8,128)(2,1)S(1)} %shard_map.104), channel_id=1, replica_groups=mesh['pipe'=8,'seq'=16,'tp'=2] {'pipe'}, dimensions={0} | all-to-all | bytes 1048576 | tf_op jit(solution)/shard_map/all_to_all | solution.py:486
  327.5 2.8 collective-permute-start.20
  346.6 20.5 %all_to_all.76.parts_ref = bf16[8,128,256]{2,1,0:T(8,128)(2,1)S(1)} all-to-all(bf16[8,128,256]{2,1,0:T(8,128)(2,1)S(1)} %shard_map.109), channel_id=1, replica_groups=mesh['pipe'=8,'seq'=16,'tp'=2] {'pipe'}, dimensions={0} | all-to-all | bytes 1048576 | tf_op jit(solution)/shard_map/all_to_all | solution.py:486
  367.2 3.5 collective-permute-start.23
  375.4 2.3 collective-permute-done.24.far_ref
  380.7 20.5 %all_to_all.77.parts_ref = bf16[8,128,256]{2,1,0:T(8,128)(2,1)S(1)} all-to-all(bf16[8,128,256]{2,1,0:T(8,128)(2,1)S(1)} %shard_map.114), channel_id=1, replica_groups=mesh['pipe'=8,'seq'=16,'tp'=2] {'pipe'}, dimensions={0} | all-to-all | bytes 1048576 | tf_op jit(solution)/shard_map/all_to_all | solution.py:486
  401.3 2.8 collective-permute-start.26
  407.6 3.6 collective-permute-done.27.far_ref
  413.2 15.6 %all_to_all.78.in_ref = bf16[16,48,128]{2,1,0:T(8,128)(2,1)S(1)} all-to-all(bf16[16,48,128]{2,1,0:T(8,128)(2,1)S(1)} %shard_map.118), channel_id=1, replica_groups=mesh['pipe'=8,'seq'=16,'tp'=2] {'seq'}, dimensions={0} | all-to-all | bytes 393216 | tf_op jit(solution)/shard_map/all_to_all | solution.py:528
  428.8 11.6 %all_to_all.79.sums_ref = bf16[16,48,128]{2,1,0:T(8,128)(2,1)S(1)} all-to-all(bf16[16,48,128]{2,1,0:T(8,128)(2,1)S(1)} %shard_map.119), channel_id=1, replica_groups=mesh['pipe'=8,'seq'=16,'tp'=2] {'seq'}, dimensions={0} | all-to-all | bytes 393216 | tf_op jit(solution)/shard_map/all_to_all | solution.py:532
  441.3 20.6 %all_to_all.80.in_ref = bf16[8,176,256]{2,1,0:T(8,128)(2,1)S(1)} all-to-all(bf16[8,176,256]{2,1,0:T(8,128)(2,1)S(1)} %shard_map.120), channel_id=1, replica_groups=mesh['pipe'=8,'seq'=16,'tp'=2] {'pipe'}, dimensions={0} | all-to-all | bytes 1441792 | tf_op jit(solution)/shard_map/all_to_all | solution.py:534
  (225 shorter events, 117.8 us)
Async XLA Ops:
  7.2 145.5 %all-gather.9.cloned.1.call-start = ((), (), s32[]{:S(2)}) async-start(), calls=%async_computation.14 | async-start | bytes 2228224 | tf_op jit(solution)/shard_map/all_gather | solution.py:365
  52.7 143.2 %all-gather.11.cloned.1.call-start = ((), (), s32[]{:S(2)}) async-start(), calls=%async_computation.15 | async-start | bytes 4456448 | tf_op jit(solution)/shard_map/all_gather | solution.py:365
  53.7 209.9 %all-gather.13.cloned.1.call-start = ((), (), s32[]{:S(2)}) async-start(), calls=%async_computation.16 | async-start | bytes 4456448 | tf_op jit(solution)/shard_map/all_gather | solution.py:365
  56.0 34.9 %all-to-all-start.1 = ((bf16[16,256,256]{2,1,0:T(8,128)(2,1)}), bf16[16,256,256]{2,1,0:T(8,128)(2,1)S(1)}, u32[]{:S(2)}, u32[]{:S(2)}) async-start(bf16[16,256,256]{2,1,0:T(8,128)(2,1)} %broadcast_in_dim.17), calls=%async_computation.1 | async-start | bytes 4194304 | tf_op jit(solution)/shard_map/all_to_all | solution.py:369
  63.5 273.5 %all-gather.15.cloned.1.call-start = ((), (), s32[]{:S(2)}) async-start(), calls=%async_computation.17 | async-start | bytes 4456448 | tf_op jit(solution)/shard_map/all_gather | solution.py:365
  64.0 2.3 collective-permute-start.1
  92.2 17.9 %all-to-all-start.2 = ((bf16[8,128,256]{2,1,0:T(8,128)(2,1)}), bf16[8,128,256]{2,1,0:T(8,128)(2,1)S(1)}, u32[]{:S(2)}, u32[]{:S(2)}) async-start(bf16[8,128,256]{2,1,0:T(8,128)(2,1)} %copy-done.40), calls=%async_computation.2 | async-start | bytes 1048576 | tf_op jit(solution)/shard_map/all_to_all | solution.py:372
  96.4 1.3 collective-permute-start
  110.0 24.2 %all-to-all-start.3 = ((bf16[8,128,256]{2,1,0:T(8,128)(2,1)}), bf16[8,128,256]{2,1,0:T(8,128)(2,1)}, u32[]{:S(2)}, u32[]{:S(2)}) async-start(bf16[8,128,256]{2,1,0:T(8,128)(2,1)} %shard_map.79), calls=%async_computation.3 | async-start | bytes 1048576 | tf_op jit(solution)/shard_map/all_to_all | solution.py:486
  114.2 17.0 %collective-permute-start.2 = (bf16[8,128,256]{2,1,0:T(8,128)(2,1)S(1)}, bf16[8,128,256]{2,1,0:T(8,128)(2,1)S(1)}, u32[]{:S(2)}, u32[]{:S(2)}) collective-permute-start(bf16[8,128,256]{2,1,0:T(8,128)(2,1)S(1)} %all-to-all-done.2.own_ref), channel_id=1, source_target_pairs={{0,2},{2,4},{4,6},{6,8},{8,10},{10,12},{12,14},{14,16},{16,18},{18... | collective-permute-start | bytes 1572872 | tf_op jit(solution)/shard_map/ppermute | solution.py:327
  116.7 11.4 %collective-permute-start.3 = (bf16[8,16,256]{2,1,0:T(8,128)(2,1)S(1)}, bf16[8,16,256]{2,1,0:T(8,128)(2,1)S(1)}, u32[]{:S(2)}, u32[]{:S(2)}) collective-permute-start(bf16[8,16,256]{2,1,0:T(8,128)(2,1)S(1)} %get-tuple-element.275), channel_id=1, source_target_pairs={{0,4},{2,6},{4,8},{6,10},{8,12},{10,14},{12,16},{14,18},{16,20},{1... | collective-permute-start | bytes 196616 | tf_op jit(solution)/shard_map/ppermute | solution.py:327
  123.5 7.7 %collective-permute-start.4 = (bf16[8,16,256]{2,1,0:T(8,128)(2,1)S(1)}, bf16[8,16,256]{2,1,0:T(8,128)(2,1)S(1)}, u32[]{:S(2)}, u32[]{:S(2)}) collective-permute-start(bf16[8,16,256]{2,1,0:T(8,128)(2,1)S(1)} %get-tuple-element.274), channel_id=1, source_target_pairs={{2,0},{4,2},{6,4},{8,6},{10,8},{12,10},{14,12},{16,14},{18,16},{20... | collective-permute-start | bytes 196616 | tf_op jit(solution)/shard_map/ppermute | solution.py:322
  136.9 12.7 %collective-permute-start.5 = (bf16[144,256]{1,0:T(8,128)(2,1)S(1)}, bf16[144,256]{1,0:T(8,128)(2,1)S(1)}, u32[]{:S(2)}, u32[]{:S(2)}) collective-permute-start(bf16[144,256]{1,0:T(8,128)(2,1)S(1)} %get-tuple-element.138.send_ref), channel_id=1, source_target_pairs={{2,0},{4,2},{6,4},{8,6},{10,8},{12,10},{14,12},{16,14},{18,16},{20... | collective-permute-start | bytes 221192 | tf_op jit(solution)/shard_map/ppermute | solution.py:322
  143.4 7.0 %collective-permute-start.6 = (bf16[16,256]{1,0:T(8,128)(2,1)S(1)}, bf16[16,256]{1,0:T(8,128)(2,1)S(1)}, u32[]{:S(2)}, u32[]{:S(2)}) collective-permute-start(bf16[16,256]{1,0:T(8,128)(2,1)S(1)} %get-tuple-element.145), channel_id=1, source_target_pairs={{4,0},{6,2},{8,4},{10,6},{12,8},{14,10},{16,12},{18,14},{20,16},{2... | collective-permute-start | bytes 24584 | tf_op jit(solution)/shard_map/ppermute | solution.py:322
  152.6 1.5 collective-permute-start.7
  182.2 8.8 %collective-permute-start.8 = (bf16[144,256]{1,0:T(8,128)(2,1)S(1)}, bf16[144,256]{1,0:T(8,128)(2,1)S(1)}, u32[]{:S(2)}, u32[]{:S(2)}) collective-permute-start(bf16[144,256]{1,0:T(8,128)(2,1)S(1)} %get-tuple-element.152.send_ref), channel_id=1, source_target_pairs={{2,0},{4,2},{6,4},{8,6},{10,8},{12,10},{14,12},{16,14},{18,16},{20... | collective-permute-start | bytes 221192 | tf_op jit(solution)/shard_map/ppermute | solution.py:322
  185.0 7.2 %collective-permute-start.9 = (bf16[16,256]{1,0:T(8,128)(2,1)S(1)}, bf16[16,256]{1,0:T(8,128)(2,1)S(1)}, u32[]{:S(2)}, u32[]{:S(2)}) collective-permute-start(bf16[16,256]{1,0:T(8,128)(2,1)S(1)} %get-tuple-element.160), channel_id=1, source_target_pairs={{4,0},{6,2},{8,4},{10,6},{12,8},{14,10},{16,12},{18,14},{20,16},{2... | collective-permute-start | bytes 24584 | tf_op jit(solution)/shard_map/ppermute | solution.py:322
  219.6 9.3 %collective-permute-start.11 = (bf16[144,256]{1,0:T(8,128)(2,1)S(1)}, bf16[144,256]{1,0:T(8,128)(2,1)S(1)}, u32[]{:S(2)}, u32[]{:S(2)}) collective-permute-start(bf16[144,256]{1,0:T(8,128)(2,1)S(1)} %get-tuple-element.167.send_ref), channel_id=1, source_target_pairs={{2,0},{4,2},{6,4},{8,6},{10,8},{12,10},{14,12},{16,14},{18,16},{20... | collective-permute-start | bytes 221192 | tf_op jit(solution)/shard_map/ppermute | solution.py:322
  223.3 7.2 %collective-permute-start.12 = (bf16[16,256]{1,0:T(8,128)(2,1)S(1)}, bf16[16,256]{1,0:T(8,128)(2,1)S(1)}, u32[]{:S(2)}, u32[]{:S(2)}) collective-permute-start(bf16[16,256]{1,0:T(8,128)(2,1)S(1)} %get-tuple-element.176), channel_id=1, source_target_pairs={{4,0},{6,2},{8,4},{10,6},{12,8},{14,10},{16,12},{18,14},{20,16},{2... | collective-permute-start | bytes 24584 | tf_op jit(solution)/shard_map/ppermute | solution.py:322
  231.3 1.3 collective-permute-start.13
  254.1 9.6 %collective-permute-start.14 = (bf16[144,256]{1,0:T(8,128)(2,1)S(1)}, bf16[144,256]{1,0:T(8,128)(2,1)S(1)}, u32[]{:S(2)}, u32[]{:S(2)}) collective-permute-start(bf16[144,256]{1,0:T(8,128)(2,1)S(1)} %get-tuple-element.183.send_ref), channel_id=1, source_target_pairs={{2,0},{4,2},{6,4},{8,6},{10,8},{12,10},{14,12},{16,14},{18,16},{20... | collective-permute-start | bytes 221192 | tf_op jit(solution)/shard_map/ppermute | solution.py:322
  257.1 7.0 %collective-permute-start.15 = (bf16[16,256]{1,0:T(8,128)(2,1)S(1)}, bf16[16,256]{1,0:T(8,128)(2,1)S(1)}, u32[]{:S(2)}, u32[]{:S(2)}) collective-permute-start(bf16[16,256]{1,0:T(8,128)(2,1)S(1)} %get-tuple-element.193), channel_id=1, source_target_pairs={{4,0},{6,2},{8,4},{10,6},{12,8},{14,10},{16,12},{18,14},{20,16},{2... | collective-permute-start | bytes 24584 | tf_op jit(solution)/shard_map/ppermute | solution.py:322
  267.1 1.3 collective-permute-start.16
  292.2 9.8 %collective-permute-start.17 = (bf16[144,256]{1,0:T(8,128)(2,1)S(1)}, bf16[144,256]{1,0:T(8,128)(2,1)S(1)}, u32[]{:S(2)}, u32[]{:S(2)}) collective-permute-start(bf16[144,256]{1,0:T(8,128)(2,1)S(1)} %get-tuple-element.201.send_ref), channel_id=1, source_target_pairs={{2,0},{4,2},{6,4},{8,6},{10,8},{12,10},{14,12},{16,14},{18,16},{20... | collective-permute-start | bytes 221192 | tf_op jit(solution)/shard_map/ppermute | solution.py:322
  296.2 7.0 %collective-permute-start.18 = (bf16[16,256]{1,0:T(8,128)(2,1)S(1)}, bf16[16,256]{1,0:T(8,128)(2,1)S(1)}, u32[]{:S(2)}, u32[]{:S(2)}) collective-permute-start(bf16[16,256]{1,0:T(8,128)(2,1)S(1)} %get-tuple-element.210), channel_id=1, source_target_pairs={{4,0},{6,2},{8,4},{10,6},{12,8},{14,10},{16,12},{18,14},{20,16},{2... | collective-permute-start | bytes 24584 | tf_op jit(solution)/shard_map/ppermute | solution.py:322
  304.1 1.3 collective-permute-start.19
  327.5 8.8 %collective-permute-start.20 = (bf16[144,256]{1,0:T(8,128)(2,1)S(1)}, bf16[144,256]{1,0:T(8,128)(2,1)S(1)}, u32[]{:S(2)}, u32[]{:S(2)}) collective-permute-start(bf16[144,256]{1,0:T(8,128)(2,1)S(1)} %get-tuple-element.217.send_ref), channel_id=1, source_target_pairs={{2,0},{4,2},{6,4},{8,6},{10,8},{12,10},{14,12},{16,14},{18,16},{20... | collective-permute-start | bytes 221192 | tf_op jit(solution)/shard_map/ppermute | solution.py:322
  330.3 7.0 %collective-permute-start.21 = (bf16[16,256]{1,0:T(8,128)(2,1)S(1)}, bf16[16,256]{1,0:T(8,128)(2,1)S(1)}, u32[]{:S(2)}, u32[]{:S(2)}) collective-permute-start(bf16[16,256]{1,0:T(8,128)(2,1)S(1)} %get-tuple-element.227), channel_id=1, source_target_pairs={{4,0},{6,2},{8,4},{10,6},{12,8},{14,10},{16,12},{18,14},{20,16},{2... | collective-permute-start | bytes 24584 | tf_op jit(solution)/shard_map/ppermute | solution.py:322
  367.2 8.2 %collective-permute-start.23 = (bf16[144,256]{1,0:T(8,128)(2,1)S(1)}, bf16[144,256]{1,0:T(8,128)(2,1)S(1)}, u32[]{:S(2)}, u32[]{:S(2)}) collective-permute-start(bf16[144,256]{1,0:T(8,128)(2,1)S(1)} %get-tuple-element.235.send_ref), channel_id=1, source_target_pairs={{2,0},{4,2},{6,4},{8,6},{10,8},{12,10},{14,12},{16,14},{18,16},{20... | collective-permute-start | bytes 221192 | tf_op jit(solution)/shard_map/ppermute | solution.py:322
  370.7 7.0 %collective-permute-start.24 = (bf16[16,256]{1,0:T(8,128)(2,1)S(1)}, bf16[16,256]{1,0:T(8,128)(2,1)S(1)}, u32[]{:S(2)}, u32[]{:S(2)}) collective-permute-start(bf16[16,256]{1,0:T(8,128)(2,1)S(1)} %get-tuple-element.244), channel_id=1, source_target_pairs={{4,0},{6,2},{8,4},{10,6},{12,8},{14,10},{16,12},{18,14},{20,16},{2... | collective-permute-start | bytes 24584 | tf_op jit(solution)/shard_map/ppermute | solution.py:322
  401.3 6.2 %collective-permute-start.26 = (bf16[144,256]{1,0:T(8,128)(2,1)S(1)}, bf16[144,256]{1,0:T(8,128)(2,1)S(1)}, u32[]{:S(2)}, u32[]{:S(2)}) collective-permute-start(bf16[144,256]{1,0:T(8,128)(2,1)S(1)} %get-tuple-element.250.send_ref), channel_id=1, source_target_pairs={{2,0},{4,2},{6,4},{8,6},{10,8},{12,10},{14,12},{16,14},{18,16},{20... | collective-permute-start | bytes 221192 | tf_op jit(solution)/shard_map/ppermute | solution.py:322
  404.1 7.0 %collective-permute-start.27 = (bf16[16,256]{1,0:T(8,128)(2,1)S(1)}, bf16[16,256]{1,0:T(8,128)(2,1)S(1)}, u32[]{:S(2)}, u32[]{:S(2)}) collective-permute-start(bf16[16,256]{1,0:T(8,128)(2,1)S(1)} %get-tuple-element.255), channel_id=1, source_target_pairs={{4,0},{6,2},{8,4},{10,6},{12,8},{14,10},{16,12},{18,14},{20,16},{2... | collective-permute-start | bytes 24584 | tf_op jit(solution)/shard_map/ppermute | solution.py:322
  (62 other events, 368.2 us)
Sparse Core Ops, SparseCore 0:
  52.8 60.6 all-gather.8
  116.0 56.4 all-gather.10
  175.0 56.7 all-gather.12
  234.1 58.0 all-gather.14

commit v5 on v2

--- a/solution.py
+++ b/solution.py
@@ -400,11 +400,6 @@
         pieces = lax.all_gather(source[first : last + 1, tokens : tokens + depth], "seq", axis=0)
         return pieces.reshape(blocks, last + 1 - first, planes, width, owned)
 
-    def copied(p):
-        copies = jnp.broadcast_to(packed[p, tokens : tokens + depth][None], (blocks, depth, owned))
-        pieces = lax.all_to_all(copies, "seq", 0, 0, tiled=True)
-        return pieces.reshape(blocks, 1, planes, width, owned)
-
     starts = call(
         functools.partial(shuffle_body, planes, width),
         shape((planes, tokens, owned), BF),
@@ -414,19 +409,24 @@
     swap = [(0, 1), (1, 0)]
     other = lax.ppermute(grad, "tp", swap)
 
-    before = {top: (from_before(packed[top:, :tokens], 1), 0)}
-    saved = {top: recomputed(top, *before[top])}
-    first_weights, saved[top], source, grad, other = lax.optimization_barrier(
-        (copied(top), saved[top], packed, grad, other)
-    )
+    copies = jnp.broadcast_to(packed[top, tokens : tokens + depth][None], (blocks, depth, owned))
+    copies, later = lax.optimization_barrier((copies, packed))
+    pieces = lax.all_to_all(copies, "seq", 0, 0, tiled=True)
+    first_weights = pieces.reshape(blocks, 1, planes, width, owned)
+    nearest = from_before(packed[top:, :tokens], 1)
+    first_weights, nearest, before2, after, source, grad, other = lax.optimization_barrier(
+        (first_weights, nearest, before2, after, packed, grad, other)
+    )
+    before = {top: (nearest, 0)}
     others = from_before(source[:top, :tokens], 1)
     before.update({p: (others, p) for p in range(top)})
+    saved = {top: recomputed(top, *before[top])}
     weights = {top: (first_weights, 0)}
     last = planes - 2
     for size in (1, 2, 2, planes):
         first = max(0, last - size + 1)
         if last >= first:
-            group = gathered(packed, first, last)
+            group = gathered(later, first, last)
             weights.update({p: (group, p - first) for p in range(first, last + 1)})
         last = first - 1
 

time: 472 us -> 480 us (1.017)
  waiting for transfers between devices: 60.1 us -> 66.5 us
    all_gather x4, waiting for transfers between devices: 6.04 us -> 13.4 us  [gathered(): lax.all_gather(source[first:last + 1, tokens:tokens + depth], 'seq', axis=0)]
    unnamed x100 -> x108, local copies, waits for them, and re-layouts: 21.5 us -> 22.3 us
  transfers between devices with their start and end apart: 35 -> 35, of which waited for: 21 -> 22; matrix products, arithmetic and copies ran while one was open for 1% -> 1% of each run, Pallas kernels for 7% -> 7%
where the time goes in v5:
time: 480 us; the launch traced here: 471 us
  blocking collectives  245 us (51%)
  starting transfers between devices  74.5 us (16%)
  waiting for transfers between devices  66.5 us (14%)
  Pallas kernels  43.4 us (9%)
  local copies, waits for them, and re-layouts  26.3 us (5%)
  between operations  15.2 us (3%)
    all_to_all x7, blocking collectives, per_device(): parts = lax.all_to_all(partial, 'pipe', 0, 0, tiled=True)  147 us
    all_to_all x1, blocking collectives, per_device(): packed = lax.all_to_all(packed, 'pipe', 0, 0, tiled=True)  52.7 us
    ppermute x17, starting transfers between devices, from_next(): return lax.ppermute(x, 'seq', [(i, i - by) for i in range(by, size)])  51.7 us
    pallas_call x36, Pallas kernels, call(): pl.pallas_call(body, out_shape=out_shape, compiler_params=pltpu.CompilerP...  32.3 us
    unnamed x108, local copies, waits for them, and re-layouts  22.3 us
    all_to_all x1, blocking collectives, per_device(): results = lax.all_to_all(merged, 'pipe', 0, 0, tiled=True)  20.6 us
    ppermute x17, waiting for transfers between devices, from_next(): return lax.ppermute(x, 'seq', [(i, i - by) for i in range(by, size)])  17.3 us
    ppermute x3, waiting for transfers between devices, from_before(): return lax.ppermute(x, 'seq', [(i, i + by) for i in range(size - by)])  17 us
  transfers between devices with their start and end apart: 35, of which 22 were waited for; matrix products, arithmetic and copies ran while one was open for 1% of the time, Pallas kernels for 7%

profile of v5, /device:TPU:2, one launch (start us, length us, event | category | flops | bytes accessed | tf_op | source)
XLA Modules:
  0.0 471.0 jit_solution(11011202571150976389)
XLA Ops:
  13.8 52.7 %all_to_all.65.own_ref.aux_ref = bf16[8,432,256]{2,1,0:T(8,128)(2,1)S(1)} all-to-all(bf16[8,432,256]{2,1,0:T(8,128)(2,1)S(1)} %shard_map.76), channel_id=1, replica_groups=mesh['pipe'=8,'seq'=16,'tp'=2] {'pipe'}, dimensions={0} | all-to-all | bytes 3538944 | tf_op jit(solution)/shard_map/all_to_all | solution.py:356
  70.5 7.6 %all-to-all-start.1 = ((bf16[16,256,256]{2,1,0:T(8,128)(2,1)}), bf16[16,256,256]{2,1,0:T(8,128)(2,1)}, u32[]{:S(2)}, u32[]{:S(2)}) async-start(bf16[16,256,256]{2,1,0:T(8,128)(2,1)} %broadcast_in_dim.17), calls=%async_computation.1 | async-start | bytes 4194304 | tf_op jit(solution)/shard_map/all_to_all | solution.py:414
  79.4 3.4 collective-permute-start.1
  82.8 4.6 collective-permute-start.2
  87.4 4.3 collective-permute-start.3
  91.7 16.6 %collective-permute-done.1.prev_ref = bf16[1,128,256]{2,1,0:T(8,128)(2,1)S(1)} collective-permute-done((bf16[1,128,256]{2,1,0:T(8,128)(2,1)S(1)}, bf16[1,128,256]{2,1,0:T(8,128)(2,1)S(1)}, u32[]{:S(2)}, u32[]{:S(2)}) %collective-permute-start.1) | collective-permute-done | bytes 65568 | tf_op jit(solution)/shard_map/ppermute | solution.py:323
  108.7 2.6 shard_map.78
  111.3 4.2 all-to-all-start.2
  122.0 8.1 %all-to-all-done.2.parts_ref = bf16[8,128,256]{2,1,0:T(8,128)(2,1)} async-done(((bf16[8,128,256]{2,1,0:T(8,128)(2,1)}), bf16[8,128,256]{2,1,0:T(8,128)(2,1)}, u32[]{:S(2)}, u32[]{:S(2)}) %all-to-all-start.2) | async-done | bytes 524320 | tf_op jit(solution)/shard_map/all_to_all | solution.py:485
  132.2 5.1 %collective-permute-start.6 = (bf16[144,256]{1,0:T(8,128)(2,1)S(1)}, bf16[144,256]{1,0:T(8,128)(2,1)S(1)}, u32[]{:S(2)}, u32[]{:S(2)}) collective-permute-start(bf16[144,256]{1,0:T(8,128)(2,1)S(1)} %get-tuple-element.144.send_ref), channel_id=1, source_target_pairs={{2,0},{4,2},{6,4},{8,6},{10,8},{12,10},{14,12},{16,14},{18,16},{20... | collective-permute-start | bytes 221192 | tf_op jit(solution)/shard_map/ppermute | solution.py:318
  142.1 2.5 collective-permute-done.7.far_ref
  150.7 20.6 %all_to_all.66.parts_ref = bf16[8,128,256]{2,1,0:T(8,128)(2,1)S(1)} all-to-all(bf16[8,128,256]{2,1,0:T(8,128)(2,1)S(1)} %shard_map.83), channel_id=1, replica_groups=mesh['pipe'=8,'seq'=16,'tp'=2] {'pipe'}, dimensions={0} | all-to-all | bytes 1048576 | tf_op jit(solution)/shard_map/all_to_all | solution.py:485
  171.4 3.0 collective-permute-start.9
  184.4 13.4 %all-gather.11.cloned.1.call-done = bf16[32,256,256]{2,1,0:T(8,128)(2,1)} async-done(((bf16[2,256,256]{2,1,0:T(8,128)(2,1)}), bf16[32,256,256]{2,1,0:T(8,128)(2,1)}) %all-gather.11.cloned.1.call-update) | async-done | bytes 4194320 | tf_op jit(solution)/shard_map/all_gather | solution.py:400
  200.8 24.2 %all_to_all.67.parts_ref = bf16[8,128,256]{2,1,0:T(8,128)(2,1)S(1)} all-to-all(bf16[8,128,256]{2,1,0:T(8,128)(2,1)S(1)} %shard_map.88), channel_id=1, replica_groups=mesh['pipe'=8,'seq'=16,'tp'=2] {'pipe'}, dimensions={0} | all-to-all | bytes 1048576 | tf_op jit(solution)/shard_map/all_to_all | solution.py:485
  225.2 4.6 collective-permute-start.12
  229.7 2.7 collective-permute-start.13
  239.8 20.5 %all_to_all.68.parts_ref = bf16[8,128,256]{2,1,0:T(8,128)(2,1)S(1)} all-to-all(bf16[8,128,256]{2,1,0:T(8,128)(2,1)S(1)} %shard_map.93), channel_id=1, replica_groups=mesh['pipe'=8,'seq'=16,'tp'=2] {'pipe'}, dimensions={0} | all-to-all | bytes 1048576 | tf_op jit(solution)/shard_map/all_to_all | solution.py:485
  260.4 3.7 collective-permute-start.15
  277.8 20.5 %all_to_all.69.parts_ref = bf16[8,128,256]{2,1,0:T(8,128)(2,1)S(1)} all-to-all(bf16[8,128,256]{2,1,0:T(8,128)(2,1)S(1)} %shard_map.98), channel_id=1, replica_groups=mesh['pipe'=8,'seq'=16,'tp'=2] {'pipe'}, dimensions={0} | all-to-all | bytes 1048576 | tf_op jit(solution)/shard_map/all_to_all | solution.py:485
  298.4 3.3 collective-permute-start.18
  311.9 20.5 %all_to_all.70.parts_ref = bf16[8,128,256]{2,1,0:T(8,128)(2,1)S(1)} all-to-all(bf16[8,128,256]{2,1,0:T(8,128)(2,1)S(1)} %shard_map.103), channel_id=1, replica_groups=mesh['pipe'=8,'seq'=16,'tp'=2] {'pipe'}, dimensions={0} | all-to-all | bytes 1048576 | tf_op jit(solution)/shard_map/all_to_all | solution.py:485
  332.5 3.1 collective-permute-start.21
  335.7 2.7 collective-permute-start.22
  349.4 20.5 %all_to_all.71.parts_ref = bf16[8,128,256]{2,1,0:T(8,128)(2,1)S(1)} all-to-all(bf16[8,128,256]{2,1,0:T(8,128)(2,1)S(1)} %shard_map.108), channel_id=1, replica_groups=mesh['pipe'=8,'seq'=16,'tp'=2] {'pipe'}, dimensions={0} | all-to-all | bytes 1048576 | tf_op jit(solution)/shard_map/all_to_all | solution.py:485
  370.0 3.9 collective-permute-start.24
  384.0 20.5 %all_to_all.72.parts_ref = bf16[8,128,256]{2,1,0:T(8,128)(2,1)S(1)} all-to-all(bf16[8,128,256]{2,1,0:T(8,128)(2,1)S(1)} %shard_map.113), channel_id=1, replica_groups=mesh['pipe'=8,'seq'=16,'tp'=2] {'pipe'}, dimensions={0} | all-to-all | bytes 1048576 | tf_op jit(solution)/shard_map/all_to_all | solution.py:485
  404.6 2.8 collective-permute-start.27
  410.8 3.6 collective-permute-done.28.far_ref
  416.4 12.9 %all_to_all.73.in_ref = bf16[16,48,128]{2,1,0:T(8,128)(2,1)S(1)} all-to-all(bf16[16,48,128]{2,1,0:T(8,128)(2,1)S(1)} %shard_map.117), channel_id=1, replica_groups=mesh['pipe'=8,'seq'=16,'tp'=2] {'seq'}, dimensions={0} | all-to-all | bytes 393216 | tf_op jit(solution)/shard_map/all_to_all | solution.py:523
  429.3 11.6 %all_to_all.74.sums_ref = bf16[16,48,128]{2,1,0:T(8,128)(2,1)S(1)} all-to-all(bf16[16,48,128]{2,1,0:T(8,128)(2,1)S(1)} %shard_map.118), channel_id=1, replica_groups=mesh['pipe'=8,'seq'=16,'tp'=2] {'seq'}, dimensions={0} | all-to-all | bytes 393216 | tf_op jit(solution)/shard_map/all_to_all | solution.py:527
  441.0 20.6 %all_to_all.75.in_ref = bf16[8,176,256]{2,1,0:T(8,128)(2,1)S(1)} all-to-all(bf16[8,176,256]{2,1,0:T(8,128)(2,1)S(1)} %shard_map.119), channel_id=1, replica_groups=mesh['pipe'=8,'seq'=16,'tp'=2] {'pipe'}, dimensions={0} | all-to-all | bytes 1441792 | tf_op jit(solution)/shard_map/all_to_all | solution.py:529
  (215 shorter events, 104.8 us)
Async XLA Ops:
  7.2 140.3 %all-gather.9.cloned.1.call-start = ((), (), s32[]{:S(2)}) async-start(), calls=%async_computation.13 | async-start | bytes 2228224 | tf_op jit(solution)/shard_map/all_gather | solution.py:400
  7.2 2.2 collective-permute-start
  68.8 129.1 %all-gather.11.cloned.1.call-start = ((), (), s32[]{:S(2)}) async-start(), calls=%async_computation.14 | async-start | bytes 4456448 | tf_op jit(solution)/shard_map/all_gather | solution.py:400
  69.8 202.9 %all-gather.13.cloned.1.call-start = ((), (), s32[]{:S(2)}) async-start(), calls=%async_computation.15 | async-start | bytes 4456448 | tf_op jit(solution)/shard_map/all_gather | solution.py:400
  70.5 38.2 %all-to-all-start.1 = ((bf16[16,256,256]{2,1,0:T(8,128)(2,1)}), bf16[16,256,256]{2,1,0:T(8,128)(2,1)}, u32[]{:S(2)}, u32[]{:S(2)}) async-start(bf16[16,256,256]{2,1,0:T(8,128)(2,1)} %broadcast_in_dim.17), calls=%async_computation.1 | async-start | bytes 4194304 | tf_op jit(solution)/shard_map/all_to_all | solution.py:414
  78.1 266.2 %all-gather.15.cloned.1.call-start = ((), (), s32[]{:S(2)}) async-start(), calls=%async_computation.16 | async-start | bytes 4456448 | tf_op jit(solution)/shard_map/all_gather | solution.py:400
  79.3 12.4 %collective-permute-start.4 = (bf16[128,256]{1,0:T(8,128)(2,1)S(1)}, bf16[128,256]{1,0:T(8,128)(2,1)S(1)}, u32[]{:S(2)}, u32[]{:S(2)}) collective-permute-start(bf16[128,256]{1,0:T(8,128)(2,1)S(1)} %dynamic-slice_bitcast_fusion.own_ref.grad_ref), channel_id=1, source_target_pairs={{0,1},{1,0},{2,3},{3,2},{4,5},{5,4},{6,7},{7,6},{8,9},{9,8},{10,11... | collective-permute-start | bytes 196616 | tf_op jit(solution)/shard_map/ppermute | solution.py:410
  79.4 28.9 %collective-permute-start.1 = (bf16[1,128,256]{2,1,0:T(8,128)(2,1)S(1)}, bf16[1,128,256]{2,1,0:T(8,128)(2,1)S(1)}, u32[]{:S(2)}, u32[]{:S(2)}) collective-permute-start(bf16[1,128,256]{2,1,0:T(8,128)(2,1)S(1)} %slice.41), channel_id=1, source_target_pairs={{0,2},{2,4},{4,6},{6,8},{8,10},{10,12},{12,14},{14,16},{16,18},{18... | collective-permute-start | bytes 196616 | tf_op jit(solution)/shard_map/ppermute | solution.py:323
  82.8 25.9 %collective-permute-start.2 = (bf16[8,16,256]{2,1,0:T(8,128)(2,1)S(1)}, bf16[8,16,256]{2,1,0:T(8,128)(2,1)S(1)}, u32[]{:S(2)}, u32[]{:S(2)}) collective-permute-start(bf16[8,16,256]{2,1,0:T(8,128)(2,1)S(1)} %get-tuple-element.275), channel_id=1, source_target_pairs={{0,4},{2,6},{4,8},{6,10},{8,12},{10,14},{12,16},{14,18},{16,20},{1... | collective-permute-start | bytes 196616 | tf_op jit(solution)/shard_map/ppermute | solution.py:323
  87.4 21.3 %collective-permute-start.3 = (bf16[8,16,256]{2,1,0:T(8,128)(2,1)S(1)}, bf16[8,16,256]{2,1,0:T(8,128)(2,1)S(1)}, u32[]{:S(2)}, u32[]{:S(2)}) collective-permute-start(bf16[8,16,256]{2,1,0:T(8,128)(2,1)S(1)} %get-tuple-element.274), channel_id=1, source_target_pairs={{2,0},{4,2},{6,4},{8,6},{10,8},{12,10},{14,12},{16,14},{18,16},{20... | collective-permute-start | bytes 196616 | tf_op jit(solution)/shard_map/ppermute | solution.py:318
  111.3 18.8 %all-to-all-start.2 = ((bf16[8,128,256]{2,1,0:T(8,128)(2,1)}), bf16[8,128,256]{2,1,0:T(8,128)(2,1)}, u32[]{:S(2)}, u32[]{:S(2)}) async-start(bf16[8,128,256]{2,1,0:T(8,128)(2,1)} %shard_map.78), calls=%async_computation.2 | async-start | bytes 1048576 | tf_op jit(solution)/shard_map/all_to_all | solution.py:485
  116.3 23.2 %collective-permute-start.5 = (bf16[7,128,256]{2,1,0:T(8,128)(2,1)}, bf16[7,128,256]{2,1,0:T(8,128)(2,1)S(1)}, u32[]{:S(2)}, u32[]{:S(2)}) collective-permute-start(bf16[7,128,256]{2,1,0:T(8,128)(2,1)} %slice.34), channel_id=1, source_target_pairs={{0,2},{2,4},{4,6},{6,8},{8,10},{10,12},{12,14},{14,16},{16,18},{18... | collective-permute-start | bytes 1376264 | tf_op jit(solution)/shard_map/ppermute | solution.py:323
  132.2 9.9 %collective-permute-start.6 = (bf16[144,256]{1,0:T(8,128)(2,1)S(1)}, bf16[144,256]{1,0:T(8,128)(2,1)S(1)}, u32[]{:S(2)}, u32[]{:S(2)}) collective-permute-start(bf16[144,256]{1,0:T(8,128)(2,1)S(1)} %get-tuple-element.144.send_ref), channel_id=1, source_target_pairs={{2,0},{4,2},{6,4},{8,6},{10,8},{12,10},{14,12},{16,14},{18,16},{20... | collective-permute-start | bytes 221192 | tf_op jit(solution)/shard_map/ppermute | solution.py:318
  137.4 7.2 %collective-permute-start.7 = (bf16[16,256]{1,0:T(8,128)(2,1)S(1)}, bf16[16,256]{1,0:T(8,128)(2,1)S(1)}, u32[]{:S(2)}, u32[]{:S(2)}) collective-permute-start(bf16[16,256]{1,0:T(8,128)(2,1)S(1)} %get-tuple-element.150), channel_id=1, source_target_pairs={{4,0},{6,2},{8,4},{10,6},{12,8},{14,10},{16,12},{18,14},{20,16},{2... | collective-permute-start | bytes 24584 | tf_op jit(solution)/shard_map/ppermute | solution.py:318
  171.4 9.2 %collective-permute-start.9 = (bf16[144,256]{1,0:T(8,128)(2,1)S(1)}, bf16[144,256]{1,0:T(8,128)(2,1)S(1)}, u32[]{:S(2)}, u32[]{:S(2)}) collective-permute-start(bf16[144,256]{1,0:T(8,128)(2,1)S(1)} %get-tuple-element.158.send_ref), channel_id=1, source_target_pairs={{2,0},{4,2},{6,4},{8,6},{10,8},{12,10},{14,12},{16,14},{18,16},{20... | collective-permute-start | bytes 221192 | tf_op jit(solution)/shard_map/ppermute | solution.py:318
  174.4 7.2 %collective-permute-start.10 = (bf16[16,256]{1,0:T(8,128)(2,1)S(1)}, bf16[16,256]{1,0:T(8,128)(2,1)S(1)}, u32[]{:S(2)}, u32[]{:S(2)}) collective-permute-start(bf16[16,256]{1,0:T(8,128)(2,1)S(1)} %get-tuple-element.166), channel_id=1, source_target_pairs={{4,0},{6,2},{8,4},{10,6},{12,8},{14,10},{16,12},{18,14},{20,16},{2... | collective-permute-start | bytes 24584 | tf_op jit(solution)/shard_map/ppermute | solution.py:318
  225.2 10.1 %collective-permute-start.12 = (bf16[144,256]{1,0:T(8,128)(2,1)S(1)}, bf16[144,256]{1,0:T(8,128)(2,1)S(1)}, u32[]{:S(2)}, u32[]{:S(2)}) collective-permute-start(bf16[144,256]{1,0:T(8,128)(2,1)S(1)} %get-tuple-element.173.send_ref), channel_id=1, source_target_pairs={{2,0},{4,2},{6,4},{8,6},{10,8},{12,10},{14,12},{16,14},{18,16},{20... | collective-permute-start | bytes 221192 | tf_op jit(solution)/shard_map/ppermute | solution.py:318
  229.7 7.0 %collective-permute-start.13 = (bf16[16,256]{1,0:T(8,128)(2,1)S(1)}, bf16[16,256]{1,0:T(8,128)(2,1)S(1)}, u32[]{:S(2)}, u32[]{:S(2)}) collective-permute-start(bf16[16,256]{1,0:T(8,128)(2,1)S(1)} %get-tuple-element.182), channel_id=1, source_target_pairs={{4,0},{6,2},{8,4},{10,6},{12,8},{14,10},{16,12},{18,14},{20,16},{2... | collective-permute-start | bytes 24584 | tf_op jit(solution)/shard_map/ppermute | solution.py:318
  237.6 1.3 collective-permute-start.14
  260.4 8.5 %collective-permute-start.15 = (bf16[144,256]{1,0:T(8,128)(2,1)S(1)}, bf16[144,256]{1,0:T(8,128)(2,1)S(1)}, u32[]{:S(2)}, u32[]{:S(2)}) collective-permute-start(bf16[144,256]{1,0:T(8,128)(2,1)S(1)} %get-tuple-element.189.send_ref), channel_id=1, source_target_pairs={{2,0},{4,2},{6,4},{8,6},{10,8},{12,10},{14,12},{16,14},{18,16},{20... | collective-permute-start | bytes 221192 | tf_op jit(solution)/shard_map/ppermute | solution.py:318
  264.0 7.0 %collective-permute-start.16 = (bf16[16,256]{1,0:T(8,128)(2,1)S(1)}, bf16[16,256]{1,0:T(8,128)(2,1)S(1)}, u32[]{:S(2)}, u32[]{:S(2)}) collective-permute-start(bf16[16,256]{1,0:T(8,128)(2,1)S(1)} %get-tuple-element.198), channel_id=1, source_target_pairs={{4,0},{6,2},{8,4},{10,6},{12,8},{14,10},{16,12},{18,14},{20,16},{2... | collective-permute-start | bytes 24584 | tf_op jit(solution)/shard_map/ppermute | solution.py:318
  272.6 1.4 collective-permute-start.17
  298.4 8.4 %collective-permute-start.18 = (bf16[144,256]{1,0:T(8,128)(2,1)S(1)}, bf16[144,256]{1,0:T(8,128)(2,1)S(1)}, u32[]{:S(2)}, u32[]{:S(2)}) collective-permute-start(bf16[144,256]{1,0:T(8,128)(2,1)S(1)} %get-tuple-element.205.send_ref), channel_id=1, source_target_pairs={{2,0},{4,2},{6,4},{8,6},{10,8},{12,10},{14,12},{16,14},{18,16},{20... | collective-permute-start | bytes 221192 | tf_op jit(solution)/shard_map/ppermute | solution.py:318
  301.7 7.2 %collective-permute-start.19 = (bf16[16,256]{1,0:T(8,128)(2,1)S(1)}, bf16[16,256]{1,0:T(8,128)(2,1)S(1)}, u32[]{:S(2)}, u32[]{:S(2)}) collective-permute-start(bf16[16,256]{1,0:T(8,128)(2,1)S(1)} %get-tuple-element.214), channel_id=1, source_target_pairs={{4,0},{6,2},{8,4},{10,6},{12,8},{14,10},{16,12},{18,14},{20,16},{2... | collective-permute-start | bytes 24584 | tf_op jit(solution)/shard_map/ppermute | solution.py:318
  309.7 1.3 collective-permute-start.20
  332.5 8.7 %collective-permute-start.21 = (bf16[144,256]{1,0:T(8,128)(2,1)S(1)}, bf16[144,256]{1,0:T(8,128)(2,1)S(1)}, u32[]{:S(2)}, u32[]{:S(2)}) collective-permute-start(bf16[144,256]{1,0:T(8,128)(2,1)S(1)} %get-tuple-element.221.send_ref), channel_id=1, source_target_pairs={{2,0},{4,2},{6,4},{8,6},{10,8},{12,10},{14,12},{16,14},{18,16},{20... | collective-permute-start | bytes 221192 | tf_op jit(solution)/shard_map/ppermute | solution.py:318
  335.7 7.0 %collective-permute-start.22 = (bf16[16,256]{1,0:T(8,128)(2,1)S(1)}, bf16[16,256]{1,0:T(8,128)(2,1)S(1)}, u32[]{:S(2)}, u32[]{:S(2)}) collective-permute-start(bf16[16,256]{1,0:T(8,128)(2,1)S(1)} %get-tuple-element.230), channel_id=1, source_target_pairs={{4,0},{6,2},{8,4},{10,6},{12,8},{14,10},{16,12},{18,14},{20,16},{2... | collective-permute-start | bytes 24584 | tf_op jit(solution)/shard_map/ppermute | solution.py:318
  344.3 1.4 collective-permute-start.23
  370.0 8.7 %collective-permute-start.24 = (bf16[144,256]{1,0:T(8,128)(2,1)S(1)}, bf16[144,256]{1,0:T(8,128)(2,1)S(1)}, u32[]{:S(2)}, u32[]{:S(2)}) collective-permute-start(bf16[144,256]{1,0:T(8,128)(2,1)S(1)} %get-tuple-element.237.send_ref), channel_id=1, source_target_pairs={{2,0},{4,2},{6,4},{8,6},{10,8},{12,10},{14,12},{16,14},{18,16},{20... | collective-permute-start | bytes 221192 | tf_op jit(solution)/shard_map/ppermute | solution.py:318
  374.0 7.0 %collective-permute-start.25 = (bf16[16,256]{1,0:T(8,128)(2,1)S(1)}, bf16[16,256]{1,0:T(8,128)(2,1)S(1)}, u32[]{:S(2)}, u32[]{:S(2)}) collective-permute-start(bf16[16,256]{1,0:T(8,128)(2,1)S(1)} %get-tuple-element.246), channel_id=1, source_target_pairs={{4,0},{6,2},{8,4},{10,6},{12,8},{14,10},{16,12},{18,14},{20,16},{2... | collective-permute-start | bytes 24584 | tf_op jit(solution)/shard_map/ppermute | solution.py:318
  404.6 6.2 %collective-permute-start.27 = (bf16[144,256]{1,0:T(8,128)(2,1)S(1)}, bf16[144,256]{1,0:T(8,128)(2,1)S(1)}, u32[]{:S(2)}, u32[]{:S(2)}) collective-permute-start(bf16[144,256]{1,0:T(8,128)(2,1)S(1)} %get-tuple-element.252.send_ref), channel_id=1, source_target_pairs={{2,0},{4,2},{6,4},{8,6},{10,8},{12,10},{14,12},{16,14},{18,16},{20... | collective-permute-start | bytes 221192 | tf_op jit(solution)/shard_map/ppermute | solution.py:318
  407.4 7.0 %collective-permute-start.28 = (bf16[16,256]{1,0:T(8,128)(2,1)S(1)}, bf16[16,256]{1,0:T(8,128)(2,1)S(1)}, u32[]{:S(2)}, u32[]{:S(2)}) collective-permute-start(bf16[16,256]{1,0:T(8,128)(2,1)S(1)} %get-tuple-element.257), channel_id=1, source_target_pairs={{4,0},{6,2},{8,4},{10,6},{12,8},{14,10},{16,12},{18,14},{20,16},{2... | collective-permute-start | bytes 24584 | tf_op jit(solution)/shard_map/ppermute | solution.py:318
  (56 other events, 412.6 us)
Sparse Core Ops, SparseCore 0:
  68.9 68.1 all-gather.8
  139.5 58.2 all-gather.10
  200.3 56.1 all-gather.12
  258.8 56.7 all-gather.14
